TPU v7x, 32 devices: a whole 2x2x4 slice. The times are simulated.
32 devices in a mesh: dp: 4 (over z), expert: 8 (over y, x, core).
Axes of the slice: x: 2, y: 2, z: 4, core: 2. Of those that a mesh axis runs over, the one named last changes fastest.
Arguments:
- queries: bfloat16 [8192, 1536], P(('dp', 'expert')), may hold values from -8 to 8
- rotated_key_heads: bfloat16 [8192, 512], P(('dp', 'expert')), may hold values from -8 to 8
- token_value_heads: bfloat16 [8192, 512], P(('dp', 'expert')), may hold values from -4 to 4
- residual: bfloat16 [8192, 1536], P(('dp', 'expert')), may hold values from -20 to 20
- lengths: int32 [32, 4], P(('dp', 'expert')), may hold values from 1 to 128, 256 in all within a row
- request_adapter_index: int32 [128], P(('dp', 'expert')), may hold values from 0 to 63
- attention_output_weight: bfloat16 [1536, 1536], P('dp'), may hold values from -0.15625 to 0.15625
- adapter_down_factor: bfloat16 [64, 1536, 16], P('expert'), may hold values from -0.15625 to 0.15625
- adapter_up_factor: bfloat16 [64, 16, 1536], P('expert'), may hold values from -1.5 to 1.5
- expert_norm_scale: float32 [1536], replicated, may hold values from 0.5 to 1.5
- router_logit_scores: float32 [8192, 8], P(('dp', 'expert')), may hold values from -4 to 404
- routes: int32 [8192, 8], P(('dp', 'expert')), may hold values from 0 to 15, all different within a row; in each aligned block of 256 rows (0 to 255, 256 to 511, ...) at most 160 rows name the same one
- expert_gate_weight: bfloat16 [16, 1536, 512], P('expert'), may hold values from -0.15625 to 0.15625
- expert_up_weight: bfloat16 [16, 1536, 512], P('expert'), may hold values from -0.15625 to 0.15625
- expert_down_weight: bfloat16 [16, 512, 1536], P('expert'), may hold values from -0.25 to 0.25
Outputs:
- block_out: bfloat16 [8192, 1536], P(('dp', 'expert'))
Inputs may be any that keep to these rules, and one draw needn't show every extreme that they name: `routes`: in the rows of one device no expert is named by more than 160 rows, a bound that some block reaches.
All inputs are finite; a program needn't handle non-finite values.
Results may differ from a plain program's by a relative error of at most 0.0044.
Values may be sent and summed in bfloat16 or wider, within the bound.
No kernel may reach another device: no remote copies, remote signals or barrier semaphores. Data moves between devices by JAX's collectives and lax.ppermute only.
A program may use at most 128 MiB of HBM per device.

v0:
```python
import jax
import jax.numpy as jnp
from jax import lax
from jax.sharding import PartitionSpec as P

HEADS = 24
KV_HEADS = 8
HEAD = 64
TOPK = 8


def segment_of(lengths_row, tokens):
    request_ends = jnp.cumsum(lengths_row)
    positions = jnp.arange(tokens, dtype=jnp.int32)
    return jnp.sum((positions[:, None] >= request_ends[None, :]).astype(jnp.int32), axis=1)


def attend(queries, rotated_key_heads, token_value_heads, segment):
    tokens = queries.shape[0]
    groups = HEADS // KV_HEADS
    grouped = queries.reshape(tokens, KV_HEADS, groups, HEAD)
    key_heads = rotated_key_heads.reshape(tokens, KV_HEADS, HEAD)
    value_heads = token_value_heads.reshape(tokens, KV_HEADS, HEAD)
    scores = jnp.einsum(
        "tkgh,skh->kgts", grouped, key_heads, preferred_element_type=jnp.float32
    ) * HEAD ** (-0.5)
    positions = jnp.arange(tokens, dtype=jnp.int32)
    allowed = (segment[:, None] == segment[None, :]) & (positions[:, None] >= positions[None, :])
    scores = jnp.where(allowed, scores, -1e30)
    row_peak = jnp.max(scores, axis=-1, keepdims=True)
    raised = jnp.exp(scores - row_peak)
    weights = (raised / jnp.sum(raised, axis=-1, keepdims=True)).astype(jnp.bfloat16)
    head_mix = jnp.einsum(
        "kgts,skh->tkgh", weights, value_heads, preferred_element_type=jnp.float32
    )
    return head_mix.reshape(tokens, HEADS * HEAD).astype(jnp.bfloat16)


def run_experts(arrived, expert_gate_weight, expert_up_weight, expert_down_weight):
    gate_part = jnp.einsum(
        "secd,edf->secf", arrived, expert_gate_weight, preferred_element_type=jnp.float32
    )
    up_part = jnp.einsum(
        "secd,edf->secf", arrived, expert_up_weight, preferred_element_type=jnp.float32
    )
    active = (jax.nn.silu(gate_part) * up_part).astype(jnp.bfloat16)
    return jnp.einsum(
        "secf,efd->secd", active, expert_down_weight, preferred_element_type=jnp.float32
    ).astype(jnp.bfloat16)


def per_device(
    queries,
    rotated_key_heads,
    token_value_heads,
    residual,
    lengths,
    request_adapter_index,
    attention_output_weight,
    adapter_down_factor,
    adapter_up_factor,
    expert_norm_scale,
    router_logit_scores,
    routes,
    expert_gate_weight,
    expert_up_weight,
    expert_down_weight,
):
    tokens = queries.shape[0]
    width = attention_output_weight.shape[1]
    requests_here = request_adapter_index.shape[0]
    segment = segment_of(lengths[0], tokens)
    context = attend(queries, rotated_key_heads, token_value_heads, segment)
    projected = jnp.dot(
        context,
        lax.all_gather(attention_output_weight, "dp", axis=0, tiled=True),
        preferred_element_type=jnp.float32,
    )
    member_int = (segment[:, None] == jnp.arange(requests_here, dtype=jnp.int32)[None, :]).astype(
        jnp.int32
    )
    pool_down, pool_up = (
        lax.all_gather(adapter_down_factor, "expert", axis=0, tiled=True),
        lax.all_gather(adapter_up_factor, "expert", axis=0, tiled=True),
    )
    chosen_down = jnp.take(pool_down, request_adapter_index, axis=0)
    chosen_up = jnp.take(pool_up, request_adapter_index, axis=0)
    rank_size = chosen_down.shape[2]
    every_low = jnp.einsum("td,rdk->trk", context, chosen_down, preferred_element_type=jnp.float32)
    picked_low = (every_low * member_int.astype(jnp.float32)[:, :, None]).astype(jnp.bfloat16)
    picked_low = picked_low.reshape(tokens, requests_here * rank_size)
    adapter_term = jnp.dot(
        picked_low,
        chosen_up.reshape(requests_here * rank_size, width),
        preferred_element_type=jnp.float32,
    )
    hidden = residual.astype(jnp.float32) + projected + adapter_term
    mean_square = jnp.mean(hidden * hidden, axis=-1, keepdims=True)
    normed = (hidden * lax.rsqrt(mean_square + 1e-06) * expert_norm_scale).astype(jnp.bfloat16)
    logit_peak = jnp.max(router_logit_scores, axis=-1, keepdims=True)
    raised = jnp.exp(router_logit_scores - logit_peak)
    gate_weights = raised / jnp.sum(raised, axis=-1, keepdims=True)
    local_experts = expert_gate_weight.shape[0]
    expert_devices = lax.axis_size("expert")
    experts_all = local_experts * expert_devices
    capacity = min(tokens, max(2, tokens * TOPK * 5 // (4 * experts_all)))
    flat_routes = routes.reshape(-1)
    route_hits = (flat_routes[:, None] == jnp.arange(experts_all, dtype=jnp.int32)[None, :]).astype(
        jnp.int32
    )
    slot_rank = jnp.sum((jnp.cumsum(route_hits, axis=0) - route_hits) * route_hits, axis=1)
    slot_index = flat_routes * capacity + slot_rank
    anchor = jnp.arange(tokens * TOPK, dtype=jnp.int32) // TOPK
    sources = jnp.zeros((experts_all * capacity,), jnp.int32).at[slot_index].set(anchor)
    filled = jnp.zeros((experts_all * capacity,), jnp.int32).at[slot_index].set(1)
    outgoing = jnp.where(
        filled[:, None] > 0, jnp.take(normed, sources, axis=0), jnp.zeros((), normed.dtype)
    )
    outgoing = outgoing.reshape(expert_devices, local_experts, capacity, width)
    arrived = lax.all_to_all(outgoing, "expert", split_axis=0, concat_axis=0, tiled=True)
    came_back = lax.all_to_all(
        run_experts(arrived, expert_gate_weight, expert_up_weight, expert_down_weight),
        "expert",
        split_axis=0,
        concat_axis=0,
        tiled=True,
    )
    picked = jnp.take(came_back.reshape(experts_all * capacity, width), slot_index, axis=0).reshape(
        tokens, TOPK, width
    )
    mixture = jnp.sum(gate_weights[:, :, None] * picked, axis=1)
    return (hidden + mixture).astype(jnp.bfloat16)


def solution(mesh):
    return jax.shard_map(
        per_device,
        mesh=mesh,
        in_specs=(
            P(("dp", "expert"), None),
            P(("dp", "expert"), None),
            P(("dp", "expert"), None),
            P(("dp", "expert"), None),
            P(("dp", "expert"), None),
            P(("dp", "expert")),
            P("dp", None),
            P("expert", None, None),
            P("expert", None, None),
            P(),
            P(("dp", "expert"), None),
            P(("dp", "expert"), None),
            P("expert", None, None),
            P("expert", None, None),
            P("expert", None, None),
        ),
        out_specs=P(("dp", "expert"), None),
        check_vma=False,
    )
```

profile of v0, /device:TPU:0, one launch (start us, length us, event | category | flops | bytes accessed | tf_op | source)
XLA Modules:
  0.0 456.1 jit_solution(2554271354359313261)
XLA Ops:
  6.5 0.7 all-gather.6.cloned.1.call-update
  8.7 0.8 copy.64
  9.8 2.3 copy.59
  12.1 1.8 copy.58
  13.9 1.8 copy.60
  15.7 0.8 reduce-window.18
  16.5 4.5 reduce-window.19
  22.2 8.1 %scatter_custom_fusion.1 = s32[2560]{0:T(1024)S(1)} fusion(s32[2048]{0:T(1024)S(1)} %bitcast.120, s32[2048]{0:T(1024)S(1)} %add_select_fusion, s32[]{:T(128)} %constant.64.clone.1), kind=kCustom, calls=%fused_computation.74 | custom fusion | bytes 10244 | tf_op jit(solution)/shard_map/scatter | solution.py:114
  30.9 8.1 %scatter_custom_fusion = s32[2560]{0:T(1024)S(1)} fusion(s32[2048]{0:T(1024)S(1)} %bitcast.121, s32[2048]{0:T(1024)S(1)} %broadcast.140, s32[]{:T(128)} %constant.64.clone.1), kind=kCustom, calls=%fused_computation.77 | custom fusion | bytes 10244 | tf_op jit(solution)/shard_map/scatter | solution.py:115
  41.6 6.0 %fusion.51 = (f32[8,3,256]{2,1,0:T(4,128)S(1)}, f32[8,3,256,256]{2,3,1,0:T(8,128)}) fusion(pred[256,256]{0,1:T(8,128)(4,1)S(1)} %fusion.29, bf16[256,8,64,1]{0,2,3,1:T(8,128)(2,1)} %bitcast.117, bf16[256,8,3,64]{0,3,2,1:T(8,128)(2,1)} %bitcast.114), kind=kOutput, calls=%fused_computation.93 | convolution fusion | flops 207618304 | bytes 7430144 | tf_op jit(solution)/shard_map/sub | solution.py:31
  47.6 4.3 fusion.26
  52.0 2.6 gather_fusion
  54.6 24.0 %all-gather.8.cloned.1.call-done = bf16[64,16,1536]{2,1,0:T(8,128)(2,1)} async-done(((bf16[8,16,1536]{2,1,0:T(8,128)(2,1)}), bf16[64,16,1536]{2,1,0:T(8,128)(2,1)}) %all-gather.8.cloned.1.call-update) | async-done | bytes 3145744 | tf_op jit(solution)/shard_map/all_gather | solution.py:84
  78.6 2.6 gather_fusion.1
  81.8 1.4 fusion.52
  83.2 2.3 convolution_bitcast_fusion
  85.5 84.1 %all-gather.4.cloned.1.call-done = bf16[1536,1536]{1,0:T(8,128)(2,1)} async-done(((bf16[384,1536]{1,0:T(8,128)(2,1)}), bf16[1536,1536]{1,0:T(8,128)(2,1)}) %all-gather.4.cloned.1.call-update) | async-done | bytes 4718608 | tf_op jit(solution)/shard_map/all_gather | solution.py:76
  169.6 4.8 %multiply_reduce_fusion.1 = (f32[256]{0:T(256)S(1)}, f32[256,1536]{1,0:T(8,128)S(1)}) fusion(f32[256,1536]{1,0:T(8,128)} %convolution_bitcast_fusion, bf16[256,1536]{0,1:T(8,128)(2,1)} %bitcast.112, bf16[1536,1536]{1,0:T(8,128)(2,1)} %all-gather.4.cloned.1.call-done, bf16[256,1536]{1,0:T(8,128)(2,1)} %param.18), kind=kOutput, calls=%fused_computation.38 | convolution fusion | flops 1209925376 | bytes 9438208 | tf_op jit(solution)/shard_map/dot_general | solution.py:74
  174.4 1.2 copy-done.2
  175.6 1.1 multiply_convert_fusion
  176.6 17.6 %gather_fusion.2 = bf16[2560,1536]{1,0:T(8,128)(2,1)} fusion(bf16[256,1536]{1,0:T(8,128)(2,1)} %multiply_convert_fusion, s32[3072]{0:T(1024)S(1)} %copy-done.8), kind=kCustom, calls=%fused_computation.2 | custom fusion | bytes 15738880 | tf_op jit(solution)/shard_map/jit(_take)/gather | solution.py:117
  194.3 4.5 select_select_fusion
  198.7 92.1 %all_to_all.10 = bf16[8,2,160,1536]{3,2,1,0:T(8,128)(2,1)S(1)} all-to-all(bf16[8,2,160,1536]{3,2,1,0:T(8,128)(2,1)S(1)} %select_select_fusion), channel_id=1, replica_groups=mesh['dp'=4,'expert'=8] {'expert'}, dimensions={0} | all-to-all | bytes 15728640 | tf_op jit(solution)/shard_map/all_to_all | solution.py:120
  290.9 3.2 copy-done.4
  294.1 5.9 %fusion.1 = f32[2,8,160,512]{3,2,1,0:T(8,128)} fusion(bf16[8,2,160,1536]{3,2,1,0:T(8,128)(2,1)S(1)} %all_to_all.10, bf16[2,1536,512]{2,1,0:T(8,128)(2,1)S(1)} %copy-done.15), kind=kOutput, calls=%fused_computation.10 | convolution fusion | flops 4026531840 | bytes 16252928 | tf_op jit(solution)/shard_map/secd,edf->secf/dot_general | solution.py:43
  300.0 14.2 %convert_bitcast_fusion = bf16[8,2,160,1536]{3,2,0,1:T(8,128)(2,1)} fusion(bf16[2,512,1536]{2,1,0:T(8,128)(2,1)S(1)} %copy-done, f32[2,8,160,512]{3,2,1,0:T(8,128)} %fusion.1, bf16[2,1536,512]{2,1,0:T(8,128)(2,1)} %param.27, bf16[8,2,160,1536]{3,2,1,0:T(8,128)(2,1)} %copy-done.4), kind=kOutput, calls=%fused_computation.8 | convolution fusion | flops 8064860160 | bytes 27262976 | tf_op jit(solution)/shard_map/secf,efd->secd/dot_general | solution.py:47
  314.2 7.1 %copy.71 = bf16[8,2,160,1536]{3,2,1,0:T(8,128)(2,1)} copy(bf16[8,2,160,1536]{3,2,0,1:T(8,128)(2,1)} %convert_bitcast_fusion) | data formatting | bytes 15728640 | tf_op jit(solution)/shard_map/convert_element_type | solution.py:49
  321.3 5.0 %all-to-all-start.1 = ((bf16[8,2,160,1536]{3,2,1,0:T(8,128)(2,1)}), bf16[8,2,160,1536]{3,2,1,0:T(8,128)(2,1)}, u32[]{:S(2)}, u32[]{:S(2)}) async-start(bf16[8,2,160,1536]{3,2,1,0:T(8,128)(2,1)} %copy.71), calls=%async_computation.1 | async-start | bytes 15728640 | tf_op jit(solution)/shard_map/all_to_all | solution.py:121
  326.9 87.9 %all-to-all-done.1 = bf16[8,2,160,1536]{3,2,1,0:T(8,128)(2,1)} async-done(((bf16[8,2,160,1536]{3,2,1,0:T(8,128)(2,1)}), bf16[8,2,160,1536]{3,2,1,0:T(8,128)(2,1)}, u32[]{:S(2)}, u32[]{:S(2)}) %all-to-all-start.1) | async-done | bytes 7864352 | tf_op jit(solution)/shard_map/all_to_all | solution.py:121
  414.8 17.7 %gather_fusion.3 = bf16[2048,1536]{1,0:T(8,128)(2,1)} fusion(bf16[2560,1536]{1,0:T(8,128)(2,1)} %bitcast.30, s32[2048]{0:T(1024)S(1)} %broadcast_clamp_fusion), kind=kCustom, calls=%fused_computation.3 | custom fusion | bytes 12591104 | tf_op jit(solution)/shard_map/jit(_take)/gather | solution.py:128
  432.5 16.0 %multiply_reduce_fusion = f32[256,1536]{1,0:T(8,128)S(1)} fusion(bf16[2048,1536]{1,0:T(8,128)(2,1)} %gather_fusion.3, f32[256,8]{1,0:T(8,128)S(1)} %copy.63, pred[256,8]{1,0:T(8,128)(4,1)S(1)} %copy.67), kind=kLoop, calls=%fused_computation.7 | loop fusion | flops 12189696 | bytes 7874560 | tf_op jit(solution)/shard_map/reduce_sum | solution.py:131
  448.5 1.1 add_convert_fusion
  (74 shorter events, 7.3 us)
Async XLA Ops:
  6.5 293.4 %copy-start = (bf16[2,512,1536]{2,1,0:T(8,128)(2,1)S(1)}, bf16[2,512,1536]{2,1,0:T(8,128)(2,1)}, u32[]{:S(2)}) copy-start(bf16[2,512,1536]{2,1,0:T(8,128)(2,1)} %param.29) | copy-start | bytes 9437188
  6.5 15.1 %copy-start.6 = (s32[256,8]{0,1:T(8,128)S(1)}, s32[256,8]{0,1:T(8,128)}, u32[]{:S(2)}) copy-start(s32[256,8]{0,1:T(8,128)} %param.26) | copy-start | bytes 24580
  6.5 33.1 %copy-start.16 = (s32[4]{0:T(128)S(1)}, s32[4]{0:T(128)}, u32[]{:S(2)}) copy-start(s32[4]{0:T(128)} %param.20) | copy-start | bytes 52
  6.5 45.4 %all-gather.6.cloned.1.call-start = ((), (), s32[]{:S(2)}) async-start(), calls=%async_computation.3 | async-start | bytes 3538944 | tf_op jit(solution)/shard_map/all_gather | solution.py:83
  7.3 71.3 %all-gather.8.cloned.1.call-start = ((), (), s32[]{:S(2)}) async-start(), calls=%async_computation.4 | async-start | bytes 3538944 | tf_op jit(solution)/shard_map/all_gather | solution.py:84
  8.0 161.6 %all-gather.4.cloned.1.call-start = ((), (), s32[]{:S(2)}) async-start(), calls=%async_computation.2 | async-start | bytes 5898240 | tf_op jit(solution)/shard_map/all_gather | solution.py:76
  22.2 18.8 %copy-start.11 = (s32[2048,1]{0,1:T(1,128)}, s32[2048,1]{0,1:T(1,128)S(1)}, u32[]{:S(2)}) copy-start(s32[2048,1]{0,1:T(1,128)S(1)} %compare_select_fusion) | copy-start | bytes 24580
  39.7 12.3 %copy-start.14 = (s32[1024]{0:T(1024)}, s32[1024]{0:T(1024)S(1)}, u32[]{:S(2)}) copy-start(s32[1024]{0:T(1024)S(1)} %pad_clamp_fusion.1) | copy-start | bytes 12292
  41.6 6.0 %copy-start.5 = (bf16[256,512]{0,1:T(8,128)(2,1)S(1)}, bf16[256,512]{0,1:T(8,128)(2,1)}, u32[]{:S(2)}) copy-start(bf16[256,512]{0,1:T(8,128)(2,1)} %copy.60) | copy-start | bytes 786436
  85.5 90.1 %copy-start.13 = (f32[1536]{0:T(1024)S(1)}, f32[1536]{0:T(1024)}, u32[]{:S(2)}) copy-start(f32[1536]{0:T(1024)} %param.24) | copy-start | bytes 18436
  85.5 91.1 %copy-start.8 = (s32[3072]{0:T(1024)S(1)}, s32[3072]{0:T(1024)}, u32[]{:S(2)}) copy-start(s32[3072]{0:T(1024)} %pad_clamp_fusion) | copy-start | bytes 36868
  174.4 1.2 copy-start.2
  176.6 17.6 %copy-start.9 = (pred[8,2,160]{2,1,0:T(4,128)(4,1)S(1)}, pred[8,2,160]{2,1,0:T(4,128)(4,1)}, u32[]{:S(2)}) copy-start(pred[8,2,160]{2,1,0:T(4,128)(4,1)} %broadcast_in_dim.102) | copy-start | bytes 7684
  176.6 17.6 %copy-start.10 = (pred[8,2,160]{2,1,0:T(4,128)(4,1)S(1)}, pred[8,2,160]{2,1,0:T(4,128)(4,1)}, u32[]{:S(2)}) copy-start(pred[8,2,160]{2,1,0:T(4,128)(4,1)} %broadcast_in_dim.100) | copy-start | bytes 7684
  198.7 95.3 %copy-start.15 = (bf16[2,1536,512]{2,1,0:T(8,128)(2,1)S(1)}, bf16[2,1536,512]{2,1,0:T(8,128)(2,1)}, u32[]{:S(2)}) copy-start(bf16[2,1536,512]{2,1,0:T(8,128)(2,1)} %param.28) | copy-start | bytes 9437188
  290.9 3.2 copy-start.4
  321.3 5.4 %copy-start.7 = (f32[256,8]{0,1:T(8,128)S(1)}, f32[256,8]{0,1:T(8,128)}, u32[]{:S(2)}) copy-start(f32[256,8]{0,1:T(8,128)} %param.25) | copy-start | bytes 24580
  321.3 5.6 %copy-start.12 = (s32[2048,1]{0,1:T(1,128)S(1)}, s32[2048,1]{0,1:T(1,128)}, u32[]{:S(2)}) copy-start(s32[2048,1]{0,1:T(1,128)} %copy-done.11) | copy-start | bytes 24580
  321.3 93.5 %all-to-all-start.1 = ((bf16[8,2,160,1536]{3,2,1,0:T(8,128)(2,1)}), bf16[8,2,160,1536]{3,2,1,0:T(8,128)(2,1)}, u32[]{:S(2)}, u32[]{:S(2)}) async-start(bf16[8,2,160,1536]{3,2,1,0:T(8,128)(2,1)} %copy.71), calls=%async_computation.1 | async-start | bytes 15728640 | tf_op jit(solution)/shard_map/all_to_all | solution.py:121
  414.8 34.8 %copy-start.1 = (bf16[2,512,1536]{2,1,0:T(8,128)(2,1)S(1)}, bf16[2,512,1536]{2,1,0:T(8,128)(2,1)}, u32[]{:S(2)}) copy-start(bf16[2,512,1536]{2,1,0:T(8,128)(2,1)} %param.29) | copy-start | bytes 9437188
  432.5 16.0 %copy-start.3 = (f32[256,1536]{1,0:T(8,128)S(1)}, f32[256,1536]{1,0:T(8,128)}, u32[]{:S(2)}) copy-start(f32[256,1536]{1,0:T(8,128)} %copy-done.2) | copy-start | bytes 4718596
Sparse Core Ops, SparseCore 0:
  9.2 35.0 all-gather.5
  46.2 32.3 all-gather.7
  80.2 89.4 all-gather.3
where the time goes:
time: 457 us; the launch traced here: 456 us
  waiting for transfers between devices  198 us (43%)
  blocking collectives  92.1 us (20%)
  local copies, waits for them, and re-layouts  77.5 us (17%)
  matrix products  38.9 us (9%)
  other arithmetic  31 us (7%)
  between operations  13.4 us (3%)
  starting transfers between devices  5.11 us (1%)
    all_to_all x1, blocking collectives, per_device(): lax.all_to_all(outgoing, 'expert', split_axis=0, concat_axis=0, tiled=True)  92.1 us
    all_to_all x1, waiting for transfers between devices, per_device(): lax.all_to_all(run_experts(arrived, expert_gate_weight, expert_up_weight,...  87.9 us
    all_gather x1, waiting for transfers between devices, per_device(): lax.all_gather(attention_output_weight, 'dp', axis=0, tiled=True)  84.1 us
    all_gather x1, waiting for transfers between devices, per_device(): lax.all_gather(adapter_up_factor, 'expert', axis=0, tiled=True)  24 us
    gather x1, local copies, waits for them, and re-layouts, per_device(): jnp.take(came_back.reshape(experts_all * capacity, width), slot_index, ax...  17.7 us
    gather x1, local copies, waits for them, and re-layouts, per_device(): jnp.take(normed, sources, axis=0)  17.6 us
    reduce_sum x1, other arithmetic, per_device(): mixture = jnp.sum(gate_weights[:, :, None] * picked, axis=1)  16 us
    dot_general x1, matrix products, run_experts(): jnp.einsum('secf,efd->secd', active, expert_down_weight, preferred_elemen...  14.2 us
  transfers between devices with their start and end apart: 4, of which 3 were waited for; matrix products, arithmetic and copies ran while one was open for 12% of the time, Pallas kernels for 0%

commit v1 on v0

v1 whole, which is shorter than its diff:
```python
import functools

import jax
import jax.numpy as jnp
from jax import lax
from jax.experimental import pallas as pl
from jax.experimental.pallas import tpu as pltpu
from jax.sharding import PartitionSpec as P

HEAD = 64
GROUPS = 3
BF16, F32 = jnp.bfloat16, jnp.float32
VMEM = pl.BlockSpec(memory_space=pltpu.VMEM)
SMEM = pl.BlockSpec(memory_space=pltpu.SMEM)
ANY = pl.BlockSpec(memory_space=pl.ANY)
LIMIT = 56 * 2**20


def call(kernel, name, out_shape, in_specs, out_specs, scratch, flops, moved, **more):
    return pl.pallas_call(
        kernel,
        name=name,
        out_shape=out_shape,
        in_specs=in_specs,
        out_specs=out_specs,
        scratch_shapes=scratch,
        compiler_params=pltpu.CompilerParams(vmem_limit_bytes=LIMIT),
        cost_estimate=pl.CostEstimate(flops=flops, bytes_accessed=moved, transcendentals=0),
        **more,
    )


def attend_kernel(lengths_ref, q_ref, k_ref, v_ref, o_ref, bias):
    tokens = q_ref.shape[0]
    half = tokens // 2

    @pl.when(pl.program_id(0) == 0)
    def _():
        row = lax.broadcasted_iota(jnp.int32, (tokens, tokens), 0)
        col = lax.broadcasted_iota(jnp.int32, (tokens, tokens), 1)
        same = row >= col
        end = 0
        for r in range(lengths_ref.shape[1]):
            end = end + lengths_ref[0, r]
            same = same & ((row < end) | (col >= end))
        bias[...] = jnp.where(same, 0.0, -1e30)

    for j in range(k_ref.shape[1] // HEAD):
        keys = k_ref[:, j * HEAD : (j + 1) * HEAD]
        values = v_ref[:, j * HEAD : (j + 1) * HEAD]
        for g in range(GROUPS):
            at = (j * GROUPS + g) * HEAD
            q = q_ref[:, at : at + HEAD] * jnp.asarray(HEAD**-0.5, BF16)
            for first, seen in ((0, half), (half, tokens)):
                s = lax.dot_general(
                    q[first : first + half],
                    keys[:seen],
                    (((1,), (1,)), ((), ())),
                    preferred_element_type=F32,
                )
                s = s + bias[first : first + half, :seen]
                p = jnp.exp(s - jnp.max(s, axis=-1, keepdims=True))
                w = (p * (1.0 / jnp.sum(p, axis=-1, keepdims=True))).astype(BF16)
                o = jnp.dot(w, values[:seen], preferred_element_type=F32)
                o_ref[first : first + half, at : at + HEAD] = o.astype(BF16)


def attend(lengths, q, k, v):
    tokens, width = q.shape
    pairs = k.shape[1] // (2 * HEAD)
    wide = width // pairs
    return pl.pallas_call(
        attend_kernel,
        name="attend",
        grid=(pairs,),
        out_shape=jax.ShapeDtypeStruct((tokens, width), BF16),
        in_specs=[
            SMEM,
            pl.BlockSpec((tokens, wide), lambda i: (0, i)),
            pl.BlockSpec((tokens, 2 * HEAD), lambda i: (0, i)),
            pl.BlockSpec((tokens, 2 * HEAD), lambda i: (0, i)),
        ],
        out_specs=pl.BlockSpec((tokens, wide), lambda i: (0, i)),
        scratch_shapes=[pltpu.VMEM((tokens, tokens), F32)],
        compiler_params=pltpu.CompilerParams(vmem_limit_bytes=LIMIT),
        cost_estimate=pl.CostEstimate(
            flops=16 * 10**9, bytes_accessed=2 * 10**6, transcendentals=0
        ),
    )(lengths, q, k, v)


def prepare_kernel(logits_ref, routes_ref, down_ref, up_ref, o_ref):
    tokens, top = logits_ref.shape
    logits = logits_ref[...]
    raised = jnp.exp(logits - jnp.max(logits, axis=-1, keepdims=True))
    gates = raised / jnp.sum(raised, axis=-1, keepdims=True)
    lane = lax.broadcasted_iota(jnp.int32, (tokens, 128), 1)
    routes = routes_ref[...]
    gain = jnp.zeros((tokens, 128), F32)
    for j in range(top):
        hit = (lane & 63) == routes[:, j : j + 1]
        gain = gain + jnp.where(hit, gates[:, j : j + 1], 0.0)
    high = gain.astype(BF16).astype(F32)
    count, rank, width = down_ref.shape
    o_ref[:, width:] = jnp.where(lane < 64, high, gain - high).astype(BF16)
    for a in range(count):
        o_ref[2 * rank * a : 2 * rank * a + rank, :width] = down_ref[a]
        o_ref[2 * rank * a + rank : 2 * rank * (a + 1), :width] = up_ref[a]


def prepare(logits, routes, down, up):
    tokens = logits.shape[0]
    width = up.shape[2]
    return call(
        prepare_kernel,
        "prepare",
        jax.ShapeDtypeStruct((tokens, width + 128), BF16),
        [VMEM] * 4,
        VMEM,
        [],
        10**6,
        2 * 10**6,
    )(logits, routes, down, up)


def project_kernel(pools, shards, rank, *refs):
    meta, ids, lengths, ctx_ref, res_ref, scale_ref = refs[:6]
    pool = refs[6 : 6 + pools]
    shard = refs[6 + pools : 6 + pools + shards]
    hidden_ref, normed_ref, low_s, up_s, wo_s, sem_a, sem_w = refs[6 + pools + shards :]
    requests = ids.shape[0]
    tokens, width = res_ref.shape

    def each_shard(do):
        for k in range(shards):
            rows = shard[k].shape[0]
            at = meta[2 * pools + k]

            @pl.when(at >= 0)
            def _():
                do(
                    pltpu.make_async_copy(
                        shard[k], wo_s.at[pl.ds(pl.multiple_of(at, rows), rows)], sem_w.at[k]
                    )
                )

    each_shard(lambda c: c.start())
    for r in range(requests):
        for k in range(pools):
            at = ids[r] - meta[2 * k]

            @pl.when((at >= 0) & (at < meta[2 * k + 1]))
            def _():
                first = pl.multiple_of(at * (2 * rank), 2 * rank)
                for half, to in ((0, low_s), (1, up_s)):
                    pltpu.make_async_copy(
                        pool[k].at[pl.ds(first + half * rank, rank), pl.ds(0, width)],
                        to.at[pl.ds(r * rank, rank)],
                        sem_a.at[r, half],
                    ).start()

    for r in range(requests):
        for half, to in ((0, low_s), (1, up_s)):
            pltpu.make_async_copy(
                pool[0].at[pl.ds(0, rank), pl.ds(0, width)],
                to.at[pl.ds(r * rank, rank)],
                sem_a.at[r, half],
            ).wait()
    ctx = ctx_ref[...]
    low = lax.dot_general(ctx, low_s[...], (((1,), (1,)), ((), ())), preferred_element_type=F32)
    row = lax.broadcasted_iota(jnp.int32, low.shape, 0)
    lane = lax.broadcasted_iota(jnp.int32, low.shape, 1)
    end = 0
    mine = lane < 0
    for r in range(requests):
        start, end = end, end + lengths[0, r]
        inside = (row >= start) & (row < end)
        mine = mine | (inside & (lane >= r * rank) & (lane < (r + 1) * rank))
    low = jnp.where(mine, low, 0.0).astype(BF16)
    hidden_ref[...] = res_ref[...].astype(F32) + jnp.dot(
        low, up_s[...], preferred_element_type=F32
    )
    each_shard(lambda c: c.wait())
    block = min(512, width)
    square = jnp.zeros((tokens, 1), F32)
    for c in range(0, width, block):
        h = hidden_ref[:, c : c + block] + jnp.dot(
            ctx, wo_s[:, c : c + block], preferred_element_type=F32
        )
        hidden_ref[:, c : c + block] = h
        square = square + jnp.sum(h * h, axis=-1, keepdims=True)
    inv = lax.rsqrt(square * (1.0 / width) + 1e-06)
    normed_ref[...] = (hidden_ref[...] * inv * scale_ref[...]).astype(BF16)


def project(meta, ids, lengths, ctx, residual, scale, pools, shards, rank):
    tokens, width = residual.shape
    requests = ids.shape[0]
    return call(
        functools.partial(project_kernel, len(pools), len(shards), rank),
        "project",
        (
            jax.ShapeDtypeStruct((tokens, width), F32),
            jax.ShapeDtypeStruct((tokens, width), BF16),
        ),
        [SMEM] * 3 + [VMEM] * 3 + [ANY] * (len(pools) + len(shards)),
        (VMEM, VMEM),
        [
            pltpu.VMEM((requests * rank, width), BF16),
            pltpu.VMEM((requests * rank, width), BF16),
            pltpu.VMEM((ctx.shape[1], width), BF16),
            pltpu.SemaphoreType.DMA((requests, 2)),
            pltpu.SemaphoreType.DMA((len(shards),)),
        ],
        4 * 10**9,
        10**7,
    )(meta, ids, lengths, ctx, residual, scale, *pools, *shards)


def experts_kernel(groups, blocks, first_ref, *refs):
    xs, gains = refs[:blocks], refs[blocks : 2 * blocks]
    w = refs[2 * blocks : 2 * blocks + 3 * groups]
    outs = refs[2 * blocks + 3 * groups : 3 * blocks + 3 * groups]
    held, strips = refs[3 * blocks + 3 * groups : -3], refs[-3]
    sem, sem_g = refs[-2:]
    local = w[0].shape[0]
    total = groups * local
    last = gains[0].shape[1] - 128
    pulls = [
        pltpu.make_async_copy(gains[b].at[:, pl.ds(last, 128)], strips.at[b], sem_g.at[b])
        for b in range(blocks)
    ]
    for p in pulls:
        p.start()

    def fetch(e):
        return [
            pltpu.make_async_copy(w[3 * (e // local) + k].at[e % local], held[k].at[e], sem.at[e, k])
            for k in range(3)
        ]

    for e in range(min(2, total)):
        for c in fetch(e):
            c.start()
    for e in range(total):
        copies = fetch(e)
        copies[0].wait()
        copies[1].wait()
        for b in range(blocks):
            x = xs[b][...]
            if e == 0:
                pulls[b].wait()
            gain = strips[b].astype(F32)
            lane = lax.broadcasted_iota(jnp.int32, gain.shape, 1)
            coef = jnp.sum(
                jnp.where((lane & 63) == first_ref[e], gain, 0.0), axis=-1, keepdims=True
            )
            gate = jnp.dot(x, held[0][e], preferred_element_type=F32)
            up = jnp.dot(x, held[1][e], preferred_element_type=F32)
            act = (gate / (1.0 + jnp.exp(-gate)) * up * coef).astype(BF16)
            if b == 0:
                copies[2].wait()
                if e + 2 < total:
                    for c in fetch(e + 2):
                        c.start()
            down = jnp.dot(act, held[2][e], preferred_element_type=F32)
            if total == 1:
                outs[b][...] = down.astype(BF16)
            elif e == 0:
                held[3][b] = down
            elif e < total - 1:
                held[3][b] += down
            else:
                outs[b][...] = (held[3][b] + down).astype(BF16)


def run_experts(numbers, xs, gains, weights):
    groups, blocks = len(weights) // 3, len(xs)
    tokens, width = xs[0].shape
    local, _, hid = weights[0].shape
    total = groups * local
    out = jax.ShapeDtypeStruct((tokens, width), BF16)
    return call(
        functools.partial(experts_kernel, groups, blocks),
        "experts",
        (out,) * blocks,
        [SMEM] + [VMEM] * blocks + [ANY] * blocks + [ANY] * (3 * groups),
        (VMEM,) * blocks,
        [
            pltpu.VMEM((total, width, hid), BF16),
            pltpu.VMEM((total, width, hid), BF16),
            pltpu.VMEM((total, hid, width), BF16),
            pltpu.VMEM((blocks, tokens, width), F32),
            pltpu.VMEM((blocks, tokens, 128), BF16),
            pltpu.SemaphoreType.DMA((total, 3)),
            pltpu.SemaphoreType.DMA((blocks,)),
        ],
        6 * blocks * tokens * width * hid * total,
        6 * total * width * hid,
    )(numbers, *xs, *gains, *weights)


def per_device(
    queries,
    rotated_key_heads,
    token_value_heads,
    residual,
    lengths,
    request_adapter_index,
    attention_output_weight,
    adapter_down_factor,
    adapter_up_factor,
    expert_norm_scale,
    router_logit_scores,
    routes,
    expert_gate_weight,
    expert_up_weight,
    expert_down_weight,
):
    tokens = queries.shape[0]
    rank = adapter_up_factor.shape[1]
    held_adapters = adapter_up_factor.shape[0]
    local = expert_gate_weight.shape[0]
    n_dp, n_ex = lax.axis_size("dp"), lax.axis_size("expert")
    z, i = lax.axis_index("dp"), lax.axis_index("expert")
    rows = attention_output_weight.shape[0]
    both = ("dp", "expert")
    down_t = jnp.swapaxes(adapter_down_factor, 1, 2)
    scale = expert_norm_scale.reshape(1, -1)
    weights = (expert_gate_weight, expert_up_weight, expert_down_weight)
    paired = n_ex == 8 and held_adapters * 2 * rank == tokens

    context = attend(lengths, queries, rotated_key_heads, token_value_heads)

    if not paired:
        padded = tokens
        packed = prepare_any(router_logit_scores, routes, down_t, adapter_up_factor)
        gains, pool = packed
        shard = lax.all_gather(attention_output_weight, "dp", axis=0, tiled=True)
        pool = lax.all_gather(pool, "expert", axis=0, tiled=True)
        meta = jnp.stack([0 * z, 0 * z + held_adapters * n_ex, 0 * z])
        hidden, normed = project(
            meta, request_adapter_index, lengths, context, residual, scale, [pool], [shard], rank
        )
        every = lax.all_gather(normed, "expert", axis=0, tiled=True)
        every_gain = lax.all_gather(gains, "expert", axis=0, tiled=True)
        numbers = i * local + jnp.arange(local, dtype=jnp.int32)
        parts = [
            run_experts(
                numbers,
                [every[d * padded : (d + 1) * padded]],
                [every_gain[d * padded : (d + 1) * padded]],
                weights,
            )[0]
            for d in range(n_ex)
        ]
        mixture = lax.psum_scatter(
            jnp.concatenate(parts, axis=0), "expert", scatter_dimension=0, tiled=True
        )
        return (hidden + mixture.astype(F32)).astype(BF16)

    def beside(a):
        return lax.ppermute(a, "expert", [(e, e ^ 1) for e in range(n_ex)])

    def across(a):
        return lax.ppermute(a, "expert", [(e, e ^ (4 if e & 1 else 2)) for e in range(n_ex)])

    def along(a, step):
        pairs = []
        for e in range(n_ex):
            for d in range(n_dp):
                to = d - 1 if e & 1 else d + 1
                origin = d + step - 1 if e & 1 else d - step + 1
                if 0 <= to < n_dp and 0 <= origin < n_dp:
                    pairs.append((d * n_ex + e, to * n_ex + e))
        return lax.ppermute(a, both, pairs)

    own = prepare(router_logit_scores, routes, down_t, adapter_up_factor)
    pair_weights = tuple(beside(w) for w in weights)
    p0 = across(own)
    other = beside(own)
    p1 = across(other)
    p0_other = beside(p0)
    p2 = across(p0_other)
    p1_other, p2_other = beside(p1), beside(p2)
    shards, at = [attention_output_weight], [z * rows]
    up_side = 1 - 2 * (i & 1)
    moving = attention_output_weight
    for step in range(1, n_dp):
        moving = along(moving, step)
        for piece, source in ((moving, z - up_side * step), (beside(moving), z + up_side * step)):
            shards.append(piece)
            at.append(jnp.where((source >= 0) & (source < n_dp), source * rows, -1))
    c = i & 1
    near = i ^ jnp.where(c == 0, 2, 4)
    near_other = i ^ jnp.where(c == 0, 4, 2)
    owners = [i, i ^ 1, near, near ^ 1, near_other ^ 1, near_other, i ^ 7, i ^ 6]
    pools = [own, other, p0, p1, p0_other, p1_other, p2, p2_other]
    meta = jnp.stack(
        [v for o in owners for v in (o * held_adapters, 0 * o + held_adapters)] + at
    )
    hidden, normed = project(
        meta, request_adapter_index, lengths, context, residual, scale, pools, shards, rank
    )
    b0 = across(normed)
    b1 = across(beside(normed))
    far = across(beside(b0))
    mine = (i - c) * local
    order = jnp.arange(local, dtype=jnp.int32)
    numbers = jnp.concatenate([mine + c * local + order, mine + (1 - c) * local + order])
    run = functools.partial(run_experts, numbers, weights=weights + pair_weights)
    (home,) = run([normed], [own])
    r0, r1 = run([b0, b1], [p0, p1])
    (r_far,) = run([far], [p2])
    back1 = beside(across(r1))
    via = beside(across(r_far))
    back0 = across((r0.astype(F32) + via.astype(F32)).astype(BF16))
    mixture = home.astype(F32) + back0.astype(F32) + back1.astype(F32)
    return (hidden + mixture).astype(BF16)


def prepare_any_kernel(logits_ref, routes_ref, down_ref, up_ref, gain_ref, pool_ref):
    tokens, top = logits_ref.shape
    logits = logits_ref[...]
    raised = jnp.exp(logits - jnp.max(logits, axis=-1, keepdims=True))
    gates = raised / jnp.sum(raised, axis=-1, keepdims=True)
    lane = lax.broadcasted_iota(jnp.int32, (tokens, 128), 1)
    routes = routes_ref[...]
    gain = jnp.zeros((tokens, 128), F32)
    for j in range(top):
        hit = (lane & 63) == routes[:, j : j + 1]
        gain = gain + jnp.where(hit, gates[:, j : j + 1], 0.0)
    high = gain.astype(BF16).astype(F32)
    gain_ref[...] = jnp.where(lane < 64, high, gain - high).astype(BF16)
    count, rank, _ = down_ref.shape
    for a in range(count):
        pool_ref[2 * rank * a : 2 * rank * a + rank] = down_ref[a]
        pool_ref[2 * rank * a + rank : 2 * rank * (a + 1)] = up_ref[a]


def prepare_any(logits, routes, down, up):
    count, rank, width = up.shape
    return call(
        prepare_any_kernel,
        "prepare_any",
        (
            jax.ShapeDtypeStruct((logits.shape[0], 128), BF16),
            jax.ShapeDtypeStruct((2 * rank * count, width), BF16),
        ),
        [VMEM] * 4,
        (VMEM, VMEM),
        [],
        10**6,
        2 * 10**6,
    )(logits, routes, down, up)


def solution(mesh):
    return jax.shard_map(
        per_device,
        mesh=mesh,
        in_specs=(
            P(("dp", "expert"), None),
            P(("dp", "expert"), None),
            P(("dp", "expert"), None),
            P(("dp", "expert"), None),
            P(("dp", "expert"), None),
            P(("dp", "expert")),
            P("dp", None),
            P("expert", None, None),
            P("expert", None, None),
            P(),
            P(("dp", "expert"), None),
            P(("dp", "expert"), None),
            P("expert", None, None),
            P("expert", None, None),
            P("expert", None, None),
        ),
        out_specs=P(("dp", "expert"), None),
        check_vma=False,
    )
```

time: 457 us -> 170 us (0.37)
  waiting for transfers between devices: 198 us -> 62 us
  blocking collectives: 92.1 us -> 0 us
  local copies, waits for them, and re-layouts: 77.5 us -> 6.79 us
  Pallas kernels: 0 us -> 63.7 us
  matrix products: 38.9 us -> 0 us
  starting transfers between devices: 5.11 us -> 32.2 us
  other arithmetic: 31 us -> 4.32 us
  between operations: 13.4 us -> 0.14 us
    all_gather x3 -> x0, waiting for transfers between devices: 108 us -> none  [the longest x1 84.1 us: per_device(): lax.all_gather(attention_output_weight, 'dp', axis=0, tiled=True)]
    all_to_all x1 -> x0, blocking collectives: 92.1 us -> none  [per_device(): lax.all_to_all(outgoing, 'expert', split_axis=0, concat_axis=0, tiled=True)]
    all_to_all x1 -> x0, waiting for transfers between devices: 87.9 us -> none  [per_device(): lax.all_to_all(run_experts(arrived, expert_gate_weight, expert_up_weight,...]
    pallas_call x0 -> x6, Pallas kernels: none -> 63.7 us  [the longest x3 40.1 us: run_experts(): call(functools.partial(experts_kernel, groups, blocks), 'experts', (out,)...]
    ppermute x0 -> x26, waiting for transfers between devices: none -> 62 us  [the longest x9 56.4 us: across(): lax.ppermute(a, 'expert', [(e, e ^ (4 if e & 1 else 2)) for e in range(n_...]
    gather x4 -> x0, local copies, waits for them, and re-layouts: 40.5 us -> none  [the longest x1 17.7 us: per_device(): jnp.take(came_back.reshape(experts_all * capacity, width), slot_index, ax...]
    ppermute x0 -> x26, starting transfers between devices: none -> 32.2 us  [the longest x14 12.9 us: beside(): return lax.ppermute(a, 'expert', [(e, e ^ 1) for e in range(n_ex)])]
    dot_general x5 -> x0, matrix products: 31.5 us -> none  [the longest x1 14.2 us: run_experts(): jnp.einsum('secf,efd->secd', active, expert_down_weight, preferred_elemen...]
  transfers between devices with their start and end apart: 4 -> 26, of which waited for: 3 -> 8; matrix products, arithmetic and copies ran while one was open for 12% -> 4% of each run, Pallas kernels for 0% -> 38%
where the time goes in v1:
time: 170 us; the launch traced here: 169 us
  Pallas kernels  63.7 us (37%)
  waiting for transfers between devices  62 us (36%)
  starting transfers between devices  32.2 us (19%)
  local copies, waits for them, and re-layouts  6.79 us (4%)
  other arithmetic  4.32 us (3%)
    ppermute x9, waiting for transfers between devices, across(): lax.ppermute(a, 'expert', [(e, e ^ (4 if e & 1 else 2)) for e in range(n_...  56.4 us
    pallas_call x3, Pallas kernels, run_experts(): call(functools.partial(experts_kernel, groups, blocks), 'experts', (out,)...  40.1 us
    ppermute x14, starting transfers between devices, beside(): return lax.ppermute(a, 'expert', [(e, e ^ 1) for e in range(n_ex)])  12.9 us
    pallas_call x1, Pallas kernels, attend(): pl.pallas_call(attend_kernel, name='attend', grid=(pairs,), out_shape=jax...  12.8 us
    ppermute x9, starting transfers between devices, across(): lax.ppermute(a, 'expert', [(e, e ^ (4 if e & 1 else 2)) for e in range(n_...  9.96 us
    ppermute x3, starting transfers between devices, along(): return lax.ppermute(a, both, pairs)  9.39 us
    pallas_call x1, Pallas kernels, project(): call(functools.partial(project_kernel, len(pools), len(shards), rank), 'p...  7.84 us
    ppermute x14, waiting for transfers between devices, beside(): return lax.ppermute(a, 'expert', [(e, e ^ 1) for e in range(n_ex)])  5.56 us
  transfers between devices with their start and end apart: 26, of which 8 were waited for; matrix products, arithmetic and copies ran while one was open for 4% of the time, Pallas kernels for 38%

profile of v1, /device:TPU:0, one launch (start us, length us, event | category | flops | bytes accessed | tf_op | source)
XLA Modules:
  0.0 169.2 jit_solution(8119603135351795335)
XLA Ops:
  0.0 5.9 %collective-permute-start.7 = (bf16[384,1536]{1,0:T(8,128)(2,1)}, bf16[384,1536]{1,0:T(8,128)(2,1)}, u32[]{:S(2)}, u32[]{:S(2)}) collective-permute-start(bf16[384,1536]{1,0:T(8,128)(2,1)} %refs_14_.1), channel_id=1, source_target_pairs={{0,8},{8,16},{16,24},{9,1},{17,9},{25,17},{2,10},{10,18},{18,26},{... | collective-permute-start | bytes 3538952 | tf_op jit(solution)/shard_map/ppermute | solution.py:376
  5.9 1.5 copy.16.logits_ref
  7.4 1.5 copy.17.routes_ref
  8.9 3.0 %prepare.1.refs_6_.refs_1_ = bf16[256,1664]{1,0:T(8,128)(2,1)} custom-call(f32[256,8]{1,0:T(8,128)} %copy.16.logits_ref, s32[256,8]{1,0:T(8,128)} %copy.17.routes_ref, bf16[8,16,1536]{2,1,0:T(8,128)(2,1)} %bitcast.16, bf16[8,16,1536]{2,1,0:T(8,128)(2,1)} %up_ref.1), custom_call_target="tpu_custom_call" | custom-call | flops 1000000 | bytes 2000000 | tf_op jit(solution)/shard_map/prepare/pallas_call | solution.py:114
  11.9 1.5 collective-permute-start.1
  13.4 11.4 %collective-permute-done.1.refs_8_.refs_2_ = bf16[256,1664]{1,0:T(8,128)(2,1)S(1)} collective-permute-done((bf16[256,1664]{1,0:T(8,128)(2,1)}, bf16[256,1664]{1,0:T(8,128)(2,1)S(1)}, u32[]{:S(2)}, u32[]{:S(2)}) %collective-permute-start.1) | collective-permute-done | bytes 852000 | tf_op jit(solution)/shard_map/ppermute | solution.py:366
  24.8 1.7 %collective-permute-start.9 = (bf16[384,1536]{1,0:T(8,128)(2,1)}, bf16[384,1536]{1,0:T(8,128)(2,1)}, u32[]{:S(2)}, u32[]{:S(2)}) collective-permute-start(bf16[384,1536]{1,0:T(8,128)(2,1)} %collective-permute-done.7.refs_15_), channel_id=1, source_target_pairs={{8,16},{16,24},{9,1},{17,9},{10,18},{18,26},{11,3},{19,11},{12,20}... | collective-permute-start | bytes 3538952 | tf_op jit(solution)/shard_map/ppermute | solution.py:376
  26.5 1.5 collective-permute-start.2
  28.7 1.7 %collective-permute-start.11 = (bf16[384,1536]{1,0:T(8,128)(2,1)}, bf16[384,1536]{1,0:T(8,128)(2,1)}, u32[]{:S(2)}, u32[]{:S(2)}) collective-permute-start(bf16[384,1536]{1,0:T(8,128)(2,1)} %collective-permute-done.9.refs_17_), channel_id=1, source_target_pairs={{16,24},{9,1},{18,26},{11,3},{20,28},{13,5},{22,30},{15,7}} | collective-permute-start | bytes 3538952 | tf_op jit(solution)/shard_map/ppermute | solution.py:376
  30.4 8.8 %collective-permute-done.2.refs_9_.refs_3_ = bf16[256,1664]{1,0:T(8,128)(2,1)S(1)} collective-permute-done((bf16[256,1664]{1,0:T(8,128)(2,1)S(1)}, bf16[256,1664]{1,0:T(8,128)(2,1)S(1)}, u32[]{:S(2)}, u32[]{:S(2)}) %collective-permute-start.2) | collective-permute-done | bytes 852000 | tf_op jit(solution)/shard_map/ppermute | solution.py:366
  39.2 4.9 %collective-permute-start.4 = (bf16[256,1664]{1,0:T(8,128)(2,1)S(1)}, bf16[256,1664]{1,0:T(8,128)(2,1)S(1)}, u32[]{:S(2)}, u32[]{:S(2)}) collective-permute-start(bf16[256,1664]{1,0:T(8,128)(2,1)S(1)} %collective-permute-done.2.refs_9_.refs_3_), channel_id=1, source_target_pairs={{0,1},{1,0},{2,3},{3,2},{4,5},{5,4},{6,7},{7,6},{8,9},{9,8},{10,11... | collective-permute-start | bytes 2555912 | tf_op jit(solution)/shard_map/ppermute | solution.py:363
  44.1 4.2 %collective-permute-done.5.refs_12_.refs_1_ = bf16[256,1664]{1,0:T(8,128)(2,1)S(1)} collective-permute-done((bf16[256,1664]{1,0:T(8,128)(2,1)S(1)}, bf16[256,1664]{1,0:T(8,128)(2,1)S(1)}, u32[]{:S(2)}, u32[]{:S(2)}) %collective-permute-start.5) | collective-permute-done | bytes 852000 | tf_op jit(solution)/shard_map/ppermute | solution.py:366
  48.4 0.9 copy-done.1
  50.3 2.5 %collective-permute-done.6.refs_13_ = bf16[256,1664]{1,0:T(8,128)(2,1)S(1)} collective-permute-done((bf16[256,1664]{1,0:T(8,128)(2,1)S(1)}, bf16[256,1664]{1,0:T(8,128)(2,1)S(1)}, u32[]{:S(2)}, u32[]{:S(2)}) %collective-permute-start.6) | collective-permute-done | bytes 852000 | tf_op jit(solution)/shard_map/ppermute | solution.py:363
  53.0 0.8 copy-done.9
  53.7 6.3 %collective-permute-start.12 = (bf16[384,1536]{1,0:T(8,128)(2,1)}, bf16[384,1536]{1,0:T(8,128)(2,1)}, u32[]{:S(2)}, u32[]{:S(2)}) collective-permute-start(bf16[384,1536]{1,0:T(8,128)(2,1)} %collective-permute-done.11.refs_19_), channel_id=1, source_target_pairs={{0,1},{1,0},{2,3},{3,2},{4,5},{5,4},{6,7},{7,6},{8,9},{9,8},{10,11... | collective-permute-start | bytes 3538952 | tf_op jit(solution)/shard_map/ppermute | solution.py:363
  60.0 12.8 %attend.1.refs_3_ = bf16[256,1536]{1,0:T(8,128)(2,1)} custom-call(s32[1,4]{1,0:T(1,128)} %refs_2_.3, bf16[256,1536]{1,0:T(8,128)(2,1)} %q_ref.1, bf16[256,512]{1,0:T(8,128)(2,1)} %k_ref.1, bf16[256,512]{1,0:T(8,128)(2,1)} %v_ref.1), custom_call_target="tpu_custom_call" | custom-call | flops 16000000000 | bytes 2000000 | tf_op jit(solution)/shard_map/attend/pallas_call | solution.py:72
  73.4 0.7 stack.63.refs_0_
  74.1 7.8 %project.1 = (f32[256,1536]{1,0:T(8,128)}, bf16[256,1536]{1,0:T(8,128)(2,1)}) custom-call(s32[23]{0:T(128)} %stack.63.refs_0_, s32[4]{0:T(128)} %refs_1_.1, s32[1,4]{1,0:T(1,128)} %refs_2_.3, bf16[256,1536]{1,0:T(8,128)(2,1)} %attend.1.refs_3_, bf16[256,1536]{1,0:T(8,128)(2,1)} %refs_4_.4, f32[1,1536]{1,0:T(1,128)} %reshape.3.refs_5_, ...), custom_call_target="tpu_custom_call" | custom-call | flops 4000000000 | bytes 10000000 | tf_op jit(solution)/shard_map/project/pallas_call | solution.py:199
  82.0 1.6 collective-permute-start.16
  83.5 10.7 %collective-permute-done.16.refs_0_ = bf16[256,1536]{1,0:T(8,128)(2,1)S(1)} collective-permute-done((bf16[256,1536]{1,0:T(8,128)(2,1)}, bf16[256,1536]{1,0:T(8,128)(2,1)S(1)}, u32[]{:S(2)}, u32[]{:S(2)}) %collective-permute-start.16) | collective-permute-done | bytes 786464 | tf_op jit(solution)/shard_map/ppermute | solution.py:366
  94.2 0.9 copy-done.11
  95.6 3.0 %collective-permute-done.19 = bf16[256,1536]{1,0:T(8,128)(2,1)} collective-permute-done((bf16[256,1536]{1,0:T(8,128)(2,1)S(1)}, bf16[256,1536]{1,0:T(8,128)(2,1)}, u32[]{:S(2)}, u32[]{:S(2)}) %collective-permute-start.19) | collective-permute-done | bytes 786464 | tf_op jit(solution)/shard_map/ppermute | solution.py:363
  98.6 1.5 collective-permute-start.20
  101.3 9.7 %collective-permute-done.20.refs_0_ = bf16[256,1536]{1,0:T(8,128)(2,1)} collective-permute-done((bf16[256,1536]{1,0:T(8,128)(2,1)}, bf16[256,1536]{1,0:T(8,128)(2,1)}, u32[]{:S(2)}, u32[]{:S(2)}) %collective-permute-start.20) | collective-permute-done | bytes 786464 | tf_op jit(solution)/shard_map/ppermute | solution.py:366
  110.9 11.5 %experts.5 = bf16[256,1536]{1,0:T(8,128)(2,1)} custom-call(s32[4]{0:T(128)} %pad_add_fusion.first_ref, bf16[256,1536]{1,0:T(8,128)(2,1)} %collective-permute-done.20.refs_0_, bf16[256,1664]{1,0:T(8,128)(2,1)} %copy-done.1, bf16[2,1536,512]{2,1,0:T(8,128)(2,1)} %refs_2_.5, bf16[2,1536,512]{2,1,0:T(8,128)(2,1)} %refs_3_.3, bf16[2,512,1536]{2,1,0:T(8,128)(2,1)} %refs_4_.7, ...), custom_call_target="tpu_custom_call" | custom-call | flops 4831838208 | bytes 18874368 | tf_op jit(solution)/shard_map/experts/pallas_call | solution.py:283
  122.5 1.6 collective-permute-start.21
  124.0 17.0 %experts.4 = (bf16[256,1536]{1,0:T(8,128)(2,1)}, bf16[256,1536]{1,0:T(8,128)(2,1)}) custom-call(s32[4]{0:T(128)} %pad_add_fusion.first_ref, bf16[256,1536]{1,0:T(8,128)(2,1)} %copy-done.11, bf16[256,1536]{1,0:T(8,128)(2,1)} %collective-permute-done.18.refs_1_, bf16[256,1664]{1,0:T(8,128)(2,1)} %copy-done.4, bf16[256,1664]{1,0:T(8,128)(2,1)} %copy-done.5, ...), custom_call_target="tpu_custom_call" | custom-call | flops 9663676416 | bytes 18874368 | tf_op jit(solution)/shard_map/experts/pallas_call | solution.py:283
  141.7 11.7 %collective-permute-done.24 = bf16[256,1536]{1,0:T(8,128)(2,1)S(1)} collective-permute-done((bf16[256,1536]{1,0:T(8,128)(2,1)}, bf16[256,1536]{1,0:T(8,128)(2,1)S(1)}, u32[]{:S(2)}, u32[]{:S(2)}) %collective-permute-start.24) | collective-permute-done | bytes 786464 | tf_op jit(solution)/shard_map/ppermute | solution.py:366
  153.4 1.3 add_convert_fusion.1
  155.3 11.5 %experts.3 = bf16[256,1536]{1,0:T(8,128)(2,1)} custom-call(s32[4]{0:T(128)} %pad_add_fusion.first_ref, bf16[256,1536]{1,0:T(8,128)(2,1)} %get-tuple-element.10.refs_0_, bf16[256,1664]{1,0:T(8,128)(2,1)} %prepare.1.refs_6_.refs_1_, bf16[2,1536,512]{2,1,0:T(8,128)(2,1)} %refs_2_.5, bf16[2,1536,512]{2,1,0:T(8,128)(2,1)} %refs_3_.3, ...), custom_call_target="tpu_custom_call" | custom-call | flops 4831838208 | bytes 18874368 | tf_op jit(solution)/shard_map/experts/pallas_call | solution.py:283
  166.8 2.4 %add_convert_fusion = bf16[256,1536]{1,0:T(8,128)(2,1)} fusion(f32[256,1536]{1,0:T(8,128)S(1)} %copy-done.2, bf16[256,1536]{1,0:T(8,128)(2,1)S(1)} %collective-permute-done.25, bf16[256,1536]{1,0:T(8,128)(2,1)S(1)} %collective-permute-done.23, bf16[256,1536]{1,0:T(8,128)(2,1)} %experts.3), kind=kLoop, calls=%fused_computation | loop fusion | flops 2752512 | bytes 4718592 | tf_op jit(solution)/shard_map/convert_element_type | solution.py:419
  (58 shorter events, 5.3 us)
Async XLA Ops:
  0.0 24.8 %collective-permute-start.7 = (bf16[384,1536]{1,0:T(8,128)(2,1)}, bf16[384,1536]{1,0:T(8,128)(2,1)}, u32[]{:S(2)}, u32[]{:S(2)}) collective-permute-start(bf16[384,1536]{1,0:T(8,128)(2,1)} %refs_14_.1), channel_id=1, source_target_pairs={{0,8},{8,16},{16,24},{9,1},{17,9},{25,17},{2,10},{10,18},{18,26},{... | collective-permute-start | bytes 3538952 | tf_op jit(solution)/shard_map/ppermute | solution.py:376
  11.9 60.9 %copy-start.10 = (f32[1536]{0:T(1024)S(1)}, f32[1536]{0:T(1024)}, u32[]{:S(2)}) copy-start(f32[1536]{0:T(1024)} %param.24) | copy-start | bytes 18436
  11.9 12.9 %collective-permute-start.1 = (bf16[256,1664]{1,0:T(8,128)(2,1)}, bf16[256,1664]{1,0:T(8,128)(2,1)S(1)}, u32[]{:S(2)}, u32[]{:S(2)}) collective-permute-start(bf16[256,1664]{1,0:T(8,128)(2,1)} %prepare.1.refs_6_.refs_1_), channel_id=1, source_target_pairs={{0,2},{1,5},{2,0},{3,7},{4,6},{5,1},{6,4},{7,3},{8,10},{9,13},{10,... | collective-permute-start | bytes 2555912 | tf_op jit(solution)/shard_map/ppermute | solution.py:366
  13.4 13.1 %collective-permute-start = (bf16[256,1664]{1,0:T(8,128)(2,1)}, bf16[256,1664]{1,0:T(8,128)(2,1)S(1)}, u32[]{:S(2)}, u32[]{:S(2)}) collective-permute-start(bf16[256,1664]{1,0:T(8,128)(2,1)} %prepare.1.refs_6_.refs_1_), channel_id=1, source_target_pairs={{0,1},{1,0},{2,3},{3,2},{4,5},{5,4},{6,7},{7,6},{8,9},{9,8},{10,11... | collective-permute-start | bytes 2555912 | tf_op jit(solution)/shard_map/ppermute | solution.py:363
  24.8 23.5 %copy-start.4 = (bf16[256,1664]{1,0:T(8,128)(2,1)}, bf16[256,1664]{1,0:T(8,128)(2,1)S(1)}, u32[]{:S(2)}) copy-start(bf16[256,1664]{1,0:T(8,128)(2,1)S(1)} %collective-permute-done.1.refs_8_.refs_2_) | copy-start | bytes 2555908
  24.8 3.2 %collective-permute-start.3 = (bf16[256,1664]{1,0:T(8,128)(2,1)S(1)}, bf16[256,1664]{1,0:T(8,128)(2,1)S(1)}, u32[]{:S(2)}, u32[]{:S(2)}) collective-permute-start(bf16[256,1664]{1,0:T(8,128)(2,1)S(1)} %collective-permute-done.1.refs_8_.refs_2_), channel_id=1, source_target_pairs={{0,1},{1,0},{2,3},{3,2},{4,5},{5,4},{6,7},{7,6},{8,9},{9,8},{10,11... | collective-permute-start | bytes 2555912 | tf_op jit(solution)/shard_map/ppermute | solution.py:363
  24.8 3.9 %collective-permute-start.9 = (bf16[384,1536]{1,0:T(8,128)(2,1)}, bf16[384,1536]{1,0:T(8,128)(2,1)}, u32[]{:S(2)}, u32[]{:S(2)}) collective-permute-start(bf16[384,1536]{1,0:T(8,128)(2,1)} %collective-permute-done.7.refs_15_), channel_id=1, source_target_pairs={{8,16},{16,24},{9,1},{17,9},{10,18},{18,26},{11,3},{19,11},{12,20}... | collective-permute-start | bytes 3538952 | tf_op jit(solution)/shard_map/ppermute | solution.py:376
  26.5 21.8 %copy-start.6 = (bf16[256,1664]{1,0:T(8,128)(2,1)}, bf16[256,1664]{1,0:T(8,128)(2,1)S(1)}, u32[]{:S(2)}) copy-start(bf16[256,1664]{1,0:T(8,128)(2,1)S(1)} %collective-permute-done.refs_7_) | copy-start | bytes 2555908
  26.5 12.7 %collective-permute-start.2 = (bf16[256,1664]{1,0:T(8,128)(2,1)S(1)}, bf16[256,1664]{1,0:T(8,128)(2,1)S(1)}, u32[]{:S(2)}, u32[]{:S(2)}) collective-permute-start(bf16[256,1664]{1,0:T(8,128)(2,1)S(1)} %collective-permute-done.refs_7_), channel_id=1, source_target_pairs={{0,2},{1,5},{2,0},{3,7},{4,6},{5,1},{6,4},{7,3},{8,10},{9,13},{10,... | collective-permute-start | bytes 2555912 | tf_op jit(solution)/shard_map/ppermute | solution.py:366
  28.0 20.3 %copy-start.7 = (bf16[256,1664]{1,0:T(8,128)(2,1)}, bf16[256,1664]{1,0:T(8,128)(2,1)S(1)}, u32[]{:S(2)}) copy-start(bf16[256,1664]{1,0:T(8,128)(2,1)S(1)} %collective-permute-done.3.refs_10_) | copy-start | bytes 2555908
  28.0 20.3 %collective-permute-start.5 = (bf16[256,1664]{1,0:T(8,128)(2,1)S(1)}, bf16[256,1664]{1,0:T(8,128)(2,1)S(1)}, u32[]{:S(2)}, u32[]{:S(2)}) collective-permute-start(bf16[256,1664]{1,0:T(8,128)(2,1)S(1)} %collective-permute-done.3.refs_10_), channel_id=1, source_target_pairs={{0,2},{1,5},{2,0},{3,7},{4,6},{5,1},{6,4},{7,3},{8,10},{9,13},{10,... | collective-permute-start | bytes 2555912 | tf_op jit(solution)/shard_map/ppermute | solution.py:366
  28.7 21.1 %collective-permute-start.8 = (bf16[384,1536]{1,0:T(8,128)(2,1)}, bf16[384,1536]{1,0:T(8,128)(2,1)S(1)}, u32[]{:S(2)}, u32[]{:S(2)}) collective-permute-start(bf16[384,1536]{1,0:T(8,128)(2,1)} %collective-permute-done.7.refs_15_), channel_id=1, source_target_pairs={{0,1},{1,0},{2,3},{3,2},{4,5},{5,4},{6,7},{7,6},{8,9},{9,8},{10,11... | collective-permute-start | bytes 3538952 | tf_op jit(solution)/shard_map/ppermute | solution.py:363
  28.7 24.3 %collective-permute-start.11 = (bf16[384,1536]{1,0:T(8,128)(2,1)}, bf16[384,1536]{1,0:T(8,128)(2,1)}, u32[]{:S(2)}, u32[]{:S(2)}) collective-permute-start(bf16[384,1536]{1,0:T(8,128)(2,1)} %collective-permute-done.9.refs_17_), channel_id=1, source_target_pairs={{16,24},{9,1},{18,26},{11,3},{20,28},{13,5},{22,30},{15,7}} | collective-permute-start | bytes 3538952 | tf_op jit(solution)/shard_map/ppermute | solution.py:376
  39.2 13.7 %copy-start.5 = (bf16[256,1664]{1,0:T(8,128)(2,1)}, bf16[256,1664]{1,0:T(8,128)(2,1)S(1)}, u32[]{:S(2)}) copy-start(bf16[256,1664]{1,0:T(8,128)(2,1)S(1)} %collective-permute-done.2.refs_9_.refs_3_) | copy-start | bytes 2555908
  39.2 10.6 %collective-permute-start.4 = (bf16[256,1664]{1,0:T(8,128)(2,1)S(1)}, bf16[256,1664]{1,0:T(8,128)(2,1)S(1)}, u32[]{:S(2)}, u32[]{:S(2)}) collective-permute-start(bf16[256,1664]{1,0:T(8,128)(2,1)S(1)} %collective-permute-done.2.refs_9_.refs_3_), channel_id=1, source_target_pairs={{0,1},{1,0},{2,3},{3,2},{4,5},{5,4},{6,7},{7,6},{8,9},{9,8},{10,11... | collective-permute-start | bytes 2555912 | tf_op jit(solution)/shard_map/ppermute | solution.py:363
  49.3 3.6 %collective-permute-start.6 = (bf16[256,1664]{1,0:T(8,128)(2,1)S(1)}, bf16[256,1664]{1,0:T(8,128)(2,1)S(1)}, u32[]{:S(2)}, u32[]{:S(2)}) collective-permute-start(bf16[256,1664]{1,0:T(8,128)(2,1)S(1)} %collective-permute-done.5.refs_12_.refs_1_), channel_id=1, source_target_pairs={{0,1},{1,0},{2,3},{3,2},{4,5},{5,4},{6,7},{7,6},{8,9},{9,8},{10,11... | collective-permute-start | bytes 2555912 | tf_op jit(solution)/shard_map/ppermute | solution.py:363
  49.3 52.0 %collective-permute-start.13 = (bf16[2,1536,512]{2,1,0:T(8,128)(2,1)}, bf16[2,1536,512]{2,1,0:T(8,128)(2,1)S(1)}, u32[]{:S(2)}, u32[]{:S(2)}) collective-permute-start(bf16[2,1536,512]{2,1,0:T(8,128)(2,1)} %refs_2_.5), channel_id=1, source_target_pairs={{0,1},{1,0},{2,3},{3,2},{4,5},{5,4},{6,7},{7,6},{8,9},{9,8},{10,11... | collective-permute-start | bytes 9437192 | tf_op jit(solution)/shard_map/ppermute | solution.py:363
  49.8 51.5 %collective-permute-start.14 = (bf16[2,1536,512]{2,1,0:T(8,128)(2,1)}, bf16[2,1536,512]{2,1,0:T(8,128)(2,1)}, u32[]{:S(2)}, u32[]{:S(2)}) collective-permute-start(bf16[2,1536,512]{2,1,0:T(8,128)(2,1)} %refs_3_.3), channel_id=1, source_target_pairs={{0,1},{1,0},{2,3},{3,2},{4,5},{5,4},{6,7},{7,6},{8,9},{9,8},{10,11... | collective-permute-start | bytes 9437192 | tf_op jit(solution)/shard_map/ppermute | solution.py:363
  49.9 51.4 %collective-permute-start.15 = (bf16[2,512,1536]{2,1,0:T(8,128)(2,1)}, bf16[2,512,1536]{2,1,0:T(8,128)(2,1)}, u32[]{:S(2)}, u32[]{:S(2)}) collective-permute-start(bf16[2,512,1536]{2,1,0:T(8,128)(2,1)} %refs_4_.7), channel_id=1, source_target_pairs={{0,1},{1,0},{2,3},{3,2},{4,5},{5,4},{6,7},{7,6},{8,9},{9,8},{10,11... | collective-permute-start | bytes 9437192 | tf_op jit(solution)/shard_map/ppermute | solution.py:363
  52.8 21.3 %collective-permute-start.10 = (bf16[384,1536]{1,0:T(8,128)(2,1)}, bf16[384,1536]{1,0:T(8,128)(2,1)}, u32[]{:S(2)}, u32[]{:S(2)}) collective-permute-start(bf16[384,1536]{1,0:T(8,128)(2,1)} %collective-permute-done.9.refs_17_), channel_id=1, source_target_pairs={{0,1},{1,0},{2,3},{3,2},{4,5},{5,4},{6,7},{7,6},{8,9},{9,8},{10,11... | collective-permute-start | bytes 3538952 | tf_op jit(solution)/shard_map/ppermute | solution.py:363
  53.7 20.4 %collective-permute-start.12 = (bf16[384,1536]{1,0:T(8,128)(2,1)}, bf16[384,1536]{1,0:T(8,128)(2,1)}, u32[]{:S(2)}, u32[]{:S(2)}) collective-permute-start(bf16[384,1536]{1,0:T(8,128)(2,1)} %collective-permute-done.11.refs_19_), channel_id=1, source_target_pairs={{0,1},{1,0},{2,3},{3,2},{4,5},{5,4},{6,7},{7,6},{8,9},{9,8},{10,11... | collective-permute-start | bytes 3538952 | tf_op jit(solution)/shard_map/ppermute | solution.py:363
  82.0 12.3 %collective-permute-start.16 = (bf16[256,1536]{1,0:T(8,128)(2,1)}, bf16[256,1536]{1,0:T(8,128)(2,1)S(1)}, u32[]{:S(2)}, u32[]{:S(2)}) collective-permute-start(bf16[256,1536]{1,0:T(8,128)(2,1)} %get-tuple-element.10.refs_0_), channel_id=1, source_target_pairs={{0,2},{1,5},{2,0},{3,7},{4,6},{5,1},{6,4},{7,3},{8,10},{9,13},{10,... | collective-permute-start | bytes 2359304 | tf_op jit(solution)/shard_map/ppermute | solution.py:366
  95.1 3.5 %collective-permute-start.19 = (bf16[256,1536]{1,0:T(8,128)(2,1)S(1)}, bf16[256,1536]{1,0:T(8,128)(2,1)}, u32[]{:S(2)}, u32[]{:S(2)}) collective-permute-start(bf16[256,1536]{1,0:T(8,128)(2,1)S(1)} %collective-permute-done.16.refs_0_), channel_id=1, source_target_pairs={{0,1},{1,0},{2,3},{3,2},{4,5},{5,4},{6,7},{7,6},{8,9},{9,8},{10,11... | collective-permute-start | bytes 2359304 | tf_op jit(solution)/shard_map/ppermute | solution.py:363
  95.1 5.0 %collective-permute-start.17 = (bf16[256,1536]{1,0:T(8,128)(2,1)}, bf16[256,1536]{1,0:T(8,128)(2,1)}, u32[]{:S(2)}, u32[]{:S(2)}) collective-permute-start(bf16[256,1536]{1,0:T(8,128)(2,1)} %get-tuple-element.10.refs_0_), channel_id=1, source_target_pairs={{0,1},{1,0},{2,3},{3,2},{4,5},{5,4},{6,7},{7,6},{8,9},{9,8},{10,11... | collective-permute-start | bytes 2359304 | tf_op jit(solution)/shard_map/ppermute | solution.py:363
  98.6 12.3 %collective-permute-start.20 = (bf16[256,1536]{1,0:T(8,128)(2,1)}, bf16[256,1536]{1,0:T(8,128)(2,1)}, u32[]{:S(2)}, u32[]{:S(2)}) collective-permute-start(bf16[256,1536]{1,0:T(8,128)(2,1)} %collective-permute-done.19), channel_id=1, source_target_pairs={{0,2},{1,5},{2,0},{3,7},{4,6},{5,1},{6,4},{7,3},{8,10},{9,13},{10,... | collective-permute-start | bytes 2359304 | tf_op jit(solution)/shard_map/ppermute | solution.py:366
  100.1 23.9 %collective-permute-start.18 = (bf16[256,1536]{1,0:T(8,128)(2,1)}, bf16[256,1536]{1,0:T(8,128)(2,1)}, u32[]{:S(2)}, u32[]{:S(2)}) collective-permute-start(bf16[256,1536]{1,0:T(8,128)(2,1)} %collective-permute-done.17), channel_id=1, source_target_pairs={{0,2},{1,5},{2,0},{3,7},{4,6},{5,1},{6,4},{7,3},{8,10},{9,13},{10,... | collective-permute-start | bytes 2359304 | tf_op jit(solution)/shard_map/ppermute | solution.py:366
  122.5 19.2 %collective-permute-start.21 = (bf16[256,1536]{1,0:T(8,128)(2,1)}, bf16[256,1536]{1,0:T(8,128)(2,1)S(1)}, u32[]{:S(2)}, u32[]{:S(2)}) collective-permute-start(bf16[256,1536]{1,0:T(8,128)(2,1)} %experts.5), channel_id=1, source_target_pairs={{0,2},{1,5},{2,0},{3,7},{4,6},{5,1},{6,4},{7,3},{8,10},{9,13},{10,... | collective-permute-start | bytes 2359304 | tf_op jit(solution)/shard_map/ppermute | solution.py:366
  141.1 12.3 %collective-permute-start.24 = (bf16[256,1536]{1,0:T(8,128)(2,1)}, bf16[256,1536]{1,0:T(8,128)(2,1)S(1)}, u32[]{:S(2)}, u32[]{:S(2)}) collective-permute-start(bf16[256,1536]{1,0:T(8,128)(2,1)} %get-tuple-element.12), channel_id=1, source_target_pairs={{0,2},{1,5},{2,0},{3,7},{4,6},{5,1},{6,4},{7,3},{8,10},{9,13},{10,... | collective-permute-start | bytes 2359304 | tf_op jit(solution)/shard_map/ppermute | solution.py:366
  141.7 11.7 %collective-permute-start.22 = (bf16[256,1536]{1,0:T(8,128)(2,1)S(1)}, bf16[256,1536]{1,0:T(8,128)(2,1)S(1)}, u32[]{:S(2)}, u32[]{:S(2)}) collective-permute-start(bf16[256,1536]{1,0:T(8,128)(2,1)S(1)} %collective-permute-done.21), channel_id=1, source_target_pairs={{0,1},{1,0},{2,3},{3,2},{4,5},{5,4},{6,7},{7,6},{8,9},{9,8},{10,11... | collective-permute-start | bytes 2359304 | tf_op jit(solution)/shard_map/ppermute | solution.py:363
  153.3 13.5 %collective-permute-start.25 = (bf16[256,1536]{1,0:T(8,128)(2,1)S(1)}, bf16[256,1536]{1,0:T(8,128)(2,1)S(1)}, u32[]{:S(2)}, u32[]{:S(2)}) collective-permute-start(bf16[256,1536]{1,0:T(8,128)(2,1)S(1)} %collective-permute-done.24), channel_id=1, source_target_pairs={{0,1},{1,0},{2,3},{3,2},{4,5},{5,4},{6,7},{7,6},{8,9},{9,8},{10,11... | collective-permute-start | bytes 2359304 | tf_op jit(solution)/shard_map/ppermute | solution.py:363
  154.7 12.2 %copy-start.2 = (f32[256,1536]{1,0:T(8,128)S(1)}, f32[256,1536]{1,0:T(8,128)}, u32[]{:S(2)}) copy-start(f32[256,1536]{1,0:T(8,128)} %get-tuple-element.9) | copy-start | bytes 4718596
  154.7 12.1 %collective-permute-start.23 = (bf16[256,1536]{1,0:T(8,128)(2,1)S(1)}, bf16[256,1536]{1,0:T(8,128)(2,1)S(1)}, u32[]{:S(2)}, u32[]{:S(2)}) collective-permute-start(bf16[256,1536]{1,0:T(8,128)(2,1)S(1)} %add_convert_fusion.1), channel_id=1, source_target_pairs={{0,2},{1,5},{2,0},{3,7},{4,6},{5,1},{6,4},{7,3},{8,10},{9,13},{10,... | collective-permute-start | bytes 2359304 | tf_op jit(solution)/shard_map/ppermute | solution.py:366
  (6 other events, 18.5 us)

commit v2 on v1

v2 whole, which is shorter than its diff:
```python
import functools

import jax
import jax.numpy as jnp
from jax import lax
from jax.experimental import pallas as pl
from jax.experimental.pallas import tpu as pltpu
from jax.sharding import PartitionSpec as P

HEAD = 64
GROUPS = 3
BF16, F32 = jnp.bfloat16, jnp.float32
VMEM = pl.BlockSpec(memory_space=pltpu.VMEM)
SMEM = pl.BlockSpec(memory_space=pltpu.SMEM)
ANY = pl.BlockSpec(memory_space=pl.ANY)
MIB = 2**20


def call(kernel, name, out_shape, in_specs, out_specs, scratch, room, flops, **more):
    return pl.pallas_call(
        kernel,
        name=name,
        out_shape=out_shape,
        in_specs=in_specs,
        out_specs=out_specs,
        scratch_shapes=scratch,
        compiler_params=pltpu.CompilerParams(vmem_limit_bytes=room * MIB),
        cost_estimate=pl.CostEstimate(flops=flops, bytes_accessed=MIB, transcendentals=0),
        **more,
    )


def attend_kernel(lengths_ref, q_ref, k_ref, v_ref, o_ref, bias):
    tokens = q_ref.shape[0]
    half = tokens // 2

    @pl.when(pl.program_id(0) == 0)
    def _():
        row = lax.broadcasted_iota(jnp.int32, (tokens, tokens), 0)
        col = lax.broadcasted_iota(jnp.int32, (tokens, tokens), 1)
        same = row >= col
        end = 0
        for r in range(lengths_ref.shape[1]):
            end = end + lengths_ref[0, r]
            same = same & ((row < end) | (col >= end))
        bias[...] = jnp.where(same, 0.0, -1e30)

    for j in range(k_ref.shape[1] // HEAD):
        keys = k_ref[:, j * HEAD : (j + 1) * HEAD]
        values = v_ref[:, j * HEAD : (j + 1) * HEAD]
        for g in range(GROUPS):
            at = (j * GROUPS + g) * HEAD
            q = q_ref[:, at : at + HEAD] * jnp.asarray(HEAD**-0.5, BF16)
            for first, seen in ((0, half), (half, tokens)):
                s = lax.dot_general(
                    q[first : first + half],
                    keys[:seen],
                    (((1,), (1,)), ((), ())),
                    preferred_element_type=F32,
                )
                s = s + bias[first : first + half, :seen]
                p = jnp.exp(s - jnp.max(s, axis=-1, keepdims=True))
                w = (p * (1.0 / jnp.sum(p, axis=-1, keepdims=True))).astype(BF16)
                o = jnp.dot(w, values[:seen], preferred_element_type=F32)
                o_ref[first : first + half, at : at + HEAD] = o.astype(BF16)


def attend(lengths, q, k, v, first, pairs):
    tokens = q.shape[0]
    wide = 2 * GROUPS * HEAD
    return pl.pallas_call(
        attend_kernel,
        name="attend",
        grid=(pairs,),
        out_shape=jax.ShapeDtypeStruct((tokens, wide * pairs), BF16),
        in_specs=[
            SMEM,
            pl.BlockSpec((tokens, wide), lambda i: (0, first + i)),
            pl.BlockSpec((tokens, 2 * HEAD), lambda i: (0, first + i)),
            pl.BlockSpec((tokens, 2 * HEAD), lambda i: (0, first + i)),
        ],
        out_specs=pl.BlockSpec((tokens, wide), lambda i: (0, i)),
        scratch_shapes=[pltpu.VMEM((tokens, tokens), F32)],
        compiler_params=pltpu.CompilerParams(vmem_limit_bytes=8 * MIB),
        cost_estimate=pl.CostEstimate(flops=10**9, bytes_accessed=MIB, transcendentals=0),
    )(lengths, q, k, v)


def prepare_kernel(logits_ref, routes_ref, down_ref, up_ref, gain_ref, pool_ref):
    top, tokens = logits_ref.shape
    logits = logits_ref[...]
    raised = jnp.exp(logits - jnp.max(logits, axis=0, keepdims=True))
    gates = raised / jnp.sum(raised, axis=0, keepdims=True)
    expert = lax.broadcasted_iota(jnp.int32, (64, tokens), 0)
    gain = jnp.zeros((64, tokens), F32)
    for j in range(top):
        gain = gain + jnp.where(expert == routes_ref[j : j + 1], gates[j : j + 1], 0.0)
    high = gain.astype(BF16).astype(F32)
    gain_ref[...] = jnp.concatenate([high, gain - high], axis=0).T.astype(BF16)
    count, rank, _ = down_ref.shape
    for a in range(count):
        pool_ref[2 * rank * a : 2 * rank * a + rank] = down_ref[a]
        pool_ref[2 * rank * a + rank : 2 * rank * (a + 1)] = up_ref[a]


def prepare_joined_kernel(logits_ref, routes_ref, down_ref, up_ref, o_ref):
    width = down_ref.shape[2]
    prepare_kernel(
        logits_ref, routes_ref, down_ref, up_ref, o_ref.at[:, width:], o_ref.at[:, :width]
    )


def prepare(logits, routes, down, up, joined):
    tokens = logits.shape[1]
    count, rank, width = up.shape
    apart = (
        jax.ShapeDtypeStruct((tokens, 128), BF16),
        jax.ShapeDtypeStruct((2 * rank * count, width), BF16),
    )
    return call(
        prepare_joined_kernel if joined else prepare_kernel,
        "prepare",
        jax.ShapeDtypeStruct((tokens, width + 128), BF16) if joined else apart,
        [VMEM] * 4,
        VMEM if joined else (VMEM, VMEM),
        [],
        4,
        10**6,
    )(logits, routes, down, up)


def each_shard(starts, shard, wo_s, sem, do):
    for k, at in enumerate(starts):
        rows = shard[k].shape[0]

        @pl.when(at >= 0)
        def _():
            to = wo_s.at[pl.ds(pl.multiple_of(at, rows), rows)]
            do(pltpu.make_async_copy(shard[k], to, sem.at[k]))


def project_kernel(owners, sources, rank, held, *refs):
    pools, shards = len(owners), len(sources)
    ids, lengths, res_ref = refs[:3]
    ctx = refs[3:-5 - 1 - pools - shards]
    pool = refs[-6 - pools - shards : -6 - shards]
    shard = refs[-6 - shards : -6]
    hidden_ref, low_s, up_s, wo_s, sem_a, sem_w = refs[-6:]
    requests = ids.shape[0]
    tokens, width = res_ref.shape
    z, i = lax.axis_index("dp"), lax.axis_index("expert")
    starts = [f(z, i) for f in sources]
    each_shard(starts, shard, wo_s, sem_w, lambda c: c.start())
    for r in range(requests):
        for k in range(pools):
            at = ids[r] - owners[k](i) * held

            @pl.when((at >= 0) & (at < pool[k].shape[0] // (2 * rank)))
            def _():
                first = pl.multiple_of(at * (2 * rank), 2 * rank)
                for half, to in ((0, low_s), (1, up_s)):
                    pltpu.make_async_copy(
                        pool[k].at[pl.ds(first + half * rank, rank), pl.ds(0, width)],
                        to.at[pl.ds(r * rank, rank)],
                        sem_a.at[r, half],
                    ).start()

    for r in range(requests):
        for half, to in ((0, low_s), (1, up_s)):
            pltpu.make_async_copy(
                pool[0].at[pl.ds(0, rank), pl.ds(0, width)],
                to.at[pl.ds(r * rank, rank)],
                sem_a.at[r, half],
            ).wait()
    low, at = 0.0, 0
    for c in ctx:
        low = low + lax.dot_general(
            c[...],
            low_s[:, at : at + c.shape[1]],
            (((1,), (1,)), ((), ())),
            preferred_element_type=F32,
        )
        at += c.shape[1]
    row = lax.broadcasted_iota(jnp.int32, low.shape, 0)
    lane = lax.broadcasted_iota(jnp.int32, low.shape, 1)
    end = 0
    mine = lane < 0
    for r in range(requests):
        start, end = end, end + lengths[0, r]
        inside = (row >= start) & (row < end)
        mine = mine | (inside & (lane >= r * rank) & (lane < (r + 1) * rank))
    low = jnp.where(mine, low, 0.0).astype(BF16)
    hidden_ref[...] = res_ref[...].astype(F32) + jnp.dot(
        low, up_s[...], preferred_element_type=F32
    )
    each_shard(starts, shard, wo_s, sem_w, lambda c: c.wait())
    for at, piece in zip(starts, shard):
        add_shard(at, piece.shape[0], ctx, wo_s, hidden_ref)


def add_shard(at, rows, ctx, wo_s, hidden_ref):
    covered = 0
    for c in ctx:
        wide = min(rows, c.shape[1])
        for first in range(0, c.shape[1], wide):

            @pl.when((at >= 0) & (covered + first >= at) & (covered + first < at + rows))
            def _():
                hidden_ref[...] += jnp.dot(
                    c[:, first : first + wide],
                    wo_s[covered + first : covered + first + wide],
                    preferred_element_type=F32,
                )

        covered += c.shape[1]


def project(ids, lengths, ctx, residual, pools, owners, shards, sources, rank, held):
    tokens, width = residual.shape
    requests = ids.shape[0]
    return call(
        functools.partial(project_kernel, owners, sources, rank, held),
        "project",
        jax.ShapeDtypeStruct((tokens, width), F32),
        [SMEM] * 2 + [VMEM] * (1 + len(ctx)) + [ANY] * (len(pools) + len(shards)),
        VMEM,
        [
            pltpu.VMEM((requests * rank, width), BF16),
            pltpu.VMEM((requests * rank, width), BF16),
            pltpu.VMEM((width, width), BF16),
            pltpu.SemaphoreType.DMA((requests, 2)),
            pltpu.SemaphoreType.DMA((len(shards),)),
        ],
        12,
        10**9,
    )(ids, lengths, residual, *ctx, *pools, *shards)


def normalise_kernel(sources, *refs):
    shards = len(sources)
    scale_ref, part_ref = refs[:2]
    if shards:
        ctx, shard = refs[2 : -4 - shards], refs[-4 - shards : -4]
        hidden_ref, normed_ref, wo_s, sem = refs[-4:]
        z, i = lax.axis_index("dp"), lax.axis_index("expert")
        starts = [f(z, i) for f in sources]
        each_shard(starts, shard, wo_s, sem, lambda c: c.start())
    else:
        hidden_ref, normed_ref = refs[-2:]
    hidden_ref[...] = part_ref[...]
    if shards:
        each_shard(starts, shard, wo_s, sem, lambda c: c.wait())
        for at, piece in zip(starts, shard):
            add_shard(at, piece.shape[0], ctx, wo_s, hidden_ref)
    h = hidden_ref[...]
    width = h.shape[1]
    inv = lax.rsqrt(jnp.sum(h * h, axis=-1, keepdims=True) * (1.0 / width) + 1e-06)
    normed_ref[...] = (h * inv * scale_ref[...].reshape(1, width)).astype(BF16)


def normalise(scale, part, ctx, shards, sources):
    tokens, width = part.shape
    extra = [pltpu.VMEM((width, width), BF16), pltpu.SemaphoreType.DMA((len(shards),))]
    more = (*ctx, *shards) if shards else ()
    return call(
        functools.partial(normalise_kernel, sources),
        "normalise",
        (
            jax.ShapeDtypeStruct((tokens, width), F32),
            jax.ShapeDtypeStruct((tokens, width), BF16),
        ),
        [VMEM] * 2 + ([VMEM] * len(ctx) + [ANY] * len(shards) if shards else []),
        (VMEM, VMEM),
        extra if shards else [],
        12,
        10**8,
    )(scale, part, *more)


def experts_kernel(groups, spread, x_ref, gain_ref, *refs):
    w, out_ref = refs[: 3 * groups], refs[3 * groups]
    total_ref, strip, sem = refs[3 * groups + 1 :]
    local = w[0].shape[0]
    total = groups * local
    pull = pltpu.make_async_copy(
        gain_ref.at[:, pl.ds(gain_ref.shape[1] - 128, 128)], strip, sem
    )
    pull.start()
    i = lax.axis_index("expert")
    x = x_ref[...]
    for e in range(total):
        g, own = divmod(e, local)
        gate = jnp.dot(x, w[3 * g][own], preferred_element_type=F32)
        up = jnp.dot(x, w[3 * g + 1][own], preferred_element_type=F32)
        if e == 0:
            pull.wait()
        number = spread(i, g) * local + own
        gain = strip[...].astype(F32)
        lane = lax.broadcasted_iota(jnp.int32, gain.shape, 1)
        coef = jnp.sum(jnp.where((lane & 63) == number, gain, 0.0), axis=-1, keepdims=True)
        act = (gate / (1.0 + jnp.exp(-gate)) * up * coef).astype(BF16)
        down = jnp.dot(act, w[3 * g + 2][own], preferred_element_type=F32)
        if total == 1:
            out_ref[...] = down.astype(BF16)
        elif e == 0:
            total_ref[...] = down
        elif e < total - 1:
            total_ref[...] += down
        else:
            out_ref[...] = (total_ref[...] + down).astype(BF16)


def run_experts(x, gain, weights, spread):
    groups = len(weights) // 3
    tokens, width = x.shape
    return call(
        functools.partial(experts_kernel, groups, spread),
        "experts",
        jax.ShapeDtypeStruct((tokens, width), BF16),
        [VMEM, ANY] + [VMEM] * (3 * groups),
        VMEM,
        [
            pltpu.VMEM((tokens, width), F32),
            pltpu.VMEM((tokens, 128), BF16),
            pltpu.SemaphoreType.DMA,
        ],
        12,
        10**9,
    )(x, gain, *weights)


def per_device(
    queries,
    rotated_key_heads,
    token_value_heads,
    residual,
    lengths,
    request_adapter_index,
    attention_output_weight,
    adapter_down_factor,
    adapter_up_factor,
    expert_norm_scale,
    router_logit_scores,
    routes,
    expert_gate_weight,
    expert_up_weight,
    expert_down_weight,
):
    tokens = queries.shape[0]
    rank = adapter_up_factor.shape[1]
    held = adapter_up_factor.shape[0]
    n_dp, n_ex = lax.axis_size("dp"), lax.axis_size("expert")
    rows, width = attention_output_weight.shape
    down_t = jnp.swapaxes(adapter_down_factor, 1, 2)
    weights = (expert_gate_weight, expert_up_weight, expert_down_weight)
    paired = n_ex == 8 and held * 2 * rank == tokens
    qkv = (lengths, queries, rotated_key_heads, token_value_heads)
    pairs = rotated_key_heads.shape[1] // (2 * HEAD)
    known = (request_adapter_index, lengths)
    packed = prepare(router_logit_scores.T, routes.T, down_t, adapter_up_factor, paired)

    if not paired:
        gains, pool = packed
        context = [attend(*qkv, 0, pairs)]
        shard = lax.all_gather(attention_output_weight, "dp", axis=0, tiled=True)
        pool = lax.all_gather(pool, "expert", axis=0, tiled=True)
        part = project(
            *known,
            context,
            residual,
            [pool],
            [lambda i: 0],
            [shard],
            [lambda z, i: z * 0],
            rank,
            held,
        )
        hidden, normed = normalise(expert_norm_scale, part, context, [], [])
        every = lax.all_gather(normed, "expert", axis=0, tiled=True)
        every_gain = lax.all_gather(gains, "expert", axis=0, tiled=True)
        parts = [
            run_experts(
                every[d * tokens : (d + 1) * tokens],
                every_gain[d * tokens : (d + 1) * tokens],
                weights,
                lambda i, g: i,
            )
            for d in range(n_ex)
        ]
        mixture = lax.psum_scatter(
            jnp.concatenate(parts, axis=0), "expert", scatter_dimension=0, tiled=True
        )
        return (hidden + mixture.astype(F32)).astype(BF16)

    def beside(a):
        return lax.ppermute(a, "expert", [(e, e ^ 1) for e in range(n_ex)])

    def across(a):
        return lax.ppermute(a, "expert", [(e, e ^ (4 if e & 1 else 2)) for e in range(n_ex)])

    def along(a, step):
        sent = []
        for e in range(n_ex):
            for d in range(n_dp):
                to = d - 1 if e & 1 else d + 1
                origin = d + step - 1 if e & 1 else d - step + 1
                if 0 <= to < n_dp and 0 <= origin < n_dp:
                    sent.append((d * n_ex + e, to * n_ex + e))
        return lax.ppermute(a, ("dp", "expert"), sent)

    def after(a, *others):
        return lax.optimization_barrier((a, *others))[0]

    def first_row(step, side):
        def at(z, i):
            source = z + side * step * (1 - 2 * (i & 1))
            return jnp.where((source >= 0) & (source < n_dp), source * rows, -1)

        return at

    own = packed
    z1 = along(attention_output_weight, 1)
    p0 = across(own)
    other = beside(own)
    p1 = across(other)
    half = pairs // 2
    ctx0 = attend(*qkv, 0, half)
    z2 = along(after(z1, ctx0), 2)
    p0_other = beside(after(p0, ctx0))
    p2 = across(p0_other)
    pair_weights = tuple(beside(after(w, p0_other)) for w in weights)
    ctx1 = attend(*qkv, half, pairs - half)
    z3 = along(after(z2, ctx1), 3)
    p1_other, p2_other = beside(p1), beside(p2)
    z1_other, z2_other, z3_other = beside(z1), beside(z2), beside(z3)
    context = [ctx0, ctx1]
    owners = [
        lambda i: i,
        lambda i: i ^ 1,
        lambda i: i ^ (2 + 2 * (i & 1)),
        lambda i: i ^ (3 + 2 * (i & 1)),
        lambda i: i ^ (5 - 2 * (i & 1)),
        lambda i: i ^ (4 - 2 * (i & 1)),
        lambda i: i ^ 7,
        lambda i: i ^ 6,
    ]
    part = project(
        *known,
        context,
        residual,
        [own, other, p0, p1, p0_other, p1_other, p2, p2_other],
        owners,
        [attention_output_weight, z1, z1_other, z2, z2_other],
        [lambda z, i: z * rows] + [first_row(s, side) for s in (1, 2) for side in (-1, 1)],
        rank,
        held,
    )
    hidden, normed = normalise(
        expert_norm_scale, part, context, [z3, z3_other], [first_row(3, -1), first_row(3, 1)]
    )
    b0 = across(normed)
    b1 = across(beside(normed))
    run = functools.partial(
        run_experts, weights=weights + pair_weights, spread=lambda i, g: i ^ g
    )
    home = run(normed, own)
    far = across(beside(after(b0, home)))
    r0 = run(after(b0, home), p0)
    r1 = run(after(b1, r0), p1)
    back1 = beside(across(r1))
    r_far = run(after(far, r1), p2)
    via = beside(across(r_far))
    back0 = across((r0.astype(F32) + via.astype(F32)).astype(BF16))
    mixture = home.astype(F32) + back0.astype(F32) + back1.astype(F32)
    return (hidden + mixture).astype(BF16)


def solution(mesh):
    return jax.shard_map(
        per_device,
        mesh=mesh,
        in_specs=(
            P(("dp", "expert"), None),
            P(("dp", "expert"), None),
            P(("dp", "expert"), None),
            P(("dp", "expert"), None),
            P(("dp", "expert"), None),
            P(("dp", "expert")),
            P("dp", None),
            P("expert", None, None),
            P("expert", None, None),
            P(),
            P(("dp", "expert"), None),
            P(("dp", "expert"), None),
            P("expert", None, None),
            P("expert", None, None),
            P("expert", None, None),
        ),
        out_specs=P(("dp", "expert"), None),
        check_vma=False,
    )
```

time: 170 us -> 145 us (0.85)
  Pallas kernels: 63.7 us -> 41.6 us
  starting transfers between devices: 32.2 us -> 39.9 us
  waiting for transfers between devices: 62 us -> 54.6 us
  other arithmetic: 4.32 us -> 1.45 us
    pallas_call x5 -> x7, Pallas kernels: 50.9 us -> 29.1 us  [the longest x4 22.5 us: run_experts(): call(functools.partial(experts_kernel, groups, spread), 'experts', jax.Sh...]
    ppermute x14, starting transfers between devices: 12.9 us -> 24.4 us  [beside(): return lax.ppermute(a, 'expert', [(e, e ^ 1) for e in range(n_ex)])]
    ppermute x9, waiting for transfers between devices: 56.4 us -> 45 us  [across(): lax.ppermute(a, 'expert', [(e, e ^ (4 if e & 1 else 2)) for e in range(n_...]
    ppermute x3, starting transfers between devices: 9.39 us -> 5 us  [along(): return lax.ppermute(a, ('dp', 'expert'), sent)]
    ppermute x3, waiting for transfers between devices: 0.01 us -> 3.97 us  [along(): return lax.ppermute(a, ('dp', 'expert'), sent)]
    pallas_call x1 -> x2, Pallas kernels: 12.8 us -> 12.4 us  [attend(): pl.pallas_call(attend_kernel, name='attend', grid=(pairs,), out_shape=jax...]
    unnamed x26 -> x30, local copies, waits for them, and re-layouts: 5.52 us -> 5.61 us
  transfers between devices with their start and end apart: 26 -> 26, of which waited for: 8 -> 11; matrix products, arithmetic and copies ran while one was open for 4% -> 0% of each run, Pallas kernels for 38% -> 25%
where the time goes in v2:
time: 145 us; the launch traced here: 143 us
  waiting for transfers between devices  54.6 us (38%)
  Pallas kernels  41.6 us (29%)
  starting transfers between devices  39.9 us (28%)
  local copies, waits for them, and re-layouts  5.61 us (4%)
  other arithmetic  1.45 us (1%)
    ppermute x9, waiting for transfers between devices, across(): lax.ppermute(a, 'expert', [(e, e ^ (4 if e & 1 else 2)) for e in range(n_...  45 us
    ppermute x14, starting transfers between devices, beside(): return lax.ppermute(a, 'expert', [(e, e ^ 1) for e in range(n_ex)])  24.4 us
    pallas_call x4, Pallas kernels, run_experts(): call(functools.partial(experts_kernel, groups, spread), 'experts', jax.Sh...  22.5 us
    pallas_call x2, Pallas kernels, attend(): pl.pallas_call(attend_kernel, name='attend', grid=(pairs,), out_shape=jax...  12.4 us
    ppermute x9, starting transfers between devices, across(): lax.ppermute(a, 'expert', [(e, e ^ (4 if e & 1 else 2)) for e in range(n_...  10.5 us
    ppermute x14, waiting for transfers between devices, beside(): return lax.ppermute(a, 'expert', [(e, e ^ 1) for e in range(n_ex)])  5.64 us
    unnamed x30, local copies, waits for them, and re-layouts  5.61 us
    pallas_call x1, Pallas kernels, project(): call(functools.partial(project_kernel, owners, sources, rank, held), 'pro...  5.14 us
  transfers between devices with their start and end apart: 26, of which 11 were waited for; matrix products, arithmetic and copies ran while one was open for 0% of the time, Pallas kernels for 25%

profile of v2, /device:TPU:0, one launch (start us, length us, event | category | flops | bytes accessed | tf_op | source)
XLA Modules:
  0.0 143.5 jit_solution(12359662808210603525)
XLA Ops:
  0.0 1.1 copy-done.5
  1.1 1.0 copy-done.6
  3.7 3.0 %collective-permute-start.1 = (bf16[256,1664]{1,0:T(8,128)(2,1)S(1)}, bf16[256,1664]{1,0:T(8,128)(2,1)S(1)}, u32[]{:S(2)}, u32[]{:S(2)}) collective-permute-start(bf16[256,1664]{1,0:T(8,128)(2,1)S(1)} %prepare.1.refs_5_.gain_ref), channel_id=1, source_target_pairs={{0,2},{1,5},{2,0},{3,7},{4,6},{5,1},{6,4},{7,3},{8,10},{9,13},{10,... | collective-permute-start | bytes 2555912 | tf_op jit(solution)/shard_map/ppermute | solution.py:399
  6.7 3.5 %collective-permute-start.7 = (bf16[384,1536]{1,0:T(8,128)(2,1)S(1)}, bf16[384,1536]{1,0:T(8,128)(2,1)S(1)}, u32[]{:S(2)}, u32[]{:S(2)}) collective-permute-start(bf16[384,1536]{1,0:T(8,128)(2,1)S(1)} %copy-done.3), channel_id=1, source_target_pairs={{0,8},{8,16},{16,24},{9,1},{17,9},{25,17},{2,10},{10,18},{18,26},{... | collective-permute-start | bytes 3538952 | tf_op jit(solution)/shard_map/ppermute | solution.py:409
  10.4 1.1 copy-done.12
  11.5 0.9 copy-done.14
  12.4 6.2 %attend.2.refs_3_.refs_2_ = bf16[256,768]{1,0:T(8,128)(2,1)S(1)} custom-call(s32[1,4]{1,0:T(1,128)S(1)} %copy-done.11, bf16[256,1536]{1,0:T(8,128)(2,1)S(1)} %copy-done.12, bf16[256,512]{1,0:T(8,128)(2,1)S(1)} %copy-done.13, bf16[256,512]{1,0:T(8,128)(2,1)S(1)} %copy-done.14), custom_call_target="tpu_custom_call" | custom-call | flops 1000000000 | bytes 1048576 | tf_op jit(solution)/shard_map/attend/pallas_call | solution.py:71
  19.9 4.0 %collective-permute-done.7.refs_14_ = bf16[384,1536]{1,0:T(8,128)(2,1)S(1)} collective-permute-done((bf16[384,1536]{1,0:T(8,128)(2,1)S(1)}, bf16[384,1536]{1,0:T(8,128)(2,1)S(1)}, u32[]{:S(2)}, u32[]{:S(2)}) %collective-permute-start.7) | collective-permute-done | bytes 1179680 | tf_op jit(solution)/shard_map/ppermute | solution.py:409
  24.9 1.5 %collective-permute-start.5 = (bf16[256,1664]{1,0:T(8,128)(2,1)S(1)}, bf16[256,1664]{1,0:T(8,128)(2,1)S(1)}, u32[]{:S(2)}, u32[]{:S(2)}) collective-permute-start(bf16[256,1664]{1,0:T(8,128)(2,1)S(1)} %collective-permute-done.3.refs_9_), channel_id=1, source_target_pairs={{0,2},{1,5},{2,0},{3,7},{4,6},{5,1},{6,4},{7,3},{8,10},{9,13},{10,... | collective-permute-start | bytes 2555912 | tf_op jit(solution)/shard_map/ppermute | solution.py:399
  26.4 5.6 %collective-permute-done.2.refs_8_.gain_ref = bf16[256,1664]{1,0:T(8,128)(2,1)S(1)} collective-permute-done((bf16[256,1664]{1,0:T(8,128)(2,1)S(1)}, bf16[256,1664]{1,0:T(8,128)(2,1)S(1)}, u32[]{:S(2)}, u32[]{:S(2)}) %collective-permute-start.2) | collective-permute-done | bytes 852000 | tf_op jit(solution)/shard_map/ppermute | solution.py:399
  32.5 8.3 %collective-permute-start.14 = (bf16[2,1536,512]{2,1,0:T(8,128)(2,1)}, bf16[2,1536,512]{2,1,0:T(8,128)(2,1)S(1)}, u32[]{:S(2)}, u32[]{:S(2)}) collective-permute-start(bf16[2,1536,512]{2,1,0:T(8,128)(2,1)} %refs_1_.9), channel_id=1, source_target_pairs={{0,1},{1,0},{2,3},{3,2},{4,5},{5,4},{6,7},{7,6},{8,9},{9,8},{10,11... | collective-permute-start | bytes 9437192 | tf_op jit(solution)/shard_map/ppermute | solution.py:396
  40.8 6.2 %attend.3.refs_4_.refs_3_ = bf16[256,768]{1,0:T(8,128)(2,1)S(1)} custom-call(s32[1,4]{1,0:T(1,128)S(1)} %copy-done.11, bf16[256,1536]{1,0:T(8,128)(2,1)S(1)} %copy-done.12, bf16[256,512]{1,0:T(8,128)(2,1)S(1)} %copy-done.13, bf16[256,512]{1,0:T(8,128)(2,1)S(1)} %copy-done.14), custom_call_target="tpu_custom_call" | custom-call | flops 1000000000 | bytes 1048576 | tf_op jit(solution)/shard_map/attend/pallas_call | solution.py:71
  47.8 1.1 collective-permute-start.6
  48.9 2.9 %collective-permute-done.6.refs_12_ = bf16[256,1664]{1,0:T(8,128)(2,1)S(1)} collective-permute-done((bf16[256,1664]{1,0:T(8,128)(2,1)S(1)}, bf16[256,1664]{1,0:T(8,128)(2,1)S(1)}, u32[]{:S(2)}, u32[]{:S(2)}) %collective-permute-start.6) | collective-permute-done | bytes 852000 | tf_op jit(solution)/shard_map/ppermute | solution.py:396
  52.1 12.8 %collective-permute-start.12 = (bf16[384,1536]{1,0:T(8,128)(2,1)S(1)}, bf16[384,1536]{1,0:T(8,128)(2,1)S(1)}, u32[]{:S(2)}, u32[]{:S(2)}) collective-permute-start(bf16[384,1536]{1,0:T(8,128)(2,1)S(1)} %collective-permute-done.11.refs_4_), channel_id=1, source_target_pairs={{0,1},{1,0},{2,3},{3,2},{4,5},{5,4},{6,7},{7,6},{8,9},{9,8},{10,11... | collective-permute-start | bytes 3538952 | tf_op jit(solution)/shard_map/ppermute | solution.py:396
  64.9 5.1 %project.1.refs_1_ = f32[256,1536]{1,0:T(8,128)S(1)} custom-call(s32[4]{0:T(128)S(1)} %copy-done.10, s32[1,4]{1,0:T(1,128)S(1)} %copy-done.11, bf16[256,1536]{1,0:T(8,128)(2,1)S(1)} %copy-done.4, bf16[256,768]{1,0:T(8,128)(2,1)S(1)} %attend.2.refs_3_.refs_2_, bf16[256,768]{1,0:T(8,128)(2,1)S(1)} %attend.3.refs_4_.refs_3_, ...), custom_call_target="tpu_custom_call" | custom-call | flops 1000000000 | bytes 1048576 | tf_op jit(solution)/shard_map/project/pallas_call | solution.py:221
  70.1 1.3 normalise.1
  72.7 5.6 %experts.4 = bf16[256,1536]{1,0:T(8,128)(2,1)S(1)} custom-call(bf16[256,1536]{1,0:T(8,128)(2,1)S(1)} %get-tuple-element.20.x_ref, bf16[256,1664]{1,0:T(8,128)(2,1)S(1)} %prepare.1.refs_5_.gain_ref, bf16[2,1536,512]{2,1,0:T(8,128)(2,1)S(1)} %copy-done, bf16[2,1536,512]{2,1,0:T(8,128)(2,1)S(1)} %copy-done.1, bf16[2,512,1536]{2,1,0:T(8,128)(2,1)S(1)} %copy-done.2, ...), custom_call_target="tpu_custom_call" | custom-call | flops 1000000000 | bytes 1048576 | tf_op jit(solution)/shard_map/experts/pallas_call | solution.py:316
  78.3 5.1 %collective-permute-done.16.x_ref = bf16[256,1536]{1,0:T(8,128)(2,1)S(1)} collective-permute-done((bf16[256,1536]{1,0:T(8,128)(2,1)S(1)}, bf16[256,1536]{1,0:T(8,128)(2,1)S(1)}, u32[]{:S(2)}, u32[]{:S(2)}) %collective-permute-start.16) | collective-permute-done | bytes 786464 | tf_op jit(solution)/shard_map/ppermute | solution.py:399
  84.2 1.5 %collective-permute-done.17 = bf16[256,1536]{1,0:T(8,128)(2,1)S(1)} collective-permute-done((bf16[256,1536]{1,0:T(8,128)(2,1)S(1)}, bf16[256,1536]{1,0:T(8,128)(2,1)S(1)}, u32[]{:S(2)}, u32[]{:S(2)}) %collective-permute-start.17) | collective-permute-done | bytes 786464 | tf_op jit(solution)/shard_map/ppermute | solution.py:396
  86.5 5.6 %experts.5 = bf16[256,1536]{1,0:T(8,128)(2,1)S(1)} custom-call(bf16[256,1536]{1,0:T(8,128)(2,1)S(1)} %collective-permute-done.16.x_ref, bf16[256,1664]{1,0:T(8,128)(2,1)S(1)} %collective-permute-done.1.refs_7_.gain_ref, bf16[2,1536,512]{2,1,0:T(8,128)(2,1)S(1)} %copy-done, bf16[2,1536,512]{2,1,0:T(8,128)(2,1)S(1)} %copy-done.1, ...), custom_call_target="tpu_custom_call" | custom-call | flops 1000000000 | bytes 1048576 | tf_op jit(solution)/shard_map/experts/pallas_call | solution.py:316
  92.1 3.4 %collective-permute-done.20.x_ref = bf16[256,1536]{1,0:T(8,128)(2,1)S(1)} collective-permute-done((bf16[256,1536]{1,0:T(8,128)(2,1)S(1)}, bf16[256,1536]{1,0:T(8,128)(2,1)S(1)}, u32[]{:S(2)}, u32[]{:S(2)}) %collective-permute-start.20) | collective-permute-done | bytes 786464 | tf_op jit(solution)/shard_map/ppermute | solution.py:399
  95.4 5.8 %experts.6 = bf16[256,1536]{1,0:T(8,128)(2,1)S(1)} custom-call(bf16[256,1536]{1,0:T(8,128)(2,1)S(1)} %collective-permute-done.20.x_ref, bf16[256,1664]{1,0:T(8,128)(2,1)S(1)} %collective-permute-done.2.refs_8_.gain_ref, bf16[2,1536,512]{2,1,0:T(8,128)(2,1)S(1)} %copy-done, bf16[2,1536,512]{2,1,0:T(8,128)(2,1)S(1)} %copy-done.1, ...), custom_call_target="tpu_custom_call" | custom-call | flops 1000000000 | bytes 1048576 | tf_op jit(solution)/shard_map/experts/pallas_call | solution.py:316
  101.3 2.6 %collective-permute-done.18.x_ref = bf16[256,1536]{1,0:T(8,128)(2,1)S(1)} collective-permute-done((bf16[256,1536]{1,0:T(8,128)(2,1)S(1)}, bf16[256,1536]{1,0:T(8,128)(2,1)S(1)}, u32[]{:S(2)}, u32[]{:S(2)}) %collective-permute-start.18) | collective-permute-done | bytes 786464 | tf_op jit(solution)/shard_map/ppermute | solution.py:399
  103.9 5.6 %experts.7 = bf16[256,1536]{1,0:T(8,128)(2,1)S(1)} custom-call(bf16[256,1536]{1,0:T(8,128)(2,1)S(1)} %collective-permute-done.18.x_ref, bf16[256,1664]{1,0:T(8,128)(2,1)S(1)} %collective-permute-done.5.refs_11_.gain_ref, bf16[2,1536,512]{2,1,0:T(8,128)(2,1)S(1)} %copy-done, bf16[2,1536,512]{2,1,0:T(8,128)(2,1)S(1)} %copy-done.1, ...), custom_call_target="tpu_custom_call" | custom-call | flops 1000000000 | bytes 1048576 | tf_op jit(solution)/shard_map/experts/pallas_call | solution.py:316
  109.5 0.8 collective-permute-start.21
  110.3 1.3 collective-permute-start.24
  111.5 10.0 %collective-permute-done.21 = bf16[256,1536]{1,0:T(8,128)(2,1)S(1)} collective-permute-done((bf16[256,1536]{1,0:T(8,128)(2,1)S(1)}, bf16[256,1536]{1,0:T(8,128)(2,1)S(1)}, u32[]{:S(2)}, u32[]{:S(2)}) %collective-permute-start.21) | collective-permute-done | bytes 786464 | tf_op jit(solution)/shard_map/ppermute | solution.py:399
  121.5 8.4 %collective-permute-done.24 = bf16[256,1536]{1,0:T(8,128)(2,1)S(1)} collective-permute-done((bf16[256,1536]{1,0:T(8,128)(2,1)S(1)}, bf16[256,1536]{1,0:T(8,128)(2,1)S(1)}, u32[]{:S(2)}, u32[]{:S(2)}) %collective-permute-start.24) | collective-permute-done | bytes 786464 | tf_op jit(solution)/shard_map/ppermute | solution.py:399
  131.0 1.2 collective-permute-done.25
  132.2 10.0 %collective-permute-done.23 = bf16[256,1536]{1,0:T(8,128)(2,1)S(1)} collective-permute-done((bf16[256,1536]{1,0:T(8,128)(2,1)S(1)}, bf16[256,1536]{1,0:T(8,128)(2,1)S(1)}, u32[]{:S(2)}, u32[]{:S(2)}) %collective-permute-start.23) | collective-permute-done | bytes 786464 | tf_op jit(solution)/shard_map/ppermute | solution.py:399
  142.2 1.3 add_convert_fusion
  (61 shorter events, 9.5 us)
Async XLA Ops:
  3.5 6.9 %copy-start.13 = (bf16[256,512]{1,0:T(8,128)(2,1)S(1)}, bf16[256,512]{1,0:T(8,128)(2,1)}, u32[]{:S(2)}) copy-start(bf16[256,512]{1,0:T(8,128)(2,1)} %k_ref.3) | copy-start | bytes 786436
  3.7 28.3 %copy-start = (bf16[2,1536,512]{2,1,0:T(8,128)(2,1)S(1)}, bf16[2,1536,512]{2,1,0:T(8,128)(2,1)}, u32[]{:S(2)}) copy-start(bf16[2,1536,512]{2,1,0:T(8,128)(2,1)} %refs_0_.11) | copy-start | bytes 9437188
  3.7 15.0 %collective-permute-start.1 = (bf16[256,1664]{1,0:T(8,128)(2,1)S(1)}, bf16[256,1664]{1,0:T(8,128)(2,1)S(1)}, u32[]{:S(2)}, u32[]{:S(2)}) collective-permute-start(bf16[256,1664]{1,0:T(8,128)(2,1)S(1)} %prepare.1.refs_5_.gain_ref), channel_id=1, source_target_pairs={{0,2},{1,5},{2,0},{3,7},{4,6},{5,1},{6,4},{7,3},{8,10},{9,13},{10,... | collective-permute-start | bytes 2555912 | tf_op jit(solution)/shard_map/ppermute | solution.py:399
  6.7 17.2 %collective-permute-start.7 = (bf16[384,1536]{1,0:T(8,128)(2,1)S(1)}, bf16[384,1536]{1,0:T(8,128)(2,1)S(1)}, u32[]{:S(2)}, u32[]{:S(2)}) collective-permute-start(bf16[384,1536]{1,0:T(8,128)(2,1)S(1)} %copy-done.3), channel_id=1, source_target_pairs={{0,8},{8,16},{16,24},{9,1},{17,9},{25,17},{2,10},{10,18},{18,26},{... | collective-permute-start | bytes 3538952 | tf_op jit(solution)/shard_map/ppermute | solution.py:409
  10.3 9.0 %collective-permute-start = (bf16[256,1664]{1,0:T(8,128)(2,1)S(1)}, bf16[256,1664]{1,0:T(8,128)(2,1)S(1)}, u32[]{:S(2)}, u32[]{:S(2)}) collective-permute-start(bf16[256,1664]{1,0:T(8,128)(2,1)S(1)} %prepare.1.refs_5_.gain_ref), channel_id=1, source_target_pairs={{0,1},{1,0},{2,3},{3,2},{4,5},{5,4},{6,7},{7,6},{8,9},{9,8},{10,11... | collective-permute-start | bytes 2555912 | tf_op jit(solution)/shard_map/ppermute | solution.py:396
  18.7 46.2 %copy-start.4 = (bf16[256,1536]{1,0:T(8,128)(2,1)S(1)}, bf16[256,1536]{1,0:T(8,128)(2,1)}, u32[]{:S(2)}) copy-start(bf16[256,1536]{1,0:T(8,128)(2,1)} %refs_2_.5) | copy-start | bytes 2359300
  18.7 46.2 %copy-start.10 = (s32[4]{0:T(128)S(1)}, s32[4]{0:T(128)}, u32[]{:S(2)}) copy-start(s32[4]{0:T(128)} %refs_0_.6) | copy-start | bytes 52
  18.7 6.2 %collective-permute-start.3 = (bf16[256,1664]{1,0:T(8,128)(2,1)S(1)}, bf16[256,1664]{1,0:T(8,128)(2,1)S(1)}, u32[]{:S(2)}, u32[]{:S(2)}) collective-permute-start(bf16[256,1664]{1,0:T(8,128)(2,1)S(1)} %collective-permute-done.1.refs_7_.gain_ref), channel_id=1, source_target_pairs={{0,1},{1,0},{2,3},{3,2},{4,5},{5,4},{6,7},{7,6},{8,9},{9,8},{10,11... | collective-permute-start | bytes 2555912 | tf_op jit(solution)/shard_map/ppermute | solution.py:396
  19.3 12.7 %collective-permute-start.2 = (bf16[256,1664]{1,0:T(8,128)(2,1)S(1)}, bf16[256,1664]{1,0:T(8,128)(2,1)S(1)}, u32[]{:S(2)}, u32[]{:S(2)}) collective-permute-start(bf16[256,1664]{1,0:T(8,128)(2,1)S(1)} %collective-permute-done.refs_6_), channel_id=1, source_target_pairs={{0,2},{1,5},{2,0},{3,7},{4,6},{5,1},{6,4},{7,3},{8,10},{9,13},{10,... | collective-permute-start | bytes 2555912 | tf_op jit(solution)/shard_map/ppermute | solution.py:399
  23.9 8.6 %collective-permute-start.9 = (bf16[384,1536]{1,0:T(8,128)(2,1)S(1)}, bf16[384,1536]{1,0:T(8,128)(2,1)S(1)}, u32[]{:S(2)}, u32[]{:S(2)}) collective-permute-start(bf16[384,1536]{1,0:T(8,128)(2,1)S(1)} %collective-permute-done.7.refs_14_), channel_id=1, source_target_pairs={{8,16},{16,24},{9,1},{17,9},{10,18},{18,26},{11,3},{19,11},{12,20}... | collective-permute-start | bytes 3538952 | tf_op jit(solution)/shard_map/ppermute | solution.py:409
  24.6 16.1 %collective-permute-start.8 = (bf16[384,1536]{1,0:T(8,128)(2,1)S(1)}, bf16[384,1536]{1,0:T(8,128)(2,1)S(1)}, u32[]{:S(2)}, u32[]{:S(2)}) collective-permute-start(bf16[384,1536]{1,0:T(8,128)(2,1)S(1)} %collective-permute-done.7.refs_14_), channel_id=1, source_target_pairs={{0,1},{1,0},{2,3},{3,2},{4,5},{5,4},{6,7},{7,6},{8,9},{9,8},{10,11... | collective-permute-start | bytes 3538952 | tf_op jit(solution)/shard_map/ppermute | solution.py:396
  24.9 22.1 %collective-permute-start.5 = (bf16[256,1664]{1,0:T(8,128)(2,1)S(1)}, bf16[256,1664]{1,0:T(8,128)(2,1)S(1)}, u32[]{:S(2)}, u32[]{:S(2)}) collective-permute-start(bf16[256,1664]{1,0:T(8,128)(2,1)S(1)} %collective-permute-done.3.refs_9_), channel_id=1, source_target_pairs={{0,2},{1,5},{2,0},{3,7},{4,6},{5,1},{6,4},{7,3},{8,10},{9,13},{10,... | collective-permute-start | bytes 2555912 | tf_op jit(solution)/shard_map/ppermute | solution.py:399
  31.9 15.8 %collective-permute-start.4 = (bf16[256,1664]{1,0:T(8,128)(2,1)S(1)}, bf16[256,1664]{1,0:T(8,128)(2,1)S(1)}, u32[]{:S(2)}, u32[]{:S(2)}) collective-permute-start(bf16[256,1664]{1,0:T(8,128)(2,1)S(1)} %collective-permute-done.2.refs_8_.gain_ref), channel_id=1, source_target_pairs={{0,1},{1,0},{2,3},{3,2},{4,5},{5,4},{6,7},{7,6},{8,9},{9,8},{10,11... | collective-permute-start | bytes 2555912 | tf_op jit(solution)/shard_map/ppermute | solution.py:396
  32.0 40.8 %collective-permute-start.13 = (bf16[2,1536,512]{2,1,0:T(8,128)(2,1)S(1)}, bf16[2,1536,512]{2,1,0:T(8,128)(2,1)S(1)}, u32[]{:S(2)}, u32[]{:S(2)}) collective-permute-start(bf16[2,1536,512]{2,1,0:T(8,128)(2,1)S(1)} %copy-done), channel_id=1, source_target_pairs={{0,1},{1,0},{2,3},{3,2},{4,5},{5,4},{6,7},{7,6},{8,9},{9,8},{10,11... | collective-permute-start | bytes 9437192 | tf_op jit(solution)/shard_map/ppermute | solution.py:396
  32.5 40.3 %collective-permute-start.14 = (bf16[2,1536,512]{2,1,0:T(8,128)(2,1)}, bf16[2,1536,512]{2,1,0:T(8,128)(2,1)S(1)}, u32[]{:S(2)}, u32[]{:S(2)}) collective-permute-start(bf16[2,1536,512]{2,1,0:T(8,128)(2,1)} %refs_1_.9), channel_id=1, source_target_pairs={{0,1},{1,0},{2,3},{3,2},{4,5},{5,4},{6,7},{7,6},{8,9},{9,8},{10,11... | collective-permute-start | bytes 9437192 | tf_op jit(solution)/shard_map/ppermute | solution.py:396
  40.8 32.0 %collective-permute-start.15 = (bf16[2,512,1536]{2,1,0:T(8,128)(2,1)}, bf16[2,512,1536]{2,1,0:T(8,128)(2,1)S(1)}, u32[]{:S(2)}, u32[]{:S(2)}) collective-permute-start(bf16[2,512,1536]{2,1,0:T(8,128)(2,1)} %refs_2_.9), channel_id=1, source_target_pairs={{0,1},{1,0},{2,3},{3,2},{4,5},{5,4},{6,7},{7,6},{8,9},{9,8},{10,11... | collective-permute-start | bytes 9437192 | tf_op jit(solution)/shard_map/ppermute | solution.py:396
  47.0 23.1 %copy-start.9 = (f32[1536]{0:T(1024)S(1)}, f32[1536]{0:T(1024)}, u32[]{:S(2)}) copy-start(f32[1536]{0:T(1024)} %refs_0_.7) | copy-start | bytes 18436
  47.0 5.1 %collective-permute-start.11 = (bf16[384,1536]{1,0:T(8,128)(2,1)S(1)}, bf16[384,1536]{1,0:T(8,128)(2,1)S(1)}, u32[]{:S(2)}, u32[]{:S(2)}) collective-permute-start(bf16[384,1536]{1,0:T(8,128)(2,1)S(1)} %collective-permute-done.9.refs_16_), channel_id=1, source_target_pairs={{16,24},{9,1},{18,26},{11,3},{20,28},{13,5},{22,30},{15,7}} | collective-permute-start | bytes 3538952 | tf_op jit(solution)/shard_map/ppermute | solution.py:409
  47.8 4.0 %collective-permute-start.6 = (bf16[256,1664]{1,0:T(8,128)(2,1)S(1)}, bf16[256,1664]{1,0:T(8,128)(2,1)S(1)}, u32[]{:S(2)}, u32[]{:S(2)}) collective-permute-start(bf16[256,1664]{1,0:T(8,128)(2,1)S(1)} %collective-permute-done.5.refs_11_.gain_ref), channel_id=1, source_target_pairs={{0,1},{1,0},{2,3},{3,2},{4,5},{5,4},{6,7},{7,6},{8,9},{9,8},{10,11... | collective-permute-start | bytes 2555912 | tf_op jit(solution)/shard_map/ppermute | solution.py:396
  51.8 13.2 %collective-permute-start.10 = (bf16[384,1536]{1,0:T(8,128)(2,1)S(1)}, bf16[384,1536]{1,0:T(8,128)(2,1)S(1)}, u32[]{:S(2)}, u32[]{:S(2)}) collective-permute-start(bf16[384,1536]{1,0:T(8,128)(2,1)S(1)} %collective-permute-done.9.refs_16_), channel_id=1, source_target_pairs={{0,1},{1,0},{2,3},{3,2},{4,5},{5,4},{6,7},{7,6},{8,9},{9,8},{10,11... | collective-permute-start | bytes 3538952 | tf_op jit(solution)/shard_map/ppermute | solution.py:396
  52.1 18.0 %collective-permute-start.12 = (bf16[384,1536]{1,0:T(8,128)(2,1)S(1)}, bf16[384,1536]{1,0:T(8,128)(2,1)S(1)}, u32[]{:S(2)}, u32[]{:S(2)}) collective-permute-start(bf16[384,1536]{1,0:T(8,128)(2,1)S(1)} %collective-permute-done.11.refs_4_), channel_id=1, source_target_pairs={{0,1},{1,0},{2,3},{3,2},{4,5},{5,4},{6,7},{7,6},{8,9},{9,8},{10,11... | collective-permute-start | bytes 3538952 | tf_op jit(solution)/shard_map/ppermute | solution.py:396
  64.9 7.8 %copy-start.2 = (bf16[2,512,1536]{2,1,0:T(8,128)(2,1)S(1)}, bf16[2,512,1536]{2,1,0:T(8,128)(2,1)}, u32[]{:S(2)}) copy-start(bf16[2,512,1536]{2,1,0:T(8,128)(2,1)} %refs_2_.9) | copy-start | bytes 9437188
  71.4 12.1 %collective-permute-start.16 = (bf16[256,1536]{1,0:T(8,128)(2,1)S(1)}, bf16[256,1536]{1,0:T(8,128)(2,1)S(1)}, u32[]{:S(2)}, u32[]{:S(2)}) collective-permute-start(bf16[256,1536]{1,0:T(8,128)(2,1)S(1)} %get-tuple-element.20.x_ref), channel_id=1, source_target_pairs={{0,2},{1,5},{2,0},{3,7},{4,6},{5,1},{6,4},{7,3},{8,10},{9,13},{10,... | collective-permute-start | bytes 2359304 | tf_op jit(solution)/shard_map/ppermute | solution.py:399
  72.2 11.2 %collective-permute-start.19 = (bf16[256,1536]{1,0:T(8,128)(2,1)S(1)}, bf16[256,1536]{1,0:T(8,128)(2,1)S(1)}, u32[]{:S(2)}, u32[]{:S(2)}) collective-permute-start(bf16[256,1536]{1,0:T(8,128)(2,1)S(1)} %get-tuple-element.20.x_ref), channel_id=1, source_target_pairs={{0,1},{1,0},{2,3},{3,2},{4,5},{5,4},{6,7},{7,6},{8,9},{9,8},{10,11... | collective-permute-start | bytes 2359304 | tf_op jit(solution)/shard_map/ppermute | solution.py:396
  83.4 2.3 %collective-permute-start.17 = (bf16[256,1536]{1,0:T(8,128)(2,1)S(1)}, bf16[256,1536]{1,0:T(8,128)(2,1)S(1)}, u32[]{:S(2)}, u32[]{:S(2)}) collective-permute-start(bf16[256,1536]{1,0:T(8,128)(2,1)S(1)} %collective-permute-done.16.x_ref), channel_id=1, source_target_pairs={{0,1},{1,0},{2,3},{3,2},{4,5},{5,4},{6,7},{7,6},{8,9},{9,8},{10,11... | collective-permute-start | bytes 2359304 | tf_op jit(solution)/shard_map/ppermute | solution.py:396
  83.5 12.0 %collective-permute-start.20 = (bf16[256,1536]{1,0:T(8,128)(2,1)S(1)}, bf16[256,1536]{1,0:T(8,128)(2,1)S(1)}, u32[]{:S(2)}, u32[]{:S(2)}) collective-permute-start(bf16[256,1536]{1,0:T(8,128)(2,1)S(1)} %collective-permute-done.19), channel_id=1, source_target_pairs={{0,2},{1,5},{2,0},{3,7},{4,6},{5,1},{6,4},{7,3},{8,10},{9,13},{10,... | collective-permute-start | bytes 2359304 | tf_op jit(solution)/shard_map/ppermute | solution.py:399
  85.7 18.1 %collective-permute-start.18 = (bf16[256,1536]{1,0:T(8,128)(2,1)S(1)}, bf16[256,1536]{1,0:T(8,128)(2,1)S(1)}, u32[]{:S(2)}, u32[]{:S(2)}) collective-permute-start(bf16[256,1536]{1,0:T(8,128)(2,1)S(1)} %collective-permute-done.17), channel_id=1, source_target_pairs={{0,2},{1,5},{2,0},{3,7},{4,6},{5,1},{6,4},{7,3},{8,10},{9,13},{10,... | collective-permute-start | bytes 2359304 | tf_op jit(solution)/shard_map/ppermute | solution.py:399
  109.5 12.1 %collective-permute-start.21 = (bf16[256,1536]{1,0:T(8,128)(2,1)S(1)}, bf16[256,1536]{1,0:T(8,128)(2,1)S(1)}, u32[]{:S(2)}, u32[]{:S(2)}) collective-permute-start(bf16[256,1536]{1,0:T(8,128)(2,1)S(1)} %experts.7), channel_id=1, source_target_pairs={{0,2},{1,5},{2,0},{3,7},{4,6},{5,1},{6,4},{7,3},{8,10},{9,13},{10,... | collective-permute-start | bytes 2359304 | tf_op jit(solution)/shard_map/ppermute | solution.py:399
  110.3 19.6 %collective-permute-start.24 = (bf16[256,1536]{1,0:T(8,128)(2,1)S(1)}, bf16[256,1536]{1,0:T(8,128)(2,1)S(1)}, u32[]{:S(2)}, u32[]{:S(2)}) collective-permute-start(bf16[256,1536]{1,0:T(8,128)(2,1)S(1)} %experts.6), channel_id=1, source_target_pairs={{0,2},{1,5},{2,0},{3,7},{4,6},{5,1},{6,4},{7,3},{8,10},{9,13},{10,... | collective-permute-start | bytes 2359304 | tf_op jit(solution)/shard_map/ppermute | solution.py:399
  121.5 8.4 %collective-permute-start.22 = (bf16[256,1536]{1,0:T(8,128)(2,1)S(1)}, bf16[256,1536]{1,0:T(8,128)(2,1)S(1)}, u32[]{:S(2)}, u32[]{:S(2)}) collective-permute-start(bf16[256,1536]{1,0:T(8,128)(2,1)S(1)} %collective-permute-done.21), channel_id=1, source_target_pairs={{0,1},{1,0},{2,3},{3,2},{4,5},{5,4},{6,7},{7,6},{8,9},{9,8},{10,11... | collective-permute-start | bytes 2359304 | tf_op jit(solution)/shard_map/ppermute | solution.py:396
  129.9 2.3 %collective-permute-start.25 = (bf16[256,1536]{1,0:T(8,128)(2,1)S(1)}, bf16[256,1536]{1,0:T(8,128)(2,1)S(1)}, u32[]{:S(2)}, u32[]{:S(2)}) collective-permute-start(bf16[256,1536]{1,0:T(8,128)(2,1)S(1)} %collective-permute-done.24), channel_id=1, source_target_pairs={{0,1},{1,0},{2,3},{3,2},{4,5},{5,4},{6,7},{7,6},{8,9},{9,8},{10,11... | collective-permute-start | bytes 2359304 | tf_op jit(solution)/shard_map/ppermute | solution.py:396
  130.1 12.1 %collective-permute-start.23 = (bf16[256,1536]{1,0:T(8,128)(2,1)S(1)}, bf16[256,1536]{1,0:T(8,128)(2,1)S(1)}, u32[]{:S(2)}, u32[]{:S(2)}) collective-permute-start(bf16[256,1536]{1,0:T(8,128)(2,1)S(1)} %add_convert_fusion.1), channel_id=1, source_target_pairs={{0,2},{1,5},{2,0},{3,7},{4,6},{5,1},{6,4},{7,3},{8,10},{9,13},{10,... | collective-permute-start | bytes 2359304 | tf_op jit(solution)/shard_map/ppermute | solution.py:399
  (9 other events, 21.8 us)

commit v3 on v2

v3 whole, which is shorter than its diff:
```python
import functools

import jax
import jax.numpy as jnp
from jax import lax
from jax.experimental import pallas as pl
from jax.experimental.pallas import tpu as pltpu
from jax.sharding import PartitionSpec as P

HEAD = 64
GROUPS = 3
BF16, F32 = jnp.bfloat16, jnp.float32
VMEM = pl.BlockSpec(memory_space=pltpu.VMEM)
SMEM = pl.BlockSpec(memory_space=pltpu.SMEM)
ANY = pl.BlockSpec(memory_space=pl.ANY)
MIB = 2**20


def call(kernel, name, out_shape, in_specs, out_specs, scratch, room, flops, **more):
    return pl.pallas_call(
        kernel,
        name=name,
        out_shape=out_shape,
        in_specs=in_specs,
        out_specs=out_specs,
        scratch_shapes=scratch,
        compiler_params=pltpu.CompilerParams(vmem_limit_bytes=room * MIB),
        cost_estimate=pl.CostEstimate(flops=flops, bytes_accessed=1024, transcendentals=0),
        **more,
    )


def attend_kernel(lengths_ref, q_ref, k_ref, v_ref, *refs):
    o_ref, bias = refs[-2:]
    tokens = q_ref.shape[0]
    half = tokens // 2

    @pl.when(pl.program_id(0) == 0)
    def _():
        row = lax.broadcasted_iota(jnp.int32, (tokens, tokens), 0)
        col = lax.broadcasted_iota(jnp.int32, (tokens, tokens), 1)
        same = row >= col
        end = 0
        for r in range(lengths_ref.shape[1]):
            end = end + lengths_ref[0, r]
            same = same & ((row < end) | (col >= end))
        bias[...] = jnp.where(same, 0.0, -1e30)

    for j in range(k_ref.shape[1] // HEAD):
        keys = k_ref[:, j * HEAD : (j + 1) * HEAD]
        values = v_ref[:, j * HEAD : (j + 1) * HEAD]
        for g in range(GROUPS):
            at = (j * GROUPS + g) * HEAD
            q = q_ref[:, at : at + HEAD] * jnp.asarray(HEAD**-0.5, BF16)
            for first, seen in ((0, half), (half, tokens)):
                s = lax.dot_general(
                    q[first : first + half],
                    keys[:seen],
                    (((1,), (1,)), ((), ())),
                    preferred_element_type=F32,
                )
                s = s + bias[first : first + half, :seen]
                p = jnp.exp(s - jnp.max(s, axis=-1, keepdims=True))
                w = (p * (1.0 / jnp.sum(p, axis=-1, keepdims=True))).astype(BF16)
                o = jnp.dot(w, values[:seen], preferred_element_type=F32)
                o_ref[first : first + half, at : at + HEAD] = o.astype(BF16)


def attend(lengths, q, k, v, first, pairs, so_far=None):
    tokens = q.shape[0]
    wide = 2 * GROUPS * HEAD
    return pl.pallas_call(
        attend_kernel,
        name="attend",
        grid=(pairs,),
        out_shape=jax.ShapeDtypeStruct(q.shape, BF16),
        in_specs=[
            SMEM,
            pl.BlockSpec((tokens, wide), lambda i: (0, first + i)),
            pl.BlockSpec((tokens, 2 * HEAD), lambda i: (0, first + i)),
            pl.BlockSpec((tokens, 2 * HEAD), lambda i: (0, first + i)),
        ]
        + ([ANY] if so_far is not None else []),
        out_specs=pl.BlockSpec((tokens, wide), lambda i: (0, first + i)),
        scratch_shapes=[pltpu.VMEM((tokens, tokens), F32)],
        compiler_params=pltpu.CompilerParams(vmem_limit_bytes=8 * MIB),
        cost_estimate=pl.CostEstimate(flops=10**9, bytes_accessed=1024, transcendentals=0),
        input_output_aliases={4: 0} if so_far is not None else {},
    )(lengths, q, k, v, *([so_far] if so_far is not None else []))


GATES, SPAN = 32, 128


def prepare_kernel(logits_ref, routes_ref, gain_ref):
    top, tokens = logits_ref.shape
    logits = logits_ref[...]
    raised = jnp.exp(logits - jnp.max(logits, axis=0, keepdims=True))
    gates = raised / jnp.sum(raised, axis=0, keepdims=True)
    expert = lax.broadcasted_iota(jnp.int32, (GATES, tokens), 0)
    gain = jnp.zeros((GATES, tokens), F32)
    for j in range(top):
        gain = gain + jnp.where(expert == routes_ref[j : j + 1], gates[j : j + 1], 0.0)
    high = gain.astype(BF16).astype(F32)
    rest = jnp.zeros((SPAN - 2 * GATES, tokens), F32)
    gain_ref[...] = jnp.concatenate([high, gain - high, rest], axis=0).T.astype(BF16)


def prepare(logits, routes):
    return call(
        prepare_kernel,
        "prepare",
        jax.ShapeDtypeStruct((logits.shape[1], SPAN), BF16),
        [VMEM] * 2,
        VMEM,
        [],
        4,
        10**9,
    )(logits, routes)


def project_kernel(owners, sources, rank, held, *refs):
    pools, shards = len(owners), len(sources)
    ids, lengths, ctx_ref, res_ref = refs[:4]
    pool, shard = refs[4 : 4 + pools], refs[4 + pools : 4 + pools + shards]
    part_ref, low_s, up_s, sem = refs[-4:]
    requests = ids.shape[0]
    z, i = lax.axis_index("dp"), lax.axis_index("expert")

    def copies(r, ref, first):
        return [
            pltpu.make_async_copy(
                ref.at[pl.ds(first + h * rank, rank)], to.at[pl.ds(r * rank, rank)], sem.at[r, h]
            )
            for h, to in ((0, low_s), (1, up_s))
        ]

    for r in range(requests):
        for k in range(pools):
            at = ids[r] - owners[k](i) * held

            @pl.when((at >= 0) & (at < pool[k].shape[0] // (2 * rank)))
            def _():
                for c in copies(r, pool[k], pl.multiple_of(at * (2 * rank), 2 * rank)):
                    c.start()

    part_ref[...] = res_ref[...].astype(F32)
    for source, piece in zip(sources, shard):
        add_shard(source(z, i), ctx_ref, piece, part_ref)
    for r in range(requests):
        for c in copies(r, pool[0], 0):
            c.wait()
    low = lax.dot_general(
        ctx_ref[...], low_s[...], (((1,), (1,)), ((), ())), preferred_element_type=F32
    )
    row = lax.broadcasted_iota(jnp.int32, low.shape, 0)
    lane = lax.broadcasted_iota(jnp.int32, low.shape, 1)
    end = 0
    mine = lane < 0
    for r in range(requests):
        start, end = end, end + lengths[0, r]
        inside = (row >= start) & (row < end)
        mine = mine | (inside & (lane >= r * rank) & (lane < (r + 1) * rank))
    low = jnp.where(mine, low, 0.0).astype(BF16)
    part_ref[...] += jnp.dot(low, up_s[...], preferred_element_type=F32)


def add_shard(at, ctx_ref, piece, total_ref):
    @pl.when(at >= 0)
    def _():
        first = pl.multiple_of(at, 128)
        total_ref[...] += jnp.dot(
            ctx_ref[:, pl.ds(first, piece.shape[0])], piece[...], preferred_element_type=F32
        )


def project(known, ctx, residual, pools, owners, shards, sources, rank, held):
    requests = known[0].shape[0]
    tokens, width = residual.shape
    return call(
        functools.partial(project_kernel, owners, sources, rank, held),
        "project",
        jax.ShapeDtypeStruct((tokens, width), F32),
        [SMEM] * 2 + [VMEM] * 2 + [ANY] * len(pools) + [VMEM] * len(shards),
        VMEM,
        [
            pltpu.VMEM((requests * rank, width), BF16),
            pltpu.VMEM((requests * rank, width), BF16),
            pltpu.SemaphoreType.DMA((requests, 2)),
        ],
        8,
        10**9,
    )(*known, ctx, residual, *pools, *shards)


def first_columns(width):
    return max(128, width // 384 * 128)


def close_kernel(sources, column, second, *refs):
    part_ref, ctx_ref, scale_ref = refs[:3]
    shard = refs[3 : 3 + len(sources)]
    hidden_ref, send_ref = refs[-2:]
    tokens, width = hidden_ref.shape
    z, i = lax.axis_index("dp"), lax.axis_index("expert")
    hidden_ref[...] = part_ref[:, column : column + width]
    beside = 0
    for source, piece in zip(sources, shard):
        wide = piece.shape[1]
        add_shard(source(z, i), ctx_ref, piece, hidden_ref.at[:, beside : beside + wide])
        beside = (beside + wide) % width
    h = hidden_ref[...]
    scale = scale_ref[...].reshape(1, -1)[:, column : column + width]
    send_ref[:, :width] = (h * scale).astype(BF16)
    if second:
        left_ref, gain_ref = refs[3 + len(sources) : -2]
        left = left_ref[...]
        square = jnp.sum(h * h, axis=-1, keepdims=True)
        square = square + jnp.sum(left * left, axis=-1, keepdims=True)
        inv = lax.rsqrt(square * (1.0 / ctx_ref.shape[1]) + 1e-06)
        high = inv.astype(BF16).astype(F32)
        lane = lax.broadcasted_iota(jnp.int32, (tokens, SPAN), 1)
        gain = gain_ref[...].astype(F32)
        gain = jnp.where(lane == 2 * GATES, high, gain)
        gain = jnp.where(lane == 2 * GATES + 1, inv - high, gain)
        send_ref[:, width:] = gain.astype(BF16)


def close(part, ctx, scale, shards, sources, left=()):
    tokens, width = part.shape
    second = len(left) > 0
    cut = first_columns(width)
    mine = width - cut if second else cut
    return call(
        functools.partial(close_kernel, sources, cut if second else 0, second),
        "close",
        (
            jax.ShapeDtypeStruct((tokens, mine), F32),
            jax.ShapeDtypeStruct((tokens, mine + SPAN if second else mine), BF16),
        ),
        [VMEM] * (3 + len(shards) + len(left)),
        (VMEM, VMEM),
        [],
        8,
        10**9,
    )(part, ctx, scale, *shards, *left)


def experts_kernel(groups, spread, a_ref, b_ref, *refs):
    w, out_ref = refs[: 3 * groups], refs[3 * groups]
    total_ref, x_ref = refs[3 * groups + 1 :]
    local = w[0].shape[0]
    cut, wide = a_ref.shape[1], b_ref.shape[1] - SPAN
    i = lax.axis_index("expert")
    x_ref[:, :cut] = a_ref[...]
    x_ref[:, cut:] = b_ref[:, :wide]
    strip = b_ref[:, wide:].astype(F32)
    lane = lax.broadcasted_iota(jnp.int32, strip.shape, 1)
    inv = strip[:, 2 * GATES : 2 * GATES + 1] + strip[:, 2 * GATES + 1 : 2 * GATES + 2]
    for e in range(groups * local):
        g, own = divmod(e, local)
        number = spread(i, g) * local + own
        mine = (lane == number) | (lane == number + GATES)
        coef = jnp.sum(jnp.where(mine, strip, 0.0), axis=-1, keepdims=True)
        gate = jnp.dot(x_ref[...], w[3 * g][own], preferred_element_type=F32) * inv
        up = jnp.dot(x_ref[...], w[3 * g + 1][own], preferred_element_type=F32)
        act = (gate / (1.0 + jnp.exp(-gate)) * (up * (inv * coef))).astype(BF16)
        down = jnp.dot(act, w[3 * g + 2][own], preferred_element_type=F32)
        if e == 0:
            total_ref[...] = down
        elif e < groups * local - 1:
            total_ref[...] += down
        else:
            out_ref[...] = (total_ref[...] + down).astype(BF16)


def run_experts(x, weights, spread):
    a, b = x
    groups = len(weights) // 3
    tokens, width = a.shape[0], weights[0].shape[1]
    return call(
        functools.partial(experts_kernel, groups, spread),
        "experts",
        jax.ShapeDtypeStruct((tokens, width), BF16),
        [VMEM] * (2 + 3 * groups),
        VMEM,
        [pltpu.VMEM((tokens, width), F32), pltpu.VMEM((tokens, width), BF16)],
        12,
        10**9,
    )(a, b, *weights)


def finish_kernel(left_ref, right_ref, *refs):
    parts, out_ref = refs[:-1], refs[-1]
    at = 0
    for hidden in (left_ref, right_ref):
        to = at + hidden.shape[1]
        total = hidden[...]
        for p in parts:
            total = total + p[:, at:to].astype(F32)
        out_ref[:, at:to] = total.astype(BF16)
        at = to


def finish(left, right, parts):
    return call(
        finish_kernel,
        "finish",
        jax.ShapeDtypeStruct(parts[0].shape, BF16),
        [VMEM] * (2 + len(parts)),
        VMEM,
        [],
        8,
        10**9,
    )(left, right, *parts)


def per_device(
    queries,
    rotated_key_heads,
    token_value_heads,
    residual,
    lengths,
    request_adapter_index,
    attention_output_weight,
    adapter_down_factor,
    adapter_up_factor,
    expert_norm_scale,
    router_logit_scores,
    routes,
    expert_gate_weight,
    expert_up_weight,
    expert_down_weight,
):
    tokens = queries.shape[0]
    rank = adapter_up_factor.shape[1]
    held = adapter_up_factor.shape[0]
    n_dp, n_ex = lax.axis_size("dp"), lax.axis_size("expert")
    rows, width = attention_output_weight.shape
    cut = first_columns(width)
    down_t = jnp.swapaxes(adapter_down_factor, 1, 2)
    weights = (expert_gate_weight, expert_up_weight, expert_down_weight)
    pairs = rotated_key_heads.shape[1] // (2 * HEAD)
    known = (request_adapter_index, lengths)
    own = jnp.concatenate([down_t, adapter_up_factor], axis=1).reshape(-1, width)
    gains = prepare(router_logit_scores.T, routes.T)

    if n_ex != 8 or n_dp != 4:
        context = attend(lengths, queries, rotated_key_heads, token_value_heads, 0, pairs)
        shard = lax.all_gather(attention_output_weight, "dp", axis=0, tiled=True)
        pool = lax.all_gather(own, "expert", axis=0, tiled=True)
        part = project(
            known,
            context,
            residual,
            [pool],
            [lambda i: 0],
            [shard],
            [lambda z, i: z * 0],
            rank,
            held,
        )
        hidden0, send0 = close(part, context, expert_norm_scale, [], [])
        hidden1, send1 = close(part, context, expert_norm_scale, [], [], (hidden0, gains))
        every0 = lax.all_gather(send0, "expert", axis=0, tiled=True)
        every1 = lax.all_gather(send1, "expert", axis=0, tiled=True)
        parts = []
        for d in range(n_ex):
            of = slice(d * tokens, (d + 1) * tokens)
            parts.append(run_experts((every0[of], every1[of]), weights, lambda i, g: i))
        mixture = lax.psum_scatter(
            jnp.concatenate(parts, axis=0), "expert", scatter_dimension=0, tiled=True
        )
        return finish(hidden0, hidden1, [mixture])

    def beside(a):
        return lax.ppermute(a, "expert", [(e, e ^ 1) for e in range(n_ex)])

    def across(a):
        return lax.ppermute(a, "expert", [(e, e ^ (4 if e & 1 else 2)) for e in range(n_ex)])

    def along(a, step):
        sent = []
        for e in range(n_ex):
            for d in range(n_dp):
                to = d - 1 if e & 1 else d + 1
                origin = d + step - 1 if e & 1 else d - step + 1
                if 0 <= to < n_dp and 0 <= origin < n_dp:
                    sent.append((d * n_ex + e, to * n_ex + e))
        return lax.ppermute(a, ("dp", "expert"), sent)

    def after(a, *others):
        return lax.optimization_barrier((a, *others))[0]

    def first_row(step, side):
        def at(z, i):
            source = z + side * step * (1 - 2 * (i & 1))
            return jnp.where((source >= 0) & (source < n_dp), source * rows, -1)

        return at

    def attend_next(first, so_far, *others):
        q = after(queries, *others)
        return attend(lengths, q, rotated_key_heads, token_value_heads, first, 1, so_far)

    z1 = along(attention_output_weight, 1)
    pair_weights = [beside(w) for w in weights[:2]]
    p0 = across(own)
    other = beside(own)
    p1 = across(other)
    context = attend_next(0, None, pair_weights[0])
    z2 = along(after(z1, context), 2)
    context = attend_next(1, context, pair_weights[1])
    p0_other = beside(after(p0, context))
    pair_weights.append(beside(weights[2]))
    context = attend_next(2, context)
    context = attend_next(3, context)
    p2 = across(after(p0_other, p1, context))
    p1_other, p2_other = beside(p1), beside(p2)
    z1_other, z2_other = beside(z1), beside(z2)
    z3 = [along(z2[:, :cut], 3), along(z2[:, cut:], 3)]
    owners = [
        lambda i: i,
        lambda i: i ^ 1,
        lambda i: i ^ (2 + 2 * (i & 1)),
        lambda i: i ^ (3 + 2 * (i & 1)),
        lambda i: i ^ (5 - 2 * (i & 1)),
        lambda i: i ^ (4 - 2 * (i & 1)),
        lambda i: i ^ 7,
        lambda i: i ^ 6,
    ]
    part = project(
        known,
        context,
        after(residual, pair_weights[2]),
        [own, other, p0, p1, p0_other, p1_other, p2, p2_other],
        owners,
        [attention_output_weight, z1, z1_other, z2, z2_other],
        [lambda z, i: z * rows] + [first_row(s, side) for s in (1, 2) for side in (-1, 1)],
        rank,
        held,
    )
    ends = [first_row(3, -1), first_row(3, 1)]
    task = functools.partial(close, part, context, expert_norm_scale)
    hidden0, send0 = task([z3[0], beside(after(z3[0], part))], ends)
    other0 = beside(send0)
    near0, next0 = across(send0), across(other0)
    late = after(z3[1], send0)
    parts = [z3[1], beside(late[:, :cut]), beside(late[:, cut:])]
    hidden1, send1 = task(parts, [ends[0], ends[1], ends[1]], (hidden0, gains))
    near0_other = beside(near0)
    far0 = across(near0_other)
    other1 = beside(send1)
    near1, next1 = across(after(send1, near0_other)), across(other1)
    run = functools.partial(
        run_experts, weights=weights + tuple(pair_weights), spread=lambda i, g: i ^ g
    )
    home = run((send0, send1))
    far1 = across(beside(after(near1, next0, home)))
    r_near = run((near0, after(near1, home)))
    r_next = run((next0, after(next1, r_near)))
    back = across(r_next)
    r_far = run((far0, after(far1, r_next)))
    via = beside(after(across(r_far), back))
    back1 = beside(back)
    back0 = across((r_near.astype(F32) + via.astype(F32)).astype(BF16))
    return finish(hidden0, hidden1, [home, back1, back0])


def solution(mesh):
    return jax.shard_map(
        per_device,
        mesh=mesh,
        in_specs=(
            P(("dp", "expert"), None),
            P(("dp", "expert"), None),
            P(("dp", "expert"), None),
            P(("dp", "expert"), None),
            P(("dp", "expert"), None),
            P(("dp", "expert")),
            P("dp", None),
            P("expert", None, None),
            P("expert", None, None),
            P(),
            P(("dp", "expert"), None),
            P(("dp", "expert"), None),
            P("expert", None, None),
            P("expert", None, None),
            P("expert", None, None),
        ),
        out_specs=P(("dp", "expert"), None),
        check_vma=False,
    )
```

time: 145 us -> 132 us (0.910); the launches traced: 143 us -> 132 us
  waiting for transfers between devices: 54.6 us -> 41.3 us
  starting transfers between devices: 39.9 us -> 44.4 us
  local copies, waits for them, and re-layouts: 5.61 us -> 2.31 us
    ppermute x9 -> x12, waiting for transfers between devices: 45 us -> 27.6 us  [across(): lax.ppermute(a, 'expert', [(e, e ^ (4 if e & 1 else 2)) for e in range(n_...]
    ppermute x9 -> x12, starting transfers between devices: 10.5 us -> 17.2 us  [across(): lax.ppermute(a, 'expert', [(e, e ^ (4 if e & 1 else 2)) for e in range(n_...]
    ppermute x14 -> x18, starting transfers between devices: 24.4 us -> 20.5 us  [beside(): return lax.ppermute(a, 'expert', [(e, e ^ 1) for e in range(n_ex)])]
    ppermute x14 -> x18, waiting for transfers between devices: 5.64 us -> 9.55 us  [beside(): return lax.ppermute(a, 'expert', [(e, e ^ 1) for e in range(n_ex)])]
    unnamed x30 -> x28, local copies, waits for them, and re-layouts: 5.61 us -> 2.14 us
    ppermute x3 -> x4, starting transfers between devices: 5 us -> 6.73 us  [along(): return lax.ppermute(a, ('dp', 'expert'), sent)]
    pallas_call x2 -> x4, Pallas kernels: 12.4 us -> 13.3 us  [attend(): pl.pallas_call(attend_kernel, name='attend', grid=(pairs,), out_shape=jax...]
    ppermute x3 -> x4, waiting for transfers between devices: 3.97 us -> 4.19 us  [along(): return lax.ppermute(a, ('dp', 'expert'), sent)]
  transfers between devices with their start and end apart: 26 -> 34, of which waited for: 11 -> 16; matrix products, arithmetic and copies ran while one was open for 0% -> 1% of each run, Pallas kernels for 25% -> 31%
where the time goes in v3:
time: 132 us
  starting transfers between devices  44.4 us (34%)
  Pallas kernels  42.3 us (32%)
  waiting for transfers between devices  41.3 us (31%)
  local copies, waits for them, and re-layouts  2.31 us (2%)
  other arithmetic  1.4 us (1%)
    ppermute x12, waiting for transfers between devices, across(): lax.ppermute(a, 'expert', [(e, e ^ (4 if e & 1 else 2)) for e in range(n_...  27.6 us
    pallas_call x4, Pallas kernels, run_experts(): call(functools.partial(experts_kernel, groups, spread), 'experts', jax.Sh...  21.9 us
    ppermute x18, starting transfers between devices, beside(): return lax.ppermute(a, 'expert', [(e, e ^ 1) for e in range(n_ex)])  20.5 us
    ppermute x12, starting transfers between devices, across(): lax.ppermute(a, 'expert', [(e, e ^ (4 if e & 1 else 2)) for e in range(n_...  17.2 us
    pallas_call x4, Pallas kernels, attend(): pl.pallas_call(attend_kernel, name='attend', grid=(pairs,), out_shape=jax...  13.3 us
    ppermute x18, waiting for transfers between devices, beside(): return lax.ppermute(a, 'expert', [(e, e ^ 1) for e in range(n_ex)])  9.55 us
    ppermute x4, starting transfers between devices, along(): return lax.ppermute(a, ('dp', 'expert'), sent)  6.73 us
    pallas_call x1, Pallas kernels, project(): call(functools.partial(project_kernel, owners, sources, rank, held), 'pro...  4.41 us
  transfers between devices with their start and end apart: 34, of which 16 were waited for; matrix products, arithmetic and copies ran while one was open for 1% of the time, Pallas kernels for 31%

profile of v3, /device:TPU:0, one launch (start us, length us, event | category | flops | bytes accessed | tf_op | source)
XLA Modules:
  0.0 132.0 jit_solution(8079657264517996534)
XLA Ops:
  2.3 4.6 %collective-permute-start.10 = (bf16[384,1536]{1,0:T(8,128)(2,1)S(1)}, bf16[384,1536]{1,0:T(8,128)(2,1)S(1)}, u32[]{:S(2)}, u32[]{:S(2)}) collective-permute-start(bf16[384,1536]{1,0:T(8,128)(2,1)S(1)} %copy-done.3), channel_id=1, source_target_pairs={{0,8},{8,16},{16,24},{9,1},{17,9},{25,17},{2,10},{10,18},{18,26},{... | collective-permute-start | bytes 3538952 | tf_op jit(solution)/shard_map/ppermute | solution.py:390
  8.1 2.9 %collective-permute-start.4 = (bf16[256,1536]{1,0:T(8,128)(2,1)S(1)}, bf16[256,1536]{1,0:T(8,128)(2,1)S(1)}, u32[]{:S(2)}, u32[]{:S(2)}) collective-permute-start(bf16[256,1536]{1,0:T(8,128)(2,1)S(1)} %bitcast.5), channel_id=1, source_target_pairs={{0,2},{1,5},{2,0},{3,7},{4,6},{5,1},{6,4},{7,3},{8,10},{9,13},{10,... | collective-permute-start | bytes 2359304 | tf_op jit(solution)/shard_map/ppermute | solution.py:380
  13.0 3.3 %attend.4.refs_0_ = bf16[256,1536]{1,0:T(8,128)(2,1)S(1)} custom-call(s32[1,4]{1,0:T(1,128)S(1)} %copy-done.7, bf16[256,1536]{1,0:T(8,128)(2,1)S(1)} %copy-done.8, bf16[256,512]{1,0:T(8,128)(2,1)S(1)} %copy-done.9, bf16[256,512]{1,0:T(8,128)(2,1)S(1)} %copy-done.10), custom_call_target="tpu_custom_call" | custom-call | flops 1000000000 | bytes 1024 | tf_op jit(solution)/shard_map/attend/pallas_call | solution.py:72
  16.4 4.2 %collective-permute-done.10.refs_13_ = bf16[384,1536]{1,0:T(8,128)(2,1)S(1)} collective-permute-done((bf16[384,1536]{1,0:T(8,128)(2,1)S(1)}, bf16[384,1536]{1,0:T(8,128)(2,1)S(1)}, u32[]{:S(2)}, u32[]{:S(2)}) %collective-permute-start.10) | collective-permute-done | bytes 1179680 | tf_op jit(solution)/shard_map/ppermute | solution.py:390
  20.6 3.3 %attend.5.refs_0_ = bf16[256,1536]{1,0:T(8,128)(2,1)S(1)} custom-call(s32[1,4]{1,0:T(1,128)S(1)} %copy-done.7, bf16[256,1536]{1,0:T(8,128)(2,1)S(1)} %copy-done.8, bf16[256,512]{1,0:T(8,128)(2,1)S(1)} %copy-done.9, bf16[256,512]{1,0:T(8,128)(2,1)S(1)} %copy-done.10, bf16[256,1536]{1,0:T(8,128)(2,1)S(1)} %attend.4.refs_0_), custom_call_target="tpu_custom_call", output_to_operand_aliasing={{}: (4, {})} | custom-call | flops 1000000000 | bytes 1024 | tf_op jit(solution)/shard_map/attend/pallas_call | solution.py:72
  25.0 3.3 %attend.6.refs_0_ = bf16[256,1536]{1,0:T(8,128)(2,1)S(1)} custom-call(s32[1,4]{1,0:T(1,128)S(1)} %copy-done.7, bf16[256,1536]{1,0:T(8,128)(2,1)S(1)} %copy-done.8, bf16[256,512]{1,0:T(8,128)(2,1)S(1)} %copy-done.9, bf16[256,512]{1,0:T(8,128)(2,1)S(1)} %copy-done.11, bf16[256,1536]{1,0:T(8,128)(2,1)S(1)} %attend.5.refs_0_), custom_call_target="tpu_custom_call", output_to_operand_aliasing={{}: (4, {})} | custom-call | flops 1000000000 | bytes 1024 | tf_op jit(solution)/shard_map/attend/pallas_call | solution.py:72
  28.3 3.3 %attend.7.refs_2_.refs_1_ = bf16[256,1536]{1,0:T(8,128)(2,1)S(1)} custom-call(s32[1,4]{1,0:T(1,128)S(1)} %copy-done.7, bf16[256,1536]{1,0:T(8,128)(2,1)S(1)} %copy-done.8, bf16[256,512]{1,0:T(8,128)(2,1)S(1)} %copy-done.9, bf16[256,512]{1,0:T(8,128)(2,1)S(1)} %copy-done.11, bf16[256,1536]{1,0:T(8,128)(2,1)S(1)} %attend.6.refs_0_), custom_call_target="tpu_custom_call", output_to_operand_aliasing={{}: (4, {})} | custom-call | flops 1000000000 | bytes 1024 | tf_op jit(solution)/shard_map/attend/pallas_call | solution.py:72
  31.7 1.7 %collective-permute-start.8 = (bf16[256,1536]{1,0:T(8,128)(2,1)S(1)}, bf16[256,1536]{1,0:T(8,128)(2,1)S(1)}, u32[]{:S(2)}, u32[]{:S(2)}) collective-permute-start(bf16[256,1536]{1,0:T(8,128)(2,1)S(1)} %collective-permute-done.6.refs_8_), channel_id=1, source_target_pairs={{0,2},{1,5},{2,0},{3,7},{4,6},{5,1},{6,4},{7,3},{8,10},{9,13},{10,... | collective-permute-start | bytes 2359304 | tf_op jit(solution)/shard_map/ppermute | solution.py:380
  33.7 8.7 %collective-permute-start.13 = (bf16[384,1536]{1,0:T(8,128)(2,1)S(1)}, bf16[384,1536]{1,0:T(8,128)(2,1)S(1)}, u32[]{:S(2)}, u32[]{:S(2)}) collective-permute-start(bf16[384,1536]{1,0:T(8,128)(2,1)S(1)} %collective-permute-done.12.refs_15_), channel_id=1, source_target_pairs={{0,1},{1,0},{2,3},{3,2},{4,5},{5,4},{6,7},{7,6},{8,9},{9,8},{10,11... | collective-permute-start | bytes 3538952 | tf_op jit(solution)/shard_map/ppermute | solution.py:377
  43.8 2.3 %collective-permute-done.7.refs_9_ = bf16[256,1536]{1,0:T(8,128)(2,1)S(1)} collective-permute-done((bf16[256,1536]{1,0:T(8,128)(2,1)S(1)}, bf16[256,1536]{1,0:T(8,128)(2,1)S(1)}, u32[]{:S(2)}, u32[]{:S(2)}) %collective-permute-start.7) | collective-permute-done | bytes 786464 | tf_op jit(solution)/shard_map/ppermute | solution.py:377
  47.6 4.4 %project.1.refs_0_ = f32[256,1536]{1,0:T(8,128)S(1)} custom-call(s32[4]{0:T(128)S(1)} %copy-done.6, s32[1,4]{1,0:T(1,128)S(1)} %copy-done.7, bf16[256,1536]{1,0:T(8,128)(2,1)S(1)} %attend.7.refs_2_.refs_1_, bf16[256,1536]{1,0:T(8,128)(2,1)S(1)} %copy-done.4, bf16[256,1536]{1,0:T(8,128)(2,1)S(1)} %bitcast.6, ...), custom_call_target="tpu_custom_call" | custom-call | flops 1000000000 | bytes 1024 | tf_op jit(solution)/shard_map/project/pallas_call | solution.py:180
  52.0 3.4 %collective-permute-start.15 = (bf16[384,512]{1,0:T(8,128)(2,1)S(1)}, bf16[384,512]{1,0:T(8,128)(2,1)S(1)}, u32[]{:S(2)}, u32[]{:S(2)}) collective-permute-start(bf16[384,512]{1,0:T(8,128)(2,1)S(1)} %collective-permute-done.14.refs_3_), channel_id=1, source_target_pairs={{0,1},{1,0},{2,3},{3,2},{4,5},{5,4},{6,7},{7,6},{8,9},{9,8},{10,11... | collective-permute-start | bytes 1179656 | tf_op jit(solution)/shard_map/ppermute | solution.py:377
  55.4 1.3 %collective-permute-done.15.refs_4_ = bf16[384,512]{1,0:T(8,128)(2,1)S(1)} collective-permute-done((bf16[384,512]{1,0:T(8,128)(2,1)S(1)}, bf16[384,512]{1,0:T(8,128)(2,1)S(1)}, u32[]{:S(2)}, u32[]{:S(2)}) %collective-permute-start.15) | collective-permute-done | bytes 393248 | tf_op jit(solution)/shard_map/ppermute | solution.py:377
  57.2 1.6 %collective-permute-start.23 = (bf16[256,512]{1,0:T(8,128)(2,1)S(1)}, bf16[256,512]{1,0:T(8,128)(2,1)S(1)}, u32[]{:S(2)}, u32[]{:S(2)}) collective-permute-start(bf16[256,512]{1,0:T(8,128)(2,1)S(1)} %get-tuple-element.31.a_ref), channel_id=1, source_target_pairs={{0,2},{1,5},{2,0},{3,7},{4,6},{5,1},{6,4},{7,3},{8,10},{9,13},{10,... | collective-permute-start | bytes 786440 | tf_op jit(solution)/shard_map/ppermute | solution.py:380
  58.8 5.2 %collective-permute-start.17 = (bf16[384,512]{1,0:T(8,128)(2,1)S(1)}, bf16[384,512]{1,0:T(8,128)(2,1)S(1)}, u32[]{:S(2)}, u32[]{:S(2)}) collective-permute-start(bf16[384,512]{1,0:T(8,128)(2,1)S(1)} %get-tuple-element.42), channel_id=1, source_target_pairs={{0,1},{1,0},{2,3},{3,2},{4,5},{5,4},{6,7},{7,6},{8,9},{9,8},{10,11... | collective-permute-start | bytes 1179656 | tf_op jit(solution)/shard_map/ppermute | solution.py:377
  66.9 1.6 %collective-permute-start.25 = (bf16[256,1152]{1,0:T(8,128)(2,1)S(1)}, bf16[256,1152]{1,0:T(8,128)(2,1)S(1)}, u32[]{:S(2)}, u32[]{:S(2)}) collective-permute-start(bf16[256,1152]{1,0:T(8,128)(2,1)S(1)} %get-tuple-element.35.b_ref), channel_id=1, source_target_pairs={{0,2},{1,5},{2,0},{3,7},{4,6},{5,1},{6,4},{7,3},{8,10},{9,13},{10,... | collective-permute-start | bytes 1769480 | tf_op jit(solution)/shard_map/ppermute | solution.py:380
  68.6 1.4 %collective-permute-done.19 = bf16[256,512]{1,0:T(8,128)(2,1)S(1)} collective-permute-done((bf16[256,512]{1,0:T(8,128)(2,1)S(1)}, bf16[256,512]{1,0:T(8,128)(2,1)S(1)}, u32[]{:S(2)}, u32[]{:S(2)}) %collective-permute-start.19) | collective-permute-done | bytes 262176 | tf_op jit(solution)/shard_map/ppermute | solution.py:377
  71.3 5.4 %experts.4.refs_0_ = bf16[256,1536]{1,0:T(8,128)(2,1)S(1)} custom-call(bf16[256,512]{1,0:T(8,128)(2,1)S(1)} %get-tuple-element.31.a_ref, bf16[256,1152]{1,0:T(8,128)(2,1)S(1)} %get-tuple-element.35.b_ref, bf16[2,1536,512]{2,1,0:T(8,128)(2,1)S(1)} %copy-done, bf16[2,1536,512]{2,1,0:T(8,128)(2,1)S(1)} %copy-done.1, bf16[2,512,1536]{2,1,0:T(8,128)(2,1)S(1)} %copy-done.2, ...), custom_call_target="tpu_custom_call" | custom-call | flops 1000000000 | bytes 1024 | tf_op jit(solution)/shard_map/experts/pallas_call | solution.py:281
  76.8 2.9 %collective-permute-done.20.a_ref = bf16[256,512]{1,0:T(8,128)(2,1)S(1)} collective-permute-done((bf16[256,512]{1,0:T(8,128)(2,1)S(1)}, bf16[256,512]{1,0:T(8,128)(2,1)S(1)}, u32[]{:S(2)}, u32[]{:S(2)}) %collective-permute-start.20) | collective-permute-done | bytes 262176 | tf_op jit(solution)/shard_map/ppermute | solution.py:380
  79.6 1.6 %collective-permute-start.22 = (bf16[256,1152]{1,0:T(8,128)(2,1)S(1)}, bf16[256,1152]{1,0:T(8,128)(2,1)S(1)}, u32[]{:S(2)}, u32[]{:S(2)}) collective-permute-start(bf16[256,1152]{1,0:T(8,128)(2,1)S(1)} %collective-permute-done.21), channel_id=1, source_target_pairs={{0,2},{1,5},{2,0},{3,7},{4,6},{5,1},{6,4},{7,3},{8,10},{9,13},{10,... | collective-permute-start | bytes 1769480 | tf_op jit(solution)/shard_map/ppermute | solution.py:380
  81.6 1.5 %collective-permute-start.30 = (bf16[256,1152]{1,0:T(8,128)(2,1)S(1)}, bf16[256,1152]{1,0:T(8,128)(2,1)S(1)}, u32[]{:S(2)}, u32[]{:S(2)}) collective-permute-start(bf16[256,1152]{1,0:T(8,128)(2,1)S(1)} %collective-permute-done.29), channel_id=1, source_target_pairs={{0,2},{1,5},{2,0},{3,7},{4,6},{5,1},{6,4},{7,3},{8,10},{9,13},{10,... | collective-permute-start | bytes 1769480 | tf_op jit(solution)/shard_map/ppermute | solution.py:380
  83.7 5.4 %experts.5 = bf16[256,1536]{1,0:T(8,128)(2,1)S(1)} custom-call(bf16[256,512]{1,0:T(8,128)(2,1)S(1)} %collective-permute-done.23.a_ref, bf16[256,1152]{1,0:T(8,128)(2,1)S(1)} %collective-permute-done.25.b_ref, bf16[2,1536,512]{2,1,0:T(8,128)(2,1)S(1)} %copy-done, bf16[2,1536,512]{2,1,0:T(8,128)(2,1)S(1)} %copy-done.1, bf16[2,512,1536]{2,1,0:T(8,128)(2,1)S(1)} %copy-done.2, ...), custom_call_target="tpu_custom_call" | custom-call | flops 1000000000 | bytes 1024 | tf_op jit(solution)/shard_map/experts/pallas_call | solution.py:281
  89.6 5.7 %experts.6 = bf16[256,1536]{1,0:T(8,128)(2,1)S(1)} custom-call(bf16[256,512]{1,0:T(8,128)(2,1)S(1)} %collective-permute-done.20.a_ref, bf16[256,1152]{1,0:T(8,128)(2,1)S(1)} %collective-permute-done.22.b_ref, bf16[2,1536,512]{2,1,0:T(8,128)(2,1)S(1)} %copy-done, bf16[2,1536,512]{2,1,0:T(8,128)(2,1)S(1)} %copy-done.1, bf16[2,512,1536]{2,1,0:T(8,128)(2,1)S(1)} %copy-done.2, ...), custom_call_target="tpu_custom_call" | custom-call | flops 1000000000 | bytes 1024 | tf_op jit(solution)/shard_map/experts/pallas_call | solution.py:281
  95.3 1.5 %collective-permute-start.26 = (bf16[256,1536]{1,0:T(8,128)(2,1)S(1)}, bf16[256,1536]{1,0:T(8,128)(2,1)S(1)}, u32[]{:S(2)}, u32[]{:S(2)}) collective-permute-start(bf16[256,1536]{1,0:T(8,128)(2,1)S(1)} %experts.6), channel_id=1, source_target_pairs={{0,2},{1,5},{2,0},{3,7},{4,6},{5,1},{6,4},{7,3},{8,10},{9,13},{10,... | collective-permute-start | bytes 2359304 | tf_op jit(solution)/shard_map/ppermute | solution.py:380
  96.8 1.9 %collective-permute-done.28.a_ref = bf16[256,512]{1,0:T(8,128)(2,1)S(1)} collective-permute-done((bf16[256,512]{1,0:T(8,128)(2,1)S(1)}, bf16[256,512]{1,0:T(8,128)(2,1)S(1)}, u32[]{:S(2)}, u32[]{:S(2)}) %collective-permute-start.28) | collective-permute-done | bytes 262176 | tf_op jit(solution)/shard_map/ppermute | solution.py:380
  98.7 5.4 %experts.7 = bf16[256,1536]{1,0:T(8,128)(2,1)S(1)} custom-call(bf16[256,512]{1,0:T(8,128)(2,1)S(1)} %collective-permute-done.28.a_ref, bf16[256,1152]{1,0:T(8,128)(2,1)S(1)} %collective-permute-done.30.b_ref, bf16[2,1536,512]{2,1,0:T(8,128)(2,1)S(1)} %copy-done, bf16[2,1536,512]{2,1,0:T(8,128)(2,1)S(1)} %copy-done.1, bf16[2,512,1536]{2,1,0:T(8,128)(2,1)S(1)} %copy-done.2, ...), custom_call_target="tpu_custom_call" | custom-call | flops 1000000000 | bytes 1024 | tf_op jit(solution)/shard_map/experts/pallas_call | solution.py:281
  104.1 1.6 %collective-permute-start.31 = (bf16[256,1536]{1,0:T(8,128)(2,1)S(1)}, bf16[256,1536]{1,0:T(8,128)(2,1)S(1)}, u32[]{:S(2)}, u32[]{:S(2)}) collective-permute-start(bf16[256,1536]{1,0:T(8,128)(2,1)S(1)} %experts.7), channel_id=1, source_target_pairs={{0,2},{1,5},{2,0},{3,7},{4,6},{5,1},{6,4},{7,3},{8,10},{9,13},{10,... | collective-permute-start | bytes 2359304 | tf_op jit(solution)/shard_map/ppermute | solution.py:380
  105.7 1.6 %collective-permute-done.26 = bf16[256,1536]{1,0:T(8,128)(2,1)S(1)} collective-permute-done((bf16[256,1536]{1,0:T(8,128)(2,1)S(1)}, bf16[256,1536]{1,0:T(8,128)(2,1)S(1)}, u32[]{:S(2)}, u32[]{:S(2)}) %collective-permute-start.26) | collective-permute-done | bytes 786464 | tf_op jit(solution)/shard_map/ppermute | solution.py:380
  107.3 8.9 %collective-permute-done.31 = bf16[256,1536]{1,0:T(8,128)(2,1)S(1)} collective-permute-done((bf16[256,1536]{1,0:T(8,128)(2,1)S(1)}, bf16[256,1536]{1,0:T(8,128)(2,1)S(1)}, u32[]{:S(2)}, u32[]{:S(2)}) %collective-permute-start.31) | collective-permute-done | bytes 786464 | tf_op jit(solution)/shard_map/ppermute | solution.py:380
  116.7 1.8 %collective-permute-done.32 = bf16[256,1536]{1,0:T(8,128)(2,1)S(1)} collective-permute-done((bf16[256,1536]{1,0:T(8,128)(2,1)S(1)}, bf16[256,1536]{1,0:T(8,128)(2,1)S(1)}, u32[]{:S(2)}, u32[]{:S(2)}) %collective-permute-start.32) | collective-permute-done | bytes 786464 | tf_op jit(solution)/shard_map/ppermute | solution.py:377
  118.7 1.6 %collective-permute-start.33 = (bf16[256,1536]{1,0:T(8,128)(2,1)S(1)}, bf16[256,1536]{1,0:T(8,128)(2,1)S(1)}, u32[]{:S(2)}, u32[]{:S(2)}) collective-permute-start(bf16[256,1536]{1,0:T(8,128)(2,1)S(1)} %add_convert_fusion), channel_id=1, source_target_pairs={{0,2},{1,5},{2,0},{3,7},{4,6},{5,1},{6,4},{7,3},{8,10},{9,13},{10,... | collective-permute-start | bytes 2359304 | tf_op jit(solution)/shard_map/ppermute | solution.py:380
  120.3 10.5 %collective-permute-done.33.refs_2_ = bf16[256,1536]{1,0:T(8,128)(2,1)S(1)} collective-permute-done((bf16[256,1536]{1,0:T(8,128)(2,1)S(1)}, bf16[256,1536]{1,0:T(8,128)(2,1)S(1)}, u32[]{:S(2)}, u32[]{:S(2)}) %collective-permute-start.33) | collective-permute-done | bytes 786464 | tf_op jit(solution)/shard_map/ppermute | solution.py:380
  (82 shorter events, 18.1 us)
Async XLA Ops:
  0.0 10.9 %collective-permute-start.1 = (bf16[2,1536,512]{2,1,0:T(8,128)(2,1)}, bf16[2,1536,512]{2,1,0:T(8,128)(2,1)S(1)}, u32[]{:S(2)}, u32[]{:S(2)}) collective-permute-start(bf16[2,1536,512]{2,1,0:T(8,128)(2,1)} %refs_0_.9), channel_id=1, source_target_pairs={{0,1},{1,0},{2,3},{3,2},{4,5},{5,4},{6,7},{7,6},{8,9},{9,8},{10,11... | collective-permute-start | bytes 9437192 | tf_op jit(solution)/shard_map/ppermute | solution.py:377
  0.5 20.0 %collective-permute-start = (bf16[2,1536,512]{2,1,0:T(8,128)(2,1)}, bf16[2,1536,512]{2,1,0:T(8,128)(2,1)S(1)}, u32[]{:S(2)}, u32[]{:S(2)}) collective-permute-start(bf16[2,1536,512]{2,1,0:T(8,128)(2,1)} %refs_1_.9), channel_id=1, source_target_pairs={{0,1},{1,0},{2,3},{3,2},{4,5},{5,4},{6,7},{7,6},{8,9},{9,8},{10,11... | collective-permute-start | bytes 9437192 | tf_op jit(solution)/shard_map/ppermute | solution.py:377
  1.8 6.3 %collective-permute-start.3 = (bf16[256,1536]{1,0:T(8,128)(2,1)S(1)}, bf16[256,1536]{1,0:T(8,128)(2,1)S(1)}, u32[]{:S(2)}, u32[]{:S(2)}) collective-permute-start(bf16[256,1536]{1,0:T(8,128)(2,1)S(1)} %bitcast.4), channel_id=1, source_target_pairs={{0,1},{1,0},{2,3},{3,2},{4,5},{5,4},{6,7},{7,6},{8,9},{9,8},{10,11... | collective-permute-start | bytes 2359304 | tf_op jit(solution)/shard_map/ppermute | solution.py:377
  2.3 18.3 %collective-permute-start.10 = (bf16[384,1536]{1,0:T(8,128)(2,1)S(1)}, bf16[384,1536]{1,0:T(8,128)(2,1)S(1)}, u32[]{:S(2)}, u32[]{:S(2)}) collective-permute-start(bf16[384,1536]{1,0:T(8,128)(2,1)S(1)} %copy-done.3), channel_id=1, source_target_pairs={{0,8},{8,16},{16,24},{9,1},{17,9},{25,17},{2,10},{10,18},{18,26},{... | collective-permute-start | bytes 3538952 | tf_op jit(solution)/shard_map/ppermute | solution.py:390
  6.9 39.9 %collective-permute-start.2 = (bf16[2,512,1536]{2,1,0:T(8,128)(2,1)}, bf16[2,512,1536]{2,1,0:T(8,128)(2,1)S(1)}, u32[]{:S(2)}, u32[]{:S(2)}) collective-permute-start(bf16[2,512,1536]{2,1,0:T(8,128)(2,1)} %refs_2_.11), channel_id=1, source_target_pairs={{0,1},{1,0},{2,3},{3,2},{4,5},{5,4},{6,7},{7,6},{8,9},{9,8},{10,11... | collective-permute-start | bytes 9437192 | tf_op jit(solution)/shard_map/ppermute | solution.py:377
  8.1 15.8 %collective-permute-start.4 = (bf16[256,1536]{1,0:T(8,128)(2,1)S(1)}, bf16[256,1536]{1,0:T(8,128)(2,1)S(1)}, u32[]{:S(2)}, u32[]{:S(2)}) collective-permute-start(bf16[256,1536]{1,0:T(8,128)(2,1)S(1)} %bitcast.5), channel_id=1, source_target_pairs={{0,2},{1,5},{2,0},{3,7},{4,6},{5,1},{6,4},{7,3},{8,10},{9,13},{10,... | collective-permute-start | bytes 2359304 | tf_op jit(solution)/shard_map/ppermute | solution.py:380
  10.9 20.7 %collective-permute-start.5 = (bf16[256,1536]{1,0:T(8,128)(2,1)S(1)}, bf16[256,1536]{1,0:T(8,128)(2,1)S(1)}, u32[]{:S(2)}, u32[]{:S(2)}) collective-permute-start(bf16[256,1536]{1,0:T(8,128)(2,1)S(1)} %collective-permute-done.3.refs_5_), channel_id=1, source_target_pairs={{0,2},{1,5},{2,0},{3,7},{4,6},{5,1},{6,4},{7,3},{8,10},{9,13},{10,... | collective-permute-start | bytes 2359304 | tf_op jit(solution)/shard_map/ppermute | solution.py:380
  23.9 7.8 %collective-permute-start.6 = (bf16[256,1536]{1,0:T(8,128)(2,1)S(1)}, bf16[256,1536]{1,0:T(8,128)(2,1)S(1)}, u32[]{:S(2)}, u32[]{:S(2)}) collective-permute-start(bf16[256,1536]{1,0:T(8,128)(2,1)S(1)} %collective-permute-done.4.refs_6_), channel_id=1, source_target_pairs={{0,1},{1,0},{2,3},{3,2},{4,5},{5,4},{6,7},{7,6},{8,9},{9,8},{10,11... | collective-permute-start | bytes 2359304 | tf_op jit(solution)/shard_map/ppermute | solution.py:377
  24.3 9.5 %collective-permute-start.12 = (bf16[384,1536]{1,0:T(8,128)(2,1)S(1)}, bf16[384,1536]{1,0:T(8,128)(2,1)S(1)}, u32[]{:S(2)}, u32[]{:S(2)}) collective-permute-start(bf16[384,1536]{1,0:T(8,128)(2,1)S(1)} %collective-permute-done.10.refs_13_), channel_id=1, source_target_pairs={{8,16},{16,24},{9,1},{17,9},{10,18},{18,26},{11,3},{19,11},{12,20}... | collective-permute-start | bytes 3538952 | tf_op jit(solution)/shard_map/ppermute | solution.py:390
  31.7 12.1 %collective-permute-start.8 = (bf16[256,1536]{1,0:T(8,128)(2,1)S(1)}, bf16[256,1536]{1,0:T(8,128)(2,1)S(1)}, u32[]{:S(2)}, u32[]{:S(2)}) collective-permute-start(bf16[256,1536]{1,0:T(8,128)(2,1)S(1)} %collective-permute-done.6.refs_8_), channel_id=1, source_target_pairs={{0,2},{1,5},{2,0},{3,7},{4,6},{5,1},{6,4},{7,3},{8,10},{9,13},{10,... | collective-permute-start | bytes 2359304 | tf_op jit(solution)/shard_map/ppermute | solution.py:380
  33.4 14.2 %collective-permute-start.11 = (bf16[384,1536]{1,0:T(8,128)(2,1)S(1)}, bf16[384,1536]{1,0:T(8,128)(2,1)S(1)}, u32[]{:S(2)}, u32[]{:S(2)}) collective-permute-start(bf16[384,1536]{1,0:T(8,128)(2,1)S(1)} %collective-permute-done.10.refs_13_), channel_id=1, source_target_pairs={{0,1},{1,0},{2,3},{3,2},{4,5},{5,4},{6,7},{7,6},{8,9},{9,8},{10,11... | collective-permute-start | bytes 3538952 | tf_op jit(solution)/shard_map/ppermute | solution.py:377
  33.7 13.8 %collective-permute-start.13 = (bf16[384,1536]{1,0:T(8,128)(2,1)S(1)}, bf16[384,1536]{1,0:T(8,128)(2,1)S(1)}, u32[]{:S(2)}, u32[]{:S(2)}) collective-permute-start(bf16[384,1536]{1,0:T(8,128)(2,1)S(1)} %collective-permute-done.12.refs_15_), channel_id=1, source_target_pairs={{0,1},{1,0},{2,3},{3,2},{4,5},{5,4},{6,7},{7,6},{8,9},{9,8},{10,11... | collective-permute-start | bytes 3538952 | tf_op jit(solution)/shard_map/ppermute | solution.py:377
  42.4 3.6 %collective-permute-start.7 = (bf16[256,1536]{1,0:T(8,128)(2,1)S(1)}, bf16[256,1536]{1,0:T(8,128)(2,1)S(1)}, u32[]{:S(2)}, u32[]{:S(2)}) collective-permute-start(bf16[256,1536]{1,0:T(8,128)(2,1)S(1)} %collective-permute-done.5.refs_7_), channel_id=1, source_target_pairs={{0,1},{1,0},{2,3},{3,2},{4,5},{5,4},{6,7},{7,6},{8,9},{9,8},{10,11... | collective-permute-start | bytes 2359304 | tf_op jit(solution)/shard_map/ppermute | solution.py:377
  43.7 3.8 %collective-permute-start.9 = (bf16[256,1536]{1,0:T(8,128)(2,1)S(1)}, bf16[256,1536]{1,0:T(8,128)(2,1)S(1)}, u32[]{:S(2)}, u32[]{:S(2)}) collective-permute-start(bf16[256,1536]{1,0:T(8,128)(2,1)S(1)} %collective-permute-done.8.refs_10_), channel_id=1, source_target_pairs={{0,1},{1,0},{2,3},{3,2},{4,5},{5,4},{6,7},{7,6},{8,9},{9,8},{10,11... | collective-permute-start | bytes 2359304 | tf_op jit(solution)/shard_map/ppermute | solution.py:377
  46.0 6.0 %collective-permute-start.14 = (bf16[384,512]{1,0:T(8,128)(2,1)S(1)}, bf16[384,512]{1,0:T(8,128)(2,1)S(1)}, u32[]{:S(2)}, u32[]{:S(2)}) collective-permute-start(bf16[384,512]{1,0:T(8,128)(2,1)S(1)} %slice.16), channel_id=1, source_target_pairs={{16,24},{9,1},{18,26},{11,3},{20,28},{13,5},{22,30},{15,7}} | collective-permute-start | bytes 1179656 | tf_op jit(solution)/shard_map/ppermute | solution.py:390
  46.8 11.9 %collective-permute-start.16 = (bf16[384,1024]{1,0:T(8,128)(2,1)S(1)}, bf16[384,1024]{1,0:T(8,128)(2,1)S(1)}, u32[]{:S(2)}, u32[]{:S(2)}) collective-permute-start(bf16[384,1024]{1,0:T(8,128)(2,1)S(1)} %slice.17), channel_id=1, source_target_pairs={{16,24},{9,1},{18,26},{11,3},{20,28},{13,5},{22,30},{15,7}} | collective-permute-start | bytes 2359304 | tf_op jit(solution)/shard_map/ppermute | solution.py:390
  52.0 4.8 %collective-permute-start.15 = (bf16[384,512]{1,0:T(8,128)(2,1)S(1)}, bf16[384,512]{1,0:T(8,128)(2,1)S(1)}, u32[]{:S(2)}, u32[]{:S(2)}) collective-permute-start(bf16[384,512]{1,0:T(8,128)(2,1)S(1)} %collective-permute-done.14.refs_3_), channel_id=1, source_target_pairs={{0,1},{1,0},{2,3},{3,2},{4,5},{5,4},{6,7},{7,6},{8,9},{9,8},{10,11... | collective-permute-start | bytes 1179656 | tf_op jit(solution)/shard_map/ppermute | solution.py:377
  57.2 6.9 %collective-permute-start.23 = (bf16[256,512]{1,0:T(8,128)(2,1)S(1)}, bf16[256,512]{1,0:T(8,128)(2,1)S(1)}, u32[]{:S(2)}, u32[]{:S(2)}) collective-permute-start(bf16[256,512]{1,0:T(8,128)(2,1)S(1)} %get-tuple-element.31.a_ref), channel_id=1, source_target_pairs={{0,2},{1,5},{2,0},{3,7},{4,6},{5,1},{6,4},{7,3},{8,10},{9,13},{10,... | collective-permute-start | bytes 786440 | tf_op jit(solution)/shard_map/ppermute | solution.py:380
  58.8 6.5 %collective-permute-start.17 = (bf16[384,512]{1,0:T(8,128)(2,1)S(1)}, bf16[384,512]{1,0:T(8,128)(2,1)S(1)}, u32[]{:S(2)}, u32[]{:S(2)}) collective-permute-start(bf16[384,512]{1,0:T(8,128)(2,1)S(1)} %get-tuple-element.42), channel_id=1, source_target_pairs={{0,1},{1,0},{2,3},{3,2},{4,5},{5,4},{6,7},{7,6},{8,9},{9,8},{10,11... | collective-permute-start | bytes 1179656 | tf_op jit(solution)/shard_map/ppermute | solution.py:377
  64.1 2.8 %collective-permute-start.24 = (bf16[256,512]{1,0:T(8,128)(2,1)S(1)}, bf16[256,512]{1,0:T(8,128)(2,1)S(1)}, u32[]{:S(2)}, u32[]{:S(2)}) collective-permute-start(bf16[256,512]{1,0:T(8,128)(2,1)S(1)} %collective-permute-done.23.a_ref), channel_id=1, source_target_pairs={{0,1},{1,0},{2,3},{3,2},{4,5},{5,4},{6,7},{7,6},{8,9},{9,8},{10,11... | collective-permute-start | bytes 786440 | tf_op jit(solution)/shard_map/ppermute | solution.py:377
  66.9 12.8 %collective-permute-start.25 = (bf16[256,1152]{1,0:T(8,128)(2,1)S(1)}, bf16[256,1152]{1,0:T(8,128)(2,1)S(1)}, u32[]{:S(2)}, u32[]{:S(2)}) collective-permute-start(bf16[256,1152]{1,0:T(8,128)(2,1)S(1)} %get-tuple-element.35.b_ref), channel_id=1, source_target_pairs={{0,2},{1,5},{2,0},{3,7},{4,6},{5,1},{6,4},{7,3},{8,10},{9,13},{10,... | collective-permute-start | bytes 1769480 | tf_op jit(solution)/shard_map/ppermute | solution.py:380
  70.0 9.7 %collective-permute-start.20 = (bf16[256,512]{1,0:T(8,128)(2,1)S(1)}, bf16[256,512]{1,0:T(8,128)(2,1)S(1)}, u32[]{:S(2)}, u32[]{:S(2)}) collective-permute-start(bf16[256,512]{1,0:T(8,128)(2,1)S(1)} %collective-permute-done.19), channel_id=1, source_target_pairs={{0,2},{1,5},{2,0},{3,7},{4,6},{5,1},{6,4},{7,3},{8,10},{9,13},{10,... | collective-permute-start | bytes 786440 | tf_op jit(solution)/shard_map/ppermute | solution.py:380
  71.2 8.4 %collective-permute-start.21 = (bf16[256,1152]{1,0:T(8,128)(2,1)S(1)}, bf16[256,1152]{1,0:T(8,128)(2,1)S(1)}, u32[]{:S(2)}, u32[]{:S(2)}) collective-permute-start(bf16[256,1152]{1,0:T(8,128)(2,1)S(1)} %get-tuple-element.35.b_ref), channel_id=1, source_target_pairs={{0,1},{1,0},{2,3},{3,2},{4,5},{5,4},{6,7},{7,6},{8,9},{9,8},{10,11... | collective-permute-start | bytes 1769480 | tf_op jit(solution)/shard_map/ppermute | solution.py:377
  79.6 2.0 %collective-permute-start.29 = (bf16[256,1152]{1,0:T(8,128)(2,1)S(1)}, bf16[256,1152]{1,0:T(8,128)(2,1)S(1)}, u32[]{:S(2)}, u32[]{:S(2)}) collective-permute-start(bf16[256,1152]{1,0:T(8,128)(2,1)S(1)} %collective-permute-done.25.b_ref), channel_id=1, source_target_pairs={{0,1},{1,0},{2,3},{3,2},{4,5},{5,4},{6,7},{7,6},{8,9},{9,8},{10,11... | collective-permute-start | bytes 1769480 | tf_op jit(solution)/shard_map/ppermute | solution.py:377
  79.6 9.9 %collective-permute-start.22 = (bf16[256,1152]{1,0:T(8,128)(2,1)S(1)}, bf16[256,1152]{1,0:T(8,128)(2,1)S(1)}, u32[]{:S(2)}, u32[]{:S(2)}) collective-permute-start(bf16[256,1152]{1,0:T(8,128)(2,1)S(1)} %collective-permute-done.21), channel_id=1, source_target_pairs={{0,2},{1,5},{2,0},{3,7},{4,6},{5,1},{6,4},{7,3},{8,10},{9,13},{10,... | collective-permute-start | bytes 1769480 | tf_op jit(solution)/shard_map/ppermute | solution.py:380
  81.6 15.2 %collective-permute-start.30 = (bf16[256,1152]{1,0:T(8,128)(2,1)S(1)}, bf16[256,1152]{1,0:T(8,128)(2,1)S(1)}, u32[]{:S(2)}, u32[]{:S(2)}) collective-permute-start(bf16[256,1152]{1,0:T(8,128)(2,1)S(1)} %collective-permute-done.29), channel_id=1, source_target_pairs={{0,2},{1,5},{2,0},{3,7},{4,6},{5,1},{6,4},{7,3},{8,10},{9,13},{10,... | collective-permute-start | bytes 1769480 | tf_op jit(solution)/shard_map/ppermute | solution.py:380
  83.1 15.6 %collective-permute-start.28 = (bf16[256,512]{1,0:T(8,128)(2,1)S(1)}, bf16[256,512]{1,0:T(8,128)(2,1)S(1)}, u32[]{:S(2)}, u32[]{:S(2)}) collective-permute-start(bf16[256,512]{1,0:T(8,128)(2,1)S(1)} %collective-permute-done.24), channel_id=1, source_target_pairs={{0,2},{1,5},{2,0},{3,7},{4,6},{5,1},{6,4},{7,3},{8,10},{9,13},{10,... | collective-permute-start | bytes 786440 | tf_op jit(solution)/shard_map/ppermute | solution.py:380
  95.3 12.1 %collective-permute-start.26 = (bf16[256,1536]{1,0:T(8,128)(2,1)S(1)}, bf16[256,1536]{1,0:T(8,128)(2,1)S(1)}, u32[]{:S(2)}, u32[]{:S(2)}) collective-permute-start(bf16[256,1536]{1,0:T(8,128)(2,1)S(1)} %experts.6), channel_id=1, source_target_pairs={{0,2},{1,5},{2,0},{3,7},{4,6},{5,1},{6,4},{7,3},{8,10},{9,13},{10,... | collective-permute-start | bytes 2359304 | tf_op jit(solution)/shard_map/ppermute | solution.py:380
  104.1 12.1 %collective-permute-start.31 = (bf16[256,1536]{1,0:T(8,128)(2,1)S(1)}, bf16[256,1536]{1,0:T(8,128)(2,1)S(1)}, u32[]{:S(2)}, u32[]{:S(2)}) collective-permute-start(bf16[256,1536]{1,0:T(8,128)(2,1)S(1)} %experts.7), channel_id=1, source_target_pairs={{0,2},{1,5},{2,0},{3,7},{4,6},{5,1},{6,4},{7,3},{8,10},{9,13},{10,... | collective-permute-start | bytes 2359304 | tf_op jit(solution)/shard_map/ppermute | solution.py:380
  116.2 2.3 %collective-permute-start.32 = (bf16[256,1536]{1,0:T(8,128)(2,1)S(1)}, bf16[256,1536]{1,0:T(8,128)(2,1)S(1)}, u32[]{:S(2)}, u32[]{:S(2)}) collective-permute-start(bf16[256,1536]{1,0:T(8,128)(2,1)S(1)} %collective-permute-done.31), channel_id=1, source_target_pairs={{0,1},{1,0},{2,3},{3,2},{4,5},{5,4},{6,7},{7,6},{8,9},{9,8},{10,11... | collective-permute-start | bytes 2359304 | tf_op jit(solution)/shard_map/ppermute | solution.py:377
  116.2 4.1 %collective-permute-start.27 = (bf16[256,1536]{1,0:T(8,128)(2,1)S(1)}, bf16[256,1536]{1,0:T(8,128)(2,1)S(1)}, u32[]{:S(2)}, u32[]{:S(2)}) collective-permute-start(bf16[256,1536]{1,0:T(8,128)(2,1)S(1)} %collective-permute-done.26), channel_id=1, source_target_pairs={{0,1},{1,0},{2,3},{3,2},{4,5},{5,4},{6,7},{7,6},{8,9},{9,8},{10,11... | collective-permute-start | bytes 2359304 | tf_op jit(solution)/shard_map/ppermute | solution.py:377
  118.7 12.1 %collective-permute-start.33 = (bf16[256,1536]{1,0:T(8,128)(2,1)S(1)}, bf16[256,1536]{1,0:T(8,128)(2,1)S(1)}, u32[]{:S(2)}, u32[]{:S(2)}) collective-permute-start(bf16[256,1536]{1,0:T(8,128)(2,1)S(1)} %add_convert_fusion), channel_id=1, source_target_pairs={{0,2},{1,5},{2,0},{3,7},{4,6},{5,1},{6,4},{7,3},{8,10},{9,13},{10,... | collective-permute-start | bytes 2359304 | tf_op jit(solution)/shard_map/ppermute | solution.py:380
  (16 other events, 119.8 us)

commit v4 on v3

--- a/solution.py
+++ b/solution.py
@@ -119,13 +119,20 @@
     )(logits, routes)
 
 
-def project_kernel(owners, sources, rank, held, *refs):
-    pools, shards = len(owners), len(sources)
-    ids, lengths, ctx_ref, res_ref = refs[:4]
-    pool, shard = refs[4 : 4 + pools], refs[4 + pools : 4 + pools + shards]
-    part_ref, low_s, up_s, sem = refs[-4:]
+def project_kernel(sources, ctx_ref, res_ref, *refs):
+    shard, part_ref = refs[:-1], refs[-1]
+    z, i = lax.axis_index("dp"), lax.axis_index("expert")
+    part_ref[...] = res_ref[...].astype(F32)
+    for source, piece in zip(sources, shard):
+        add_shard(source(z, i), ctx_ref, piece, part_ref)
+
+
+def adapt_kernel(owners, rank, *refs):
+    ids, lengths, ctx_ref, part_ref = refs[:4]
+    pool = refs[4:-4]
+    out_ref, low_s, up_s, sem = refs[-4:]
     requests = ids.shape[0]
-    z, i = lax.axis_index("dp"), lax.axis_index("expert")
+    i = lax.axis_index("expert")
 
     def copies(r, ref, first):
         return [
@@ -136,17 +143,14 @@
         ]
 
     for r in range(requests):
-        for k in range(pools):
-            at = ids[r] - owners[k](i) * held
+        for k, owner in enumerate(owners):
+            at = ids[r] - owner(i)
 
             @pl.when((at >= 0) & (at < pool[k].shape[0] // (2 * rank)))
             def _():
                 for c in copies(r, pool[k], pl.multiple_of(at * (2 * rank), 2 * rank)):
                     c.start()
 
-    part_ref[...] = res_ref[...].astype(F32)
-    for source, piece in zip(sources, shard):
-        add_shard(source(z, i), ctx_ref, piece, part_ref)
     for r in range(requests):
         for c in copies(r, pool[0], 0):
             c.wait()
@@ -162,7 +166,7 @@
         inside = (row >= start) & (row < end)
         mine = mine | (inside & (lane >= r * rank) & (lane < (r + 1) * rank))
     low = jnp.where(mine, low, 0.0).astype(BF16)
-    part_ref[...] += jnp.dot(low, up_s[...], preferred_element_type=F32)
+    out_ref[...] = part_ref[...] + jnp.dot(low, up_s[...], preferred_element_type=F32)
 
 
 def add_shard(at, ctx_ref, piece, total_ref):
@@ -174,14 +178,26 @@
         )
 
 
-def project(known, ctx, residual, pools, owners, shards, sources, rank, held):
-    requests = known[0].shape[0]
-    tokens, width = residual.shape
+def project(ctx, residual, shards, sources):
     return call(
-        functools.partial(project_kernel, owners, sources, rank, held),
+        functools.partial(project_kernel, sources),
         "project",
-        jax.ShapeDtypeStruct((tokens, width), F32),
-        [SMEM] * 2 + [VMEM] * 2 + [ANY] * len(pools) + [VMEM] * len(shards),
+        jax.ShapeDtypeStruct(residual.shape, F32),
+        [VMEM] * (2 + len(shards)),
+        VMEM,
+        [],
+        8,
+        10**9,
+    )(ctx, residual, *shards)
+
+
+def adapt(known, ctx, part, pools, owners, rank):
+    requests, width = known[0].shape[0], part.shape[1]
+    return call(
+        functools.partial(adapt_kernel, owners, rank),
+        "adapt",
+        jax.ShapeDtypeStruct(part.shape, F32),
+        [SMEM] * 2 + [VMEM] * 2 + [ANY] * len(pools),
         VMEM,
         [
             pltpu.VMEM((requests * rank, width), BF16),
@@ -190,7 +206,7 @@
         ],
         8,
         10**9,
-    )(*known, ctx, residual, *pools, *shards)
+    )(*known, ctx, part, *pools)
 
 
 def first_columns(width):
@@ -349,17 +365,8 @@
         context = attend(lengths, queries, rotated_key_heads, token_value_heads, 0, pairs)
         shard = lax.all_gather(attention_output_weight, "dp", axis=0, tiled=True)
         pool = lax.all_gather(own, "expert", axis=0, tiled=True)
-        part = project(
-            known,
-            context,
-            residual,
-            [pool],
-            [lambda i: 0],
-            [shard],
-            [lambda z, i: z * 0],
-            rank,
-            held,
-        )
+        part = project(context, residual, [shard], [lambda z, i: z * 0])
+        part = adapt(known, context, part, [pool], [lambda i: i * 0], rank)
         hidden0, send0 = close(part, context, expert_norm_scale, [], [])
         hidden1, send1 = close(part, context, expert_norm_scale, [], [], (hidden0, gains))
         every0 = lax.all_gather(send0, "expert", axis=0, tiled=True)
@@ -379,6 +386,9 @@
     def across(a):
         return lax.ppermute(a, "expert", [(e, e ^ (4 if e & 1 else 2)) for e in range(n_ex)])
 
+    def turned(a):
+        return lax.ppermute(a, "expert", [(e, e ^ (3 if e & 1 else 5)) for e in range(n_ex)])
+
     def along(a, step):
         sent = []
         for e in range(n_ex):
@@ -410,39 +420,39 @@
     p1 = across(other)
     context = attend_next(0, None, pair_weights[0])
     z2 = along(after(z1, context), 2)
+    p0_other = beside(after(p0, context))
     context = attend_next(1, context, pair_weights[1])
-    p0_other = beside(after(p0, context))
     pair_weights.append(beside(weights[2]))
-    context = attend_next(2, context)
+    context = attend_next(2, context, pair_weights[2])
     context = attend_next(3, context)
     p2 = across(after(p0_other, p1, context))
-    p1_other, p2_other = beside(p1), beside(p2)
+    p1_other = beside(p1)
     z1_other, z2_other = beside(z1), beside(z2)
     z3 = [along(z2[:, :cut], 3), along(z2[:, cut:], 3)]
+    few = held * 3 // 4
     owners = [
-        lambda i: i,
-        lambda i: i ^ 1,
-        lambda i: i ^ (2 + 2 * (i & 1)),
-        lambda i: i ^ (3 + 2 * (i & 1)),
-        lambda i: i ^ (5 - 2 * (i & 1)),
-        lambda i: i ^ (4 - 2 * (i & 1)),
-        lambda i: i ^ 7,
-        lambda i: i ^ 6,
+        lambda i: i * held,
+        lambda i: (i ^ 1) * held,
+        lambda i: (i ^ (2 + 2 * (i & 1))) * held,
+        lambda i: (i ^ (3 + 2 * (i & 1))) * held,
+        lambda i: (i ^ (5 - 2 * (i & 1))) * held,
+        lambda i: (i ^ (4 - 2 * (i & 1))) * held,
+        lambda i: (i ^ 7) * held,
+        lambda i: (i ^ 6) * held,
+        lambda i: (i ^ 6) * held + few,
     ]
     part = project(
-        known,
         context,
-        after(residual, pair_weights[2]),
-        [own, other, p0, p1, p0_other, p1_other, p2, p2_other],
-        owners,
+        residual,
         [attention_output_weight, z1, z1_other, z2, z2_other],
         [lambda z, i: z * rows] + [first_row(s, side) for s in (1, 2) for side in (-1, 1)],
-        rank,
-        held,
     )
+    p2_other = [beside(p2[: few * 2 * rank]), beside(p2[few * 2 * rank :])]
+    pools = [own, other, p0, p1, p0_other, p1_other, p2, *p2_other]
+    whole = adapt(known, context, part, pools, owners, rank)
     ends = [first_row(3, -1), first_row(3, 1)]
-    task = functools.partial(close, part, context, expert_norm_scale)
-    hidden0, send0 = task([z3[0], beside(after(z3[0], part))], ends)
+    task = functools.partial(close, whole, context, expert_norm_scale)
+    hidden0, send0 = task([z3[0], beside(z3[0])], ends)
     other0 = beside(send0)
     near0, next0 = across(send0), across(other0)
     late = after(z3[1], send0)
@@ -461,9 +471,10 @@
     r_next = run((next0, after(next1, r_near)))
     back = across(r_next)
     r_far = run((far0, after(far1, r_next)))
-    via = beside(after(across(r_far), back))
+    ready = beside(r_near)
+    far_sum = across(r_far).astype(F32) + ready.astype(F32)
     back1 = beside(back)
-    back0 = across((r_near.astype(F32) + via.astype(F32)).astype(BF16))
+    back0 = turned(far_sum.astype(BF16))
     return finish(hidden0, hidden1, [home, back1, back0])
 
 

time: 132 us -> 125 us (0.947)
  starting transfers between devices: 44.4 us -> 32.7 us
  waiting for transfers between devices: 41.3 us -> 47.4 us
  local copies, waits for them, and re-layouts: 2.31 us -> 0.29 us
    ppermute x0 -> x1, waiting for transfers between devices: none -> 11.4 us  [turned(): lax.ppermute(a, 'expert', [(e, e ^ (3 if e & 1 else 5)) for e in range(n_...]
    ppermute x18 -> x19, starting transfers between devices: 20.5 us -> 14 us  [beside(): return lax.ppermute(a, 'expert', [(e, e ^ 1) for e in range(n_ex)])]
    ppermute x18 -> x19, waiting for transfers between devices: 9.55 us -> 3.83 us  [beside(): return lax.ppermute(a, 'expert', [(e, e ^ 1) for e in range(n_ex)])]
    ppermute x12 -> x11, starting transfers between devices: 17.2 us -> 11.7 us  [across(): lax.ppermute(a, 'expert', [(e, e ^ (4 if e & 1 else 2)) for e in range(n_...]
    ppermute x4, waiting for transfers between devices: 4.19 us -> 7.41 us  [along(): return lax.ppermute(a, ('dp', 'expert'), sent)]
    ppermute x12 -> x11, waiting for transfers between devices: 27.6 us -> 24.8 us  [across(): lax.ppermute(a, 'expert', [(e, e ^ (4 if e & 1 else 2)) for e in range(n_...]
    unnamed x28 -> x26, local copies, waits for them, and re-layouts: 2.14 us -> 0.06 us
    pallas_call x1 -> x2, Pallas kernels: 4.41 us -> 4.41 us  [the longest x1 2.58 us: adapt(): call(functools.partial(adapt_kernel, owners, rank), 'adapt', jax.ShapeDty...]
  transfers between devices with their start and end apart: 34 -> 35, of which waited for: 16 -> 12; matrix products, arithmetic and copies ran while one was open for 1% -> 1% of each run, Pallas kernels for 31% -> 33%
where the time goes in v4:
time: 125 us; the launch traced here: 124 us
  waiting for transfers between devices  47.4 us (38%)
  Pallas kernels  42.3 us (34%)
  starting transfers between devices  32.7 us (26%)
  other arithmetic  1.4 us (1%)
    ppermute x11, waiting for transfers between devices, across(): lax.ppermute(a, 'expert', [(e, e ^ (4 if e & 1 else 2)) for e in range(n_...  24.8 us
    pallas_call x4, Pallas kernels, run_experts(): call(functools.partial(experts_kernel, groups, spread), 'experts', jax.Sh...  22 us
    ppermute x19, starting transfers between devices, beside(): return lax.ppermute(a, 'expert', [(e, e ^ 1) for e in range(n_ex)])  14 us
    pallas_call x4, Pallas kernels, attend(): pl.pallas_call(attend_kernel, name='attend', grid=(pairs,), out_shape=jax...  13.3 us
    ppermute x11, starting transfers between devices, across(): lax.ppermute(a, 'expert', [(e, e ^ (4 if e & 1 else 2)) for e in range(n_...  11.7 us
    ppermute x1, waiting for transfers between devices, turned(): lax.ppermute(a, 'expert', [(e, e ^ (3 if e & 1 else 5)) for e in range(n_...  11.4 us
    ppermute x4, waiting for transfers between devices, along(): return lax.ppermute(a, ('dp', 'expert'), sent)  7.41 us
    ppermute x4, starting transfers between devices, along(): return lax.ppermute(a, ('dp', 'expert'), sent)  6.86 us
  transfers between devices with their start and end apart: 35, of which 12 were waited for; matrix products, arithmetic and copies ran while one was open for 1% of the time, Pallas kernels for 33%

profile of v4, /device:TPU:0, one launch (start us, length us, event | category | flops | bytes accessed | tf_op | source)
XLA Modules:
  0.0 124.5 jit_solution(16212794113142543814)
XLA Ops:
  1.0 4.6 %collective-permute-start.3 = (bf16[384,1536]{1,0:T(8,128)(2,1)}, bf16[384,1536]{1,0:T(8,128)(2,1)S(1)}, u32[]{:S(2)}, u32[]{:S(2)}) collective-permute-start(bf16[384,1536]{1,0:T(8,128)(2,1)} %refs_0_.6), channel_id=1, source_target_pairs={{0,8},{8,16},{16,24},{9,1},{17,9},{25,17},{2,10},{10,18},{18,26},{... | collective-permute-start | bytes 3538952 | tf_op jit(solution)/shard_map/ppermute | solution.py:400
  5.7 1.2 pad_maximum_fusion
  7.0 1.9 %collective-permute-start.8 = (bf16[256,1536]{1,0:T(8,128)(2,1)S(1)}, bf16[256,1536]{1,0:T(8,128)(2,1)S(1)}, u32[]{:S(2)}, u32[]{:S(2)}) collective-permute-start(bf16[256,1536]{1,0:T(8,128)(2,1)S(1)} %bitcast.5), channel_id=1, source_target_pairs={{0,2},{1,5},{2,0},{3,7},{4,6},{5,1},{6,4},{7,3},{8,10},{9,13},{10,... | collective-permute-start | bytes 2359304 | tf_op jit(solution)/shard_map/ppermute | solution.py:387
  8.9 3.3 %attend.4.refs_0_ = bf16[256,1536]{1,0:T(8,128)(2,1)S(1)} custom-call(s32[1,4]{1,0:T(1,128)S(1)} %copy-done.7, bf16[256,1536]{1,0:T(8,128)(2,1)S(1)} %copy-done.8, bf16[256,512]{1,0:T(8,128)(2,1)S(1)} %copy-done.9, bf16[256,512]{1,0:T(8,128)(2,1)S(1)} %copy-done.10), custom_call_target="tpu_custom_call" | custom-call | flops 1000000000 | bytes 1024 | tf_op jit(solution)/shard_map/attend/pallas_call | solution.py:72
  12.2 7.4 %collective-permute-done.3.refs_1_ = bf16[384,1536]{1,0:T(8,128)(2,1)S(1)} collective-permute-done((bf16[384,1536]{1,0:T(8,128)(2,1)}, bf16[384,1536]{1,0:T(8,128)(2,1)S(1)}, u32[]{:S(2)}, u32[]{:S(2)}) %collective-permute-start.3) | collective-permute-done | bytes 1179680 | tf_op jit(solution)/shard_map/ppermute | solution.py:400
  20.4 1.6 %collective-permute-start.9 = (bf16[256,1536]{1,0:T(8,128)(2,1)S(1)}, bf16[256,1536]{1,0:T(8,128)(2,1)S(1)}, u32[]{:S(2)}, u32[]{:S(2)}) collective-permute-start(bf16[256,1536]{1,0:T(8,128)(2,1)S(1)} %collective-permute-done.7.refs_5_), channel_id=1, source_target_pairs={{0,2},{1,5},{2,0},{3,7},{4,6},{5,1},{6,4},{7,3},{8,10},{9,13},{10,... | collective-permute-start | bytes 2359304 | tf_op jit(solution)/shard_map/ppermute | solution.py:387
  22.4 3.3 %attend.5.refs_0_ = bf16[256,1536]{1,0:T(8,128)(2,1)S(1)} custom-call(s32[1,4]{1,0:T(1,128)S(1)} %copy-done.7, bf16[256,1536]{1,0:T(8,128)(2,1)S(1)} %copy-done.8, bf16[256,512]{1,0:T(8,128)(2,1)S(1)} %copy-done.9, bf16[256,512]{1,0:T(8,128)(2,1)S(1)} %copy-done.10, bf16[256,1536]{1,0:T(8,128)(2,1)S(1)} %attend.4.refs_0_), custom_call_target="tpu_custom_call", output_to_operand_aliasing={{}: (4, {})} | custom-call | flops 1000000000 | bytes 1024 | tf_op jit(solution)/shard_map/attend/pallas_call | solution.py:72
  25.8 3.3 %attend.6.refs_0_ = bf16[256,1536]{1,0:T(8,128)(2,1)S(1)} custom-call(s32[1,4]{1,0:T(1,128)S(1)} %copy-done.7, bf16[256,1536]{1,0:T(8,128)(2,1)S(1)} %copy-done.8, bf16[256,512]{1,0:T(8,128)(2,1)S(1)} %copy-done.9, bf16[256,512]{1,0:T(8,128)(2,1)S(1)} %copy-done.10, bf16[256,1536]{1,0:T(8,128)(2,1)S(1)} %attend.5.refs_0_), custom_call_target="tpu_custom_call", output_to_operand_aliasing={{}: (4, {})} | custom-call | flops 1000000000 | bytes 1024 | tf_op jit(solution)/shard_map/attend/pallas_call | solution.py:72
  29.1 3.3 %attend.7.ctx_ref.refs_2_.refs_1_ = bf16[256,1536]{1,0:T(8,128)(2,1)S(1)} custom-call(s32[1,4]{1,0:T(1,128)S(1)} %copy-done.7, bf16[256,1536]{1,0:T(8,128)(2,1)S(1)} %copy-done.8, bf16[256,512]{1,0:T(8,128)(2,1)S(1)} %copy-done.9, bf16[256,512]{1,0:T(8,128)(2,1)S(1)} %copy-done.10, bf16[256,1536]{1,0:T(8,128)(2,1)S(1)} %attend.6.refs_0_), custom_call_target="tpu_custom_call", output_to_operand_aliasing={{}: (4, {})} | custom-call | flops 1000000000 | bytes 1024 | tf_op jit(solution)/shard_map/attend/pallas_call | solution.py:72
  32.4 1.5 %collective-permute-start.12 = (bf16[256,1536]{1,0:T(8,128)(2,1)S(1)}, bf16[256,1536]{1,0:T(8,128)(2,1)S(1)}, u32[]{:S(2)}, u32[]{:S(2)}) collective-permute-start(bf16[256,1536]{1,0:T(8,128)(2,1)S(1)} %collective-permute-done.10.refs_8_), channel_id=1, source_target_pairs={{0,2},{1,5},{2,0},{3,7},{4,6},{5,1},{6,4},{7,3},{8,10},{9,13},{10,... | collective-permute-start | bytes 2359304 | tf_op jit(solution)/shard_map/ppermute | solution.py:387
  33.9 3.2 %collective-permute-start.6 = (bf16[384,1536]{1,0:T(8,128)(2,1)S(1)}, bf16[384,1536]{1,0:T(8,128)(2,1)S(1)}, u32[]{:S(2)}, u32[]{:S(2)}) collective-permute-start(bf16[384,1536]{1,0:T(8,128)(2,1)S(1)} %collective-permute-done.5.refs_3_), channel_id=1, source_target_pairs={{0,1},{1,0},{2,3},{3,2},{4,5},{5,4},{6,7},{7,6},{8,9},{9,8},{10,11... | collective-permute-start | bytes 3538952 | tf_op jit(solution)/shard_map/ppermute | solution.py:384
  38.1 6.4 %collective-permute-done.12.refs_10_ = bf16[256,1536]{1,0:T(8,128)(2,1)S(1)} collective-permute-done((bf16[256,1536]{1,0:T(8,128)(2,1)S(1)}, bf16[256,1536]{1,0:T(8,128)(2,1)S(1)}, u32[]{:S(2)}, u32[]{:S(2)}) %collective-permute-start.12) | collective-permute-done | bytes 786464 | tf_op jit(solution)/shard_map/ppermute | solution.py:387
  45.4 0.9 collective-permute-start.16
  46.4 1.8 %project.1.refs_3_ = f32[256,1536]{1,0:T(8,128)S(1)} custom-call(bf16[256,1536]{1,0:T(8,128)(2,1)S(1)} %attend.7.ctx_ref.refs_2_.refs_1_, bf16[256,1536]{1,0:T(8,128)(2,1)S(1)} %copy-done.4, bf16[384,1536]{1,0:T(8,128)(2,1)S(1)} %copy-done.3, bf16[384,1536]{1,0:T(8,128)(2,1)S(1)} %collective-permute-done.3.refs_1_, ...), custom_call_target="tpu_custom_call" | custom-call | flops 1000000000 | bytes 1024 | tf_op jit(solution)/shard_map/project/pallas_call | solution.py:182
  48.3 2.6 %adapt.1.refs_0_ = f32[256,1536]{1,0:T(8,128)S(1)} custom-call(s32[4]{0:T(128)S(1)} %copy-done.6, s32[1,4]{1,0:T(1,128)S(1)} %copy-done.7, bf16[256,1536]{1,0:T(8,128)(2,1)S(1)} %attend.7.ctx_ref.refs_2_.refs_1_, f32[256,1536]{1,0:T(8,128)S(1)} %project.1.refs_3_, bf16[256,1536]{1,0:T(8,128)(2,1)S(1)} %bitcast.6, ...), custom_call_target="tpu_custom_call" | custom-call | flops 1000000000 | bytes 1024 | tf_op jit(solution)/shard_map/adapt/pallas_call | solution.py:196
  51.3 1.6 %collective-permute-start.24 = (bf16[256,512]{1,0:T(8,128)(2,1)S(1)}, bf16[256,512]{1,0:T(8,128)(2,1)S(1)}, u32[]{:S(2)}, u32[]{:S(2)}) collective-permute-start(bf16[256,512]{1,0:T(8,128)(2,1)S(1)} %get-tuple-element.28.a_ref), channel_id=1, source_target_pairs={{0,2},{1,5},{2,0},{3,7},{4,6},{5,1},{6,4},{7,3},{8,10},{9,13},{10,... | collective-permute-start | bytes 786440 | tf_op jit(solution)/shard_map/ppermute | solution.py:387
  53.0 6.4 %collective-permute-start.18 = (bf16[384,512]{1,0:T(8,128)(2,1)S(1)}, bf16[384,512]{1,0:T(8,128)(2,1)S(1)}, u32[]{:S(2)}, u32[]{:S(2)}) collective-permute-start(bf16[384,512]{1,0:T(8,128)(2,1)S(1)} %get-tuple-element.38), channel_id=1, source_target_pairs={{0,1},{1,0},{2,3},{3,2},{4,5},{5,4},{6,7},{7,6},{8,9},{9,8},{10,11... | collective-permute-start | bytes 1179656 | tf_op jit(solution)/shard_map/ppermute | solution.py:384
  61.3 0.9 close.3
  62.8 1.1 collective-permute-start.20
  63.9 1.2 collective-permute-done.20
  65.9 5.4 %experts.4.refs_0_ = bf16[256,1536]{1,0:T(8,128)(2,1)S(1)} custom-call(bf16[256,512]{1,0:T(8,128)(2,1)S(1)} %get-tuple-element.28.a_ref, bf16[256,1152]{1,0:T(8,128)(2,1)S(1)} %get-tuple-element.32.b_ref, bf16[2,1536,512]{2,1,0:T(8,128)(2,1)S(1)} %copy-done, bf16[2,1536,512]{2,1,0:T(8,128)(2,1)S(1)} %copy-done.1, bf16[2,512,1536]{2,1,0:T(8,128)(2,1)S(1)} %copy-done.2, ...), custom_call_target="tpu_custom_call" | custom-call | flops 1000000000 | bytes 1024 | tf_op jit(solution)/shard_map/experts/pallas_call | solution.py:297
  71.3 3.7 %collective-permute-done.21.a_ref = bf16[256,512]{1,0:T(8,128)(2,1)S(1)} collective-permute-done((bf16[256,512]{1,0:T(8,128)(2,1)S(1)}, bf16[256,512]{1,0:T(8,128)(2,1)S(1)}, u32[]{:S(2)}, u32[]{:S(2)}) %collective-permute-start.21) | collective-permute-done | bytes 262176 | tf_op jit(solution)/shard_map/ppermute | solution.py:387
  75.6 1.4 %collective-permute-done.30 = bf16[256,1152]{1,0:T(8,128)(2,1)S(1)} collective-permute-done((bf16[256,1152]{1,0:T(8,128)(2,1)S(1)}, bf16[256,1152]{1,0:T(8,128)(2,1)S(1)}, u32[]{:S(2)}, u32[]{:S(2)}) %collective-permute-start.30) | collective-permute-done | bytes 589856 | tf_op jit(solution)/shard_map/ppermute | solution.py:384
  77.5 1.5 %collective-permute-start.29 = (bf16[256,512]{1,0:T(8,128)(2,1)S(1)}, bf16[256,512]{1,0:T(8,128)(2,1)S(1)}, u32[]{:S(2)}, u32[]{:S(2)}) collective-permute-start(bf16[256,512]{1,0:T(8,128)(2,1)S(1)} %collective-permute-done.25), channel_id=1, source_target_pairs={{0,2},{1,5},{2,0},{3,7},{4,6},{5,1},{6,4},{7,3},{8,10},{9,13},{10,... | collective-permute-start | bytes 786440 | tf_op jit(solution)/shard_map/ppermute | solution.py:387
  79.0 5.4 %experts.5 = bf16[256,1536]{1,0:T(8,128)(2,1)S(1)} custom-call(bf16[256,512]{1,0:T(8,128)(2,1)S(1)} %collective-permute-done.24.a_ref, bf16[256,1152]{1,0:T(8,128)(2,1)S(1)} %collective-permute-done.26.b_ref, bf16[2,1536,512]{2,1,0:T(8,128)(2,1)S(1)} %copy-done, bf16[2,1536,512]{2,1,0:T(8,128)(2,1)S(1)} %copy-done.1, bf16[2,512,1536]{2,1,0:T(8,128)(2,1)S(1)} %copy-done.2, ...), custom_call_target="tpu_custom_call" | custom-call | flops 1000000000 | bytes 1024 | tf_op jit(solution)/shard_map/experts/pallas_call | solution.py:297
  84.9 5.7 %experts.6 = bf16[256,1536]{1,0:T(8,128)(2,1)S(1)} custom-call(bf16[256,512]{1,0:T(8,128)(2,1)S(1)} %collective-permute-done.21.a_ref, bf16[256,1152]{1,0:T(8,128)(2,1)S(1)} %collective-permute-done.23.b_ref, bf16[2,1536,512]{2,1,0:T(8,128)(2,1)S(1)} %copy-done, bf16[2,1536,512]{2,1,0:T(8,128)(2,1)S(1)} %copy-done.1, bf16[2,512,1536]{2,1,0:T(8,128)(2,1)S(1)} %copy-done.2, ...), custom_call_target="tpu_custom_call" | custom-call | flops 1000000000 | bytes 1024 | tf_op jit(solution)/shard_map/experts/pallas_call | solution.py:297
  91.3 2.8 %collective-permute-done.29.a_ref = bf16[256,512]{1,0:T(8,128)(2,1)S(1)} collective-permute-done((bf16[256,512]{1,0:T(8,128)(2,1)S(1)}, bf16[256,512]{1,0:T(8,128)(2,1)S(1)}, u32[]{:S(2)}, u32[]{:S(2)}) %collective-permute-start.29) | collective-permute-done | bytes 262176 | tf_op jit(solution)/shard_map/ppermute | solution.py:387
  94.1 5.4 %experts.7 = bf16[256,1536]{1,0:T(8,128)(2,1)S(1)} custom-call(bf16[256,512]{1,0:T(8,128)(2,1)S(1)} %collective-permute-done.29.a_ref, bf16[256,1152]{1,0:T(8,128)(2,1)S(1)} %collective-permute-done.31.b_ref, bf16[2,1536,512]{2,1,0:T(8,128)(2,1)S(1)} %copy-done, bf16[2,1536,512]{2,1,0:T(8,128)(2,1)S(1)} %copy-done.1, bf16[2,512,1536]{2,1,0:T(8,128)(2,1)S(1)} %copy-done.2, ...), custom_call_target="tpu_custom_call" | custom-call | flops 1000000000 | bytes 1024 | tf_op jit(solution)/shard_map/experts/pallas_call | solution.py:297
  100.1 2.6 %collective-permute-done.27 = bf16[256,1536]{1,0:T(8,128)(2,1)S(1)} collective-permute-done((bf16[256,1536]{1,0:T(8,128)(2,1)S(1)}, bf16[256,1536]{1,0:T(8,128)(2,1)S(1)}, u32[]{:S(2)}, u32[]{:S(2)}) %collective-permute-start.27) | collective-permute-done | bytes 786464 | tf_op jit(solution)/shard_map/ppermute | solution.py:387
  102.7 8.9 %collective-permute-done.32 = bf16[256,1536]{1,0:T(8,128)(2,1)S(1)} collective-permute-done((bf16[256,1536]{1,0:T(8,128)(2,1)S(1)}, bf16[256,1536]{1,0:T(8,128)(2,1)S(1)}, u32[]{:S(2)}, u32[]{:S(2)}) %collective-permute-start.32) | collective-permute-done | bytes 786464 | tf_op jit(solution)/shard_map/ppermute | solution.py:387
  111.9 11.4 %collective-permute-done.34.refs_2_ = bf16[256,1536]{1,0:T(8,128)(2,1)S(1)} collective-permute-done((bf16[256,1536]{1,0:T(8,128)(2,1)S(1)}, bf16[256,1536]{1,0:T(8,128)(2,1)S(1)}, u32[]{:S(2)}, u32[]{:S(2)}) %collective-permute-start.34) | collective-permute-done | bytes 786464 | tf_op jit(solution)/shard_map/ppermute | solution.py:390
  123.3 1.2 finish.1
  (85 shorter events, 11.3 us)
Async XLA Ops:
  0.0 6.9 %collective-permute-start.2 = (bf16[2,1536,512]{2,1,0:T(8,128)(2,1)}, bf16[2,1536,512]{2,1,0:T(8,128)(2,1)S(1)}, u32[]{:S(2)}, u32[]{:S(2)}) collective-permute-start(bf16[2,1536,512]{2,1,0:T(8,128)(2,1)} %refs_0_.11), channel_id=1, source_target_pairs={{0,1},{1,0},{2,3},{3,2},{4,5},{5,4},{6,7},{7,6},{8,9},{9,8},{10,11... | collective-permute-start | bytes 9437192 | tf_op jit(solution)/shard_map/ppermute | solution.py:384
  0.5 21.8 %collective-permute-start.1 = (bf16[2,1536,512]{2,1,0:T(8,128)(2,1)}, bf16[2,1536,512]{2,1,0:T(8,128)(2,1)S(1)}, u32[]{:S(2)}, u32[]{:S(2)}) collective-permute-start(bf16[2,1536,512]{2,1,0:T(8,128)(2,1)} %refs_1_.9), channel_id=1, source_target_pairs={{0,1},{1,0},{2,3},{3,2},{4,5},{5,4},{6,7},{7,6},{8,9},{9,8},{10,11... | collective-permute-start | bytes 9437192 | tf_op jit(solution)/shard_map/ppermute | solution.py:384
  0.6 21.8 %collective-permute-start = (bf16[2,512,1536]{2,1,0:T(8,128)(2,1)}, bf16[2,512,1536]{2,1,0:T(8,128)(2,1)S(1)}, u32[]{:S(2)}, u32[]{:S(2)}) collective-permute-start(bf16[2,512,1536]{2,1,0:T(8,128)(2,1)} %refs_2_.11), channel_id=1, source_target_pairs={{0,1},{1,0},{2,3},{3,2},{4,5},{5,4},{6,7},{7,6},{8,9},{9,8},{10,11... | collective-permute-start | bytes 9437192 | tf_op jit(solution)/shard_map/ppermute | solution.py:384
  1.0 18.6 %collective-permute-start.3 = (bf16[384,1536]{1,0:T(8,128)(2,1)}, bf16[384,1536]{1,0:T(8,128)(2,1)S(1)}, u32[]{:S(2)}, u32[]{:S(2)}) collective-permute-start(bf16[384,1536]{1,0:T(8,128)(2,1)} %refs_0_.6), channel_id=1, source_target_pairs={{0,8},{8,16},{16,24},{9,1},{17,9},{25,17},{2,10},{10,18},{18,26},{... | collective-permute-start | bytes 3538952 | tf_op jit(solution)/shard_map/ppermute | solution.py:400
  6.9 13.5 %collective-permute-start.7 = (bf16[256,1536]{1,0:T(8,128)(2,1)S(1)}, bf16[256,1536]{1,0:T(8,128)(2,1)S(1)}, u32[]{:S(2)}, u32[]{:S(2)}) collective-permute-start(bf16[256,1536]{1,0:T(8,128)(2,1)S(1)} %bitcast.4), channel_id=1, source_target_pairs={{0,1},{1,0},{2,3},{3,2},{4,5},{5,4},{6,7},{7,6},{8,9},{9,8},{10,11... | collective-permute-start | bytes 2359304 | tf_op jit(solution)/shard_map/ppermute | solution.py:384
  7.0 15.0 %collective-permute-start.8 = (bf16[256,1536]{1,0:T(8,128)(2,1)S(1)}, bf16[256,1536]{1,0:T(8,128)(2,1)S(1)}, u32[]{:S(2)}, u32[]{:S(2)}) collective-permute-start(bf16[256,1536]{1,0:T(8,128)(2,1)S(1)} %bitcast.5), channel_id=1, source_target_pairs={{0,2},{1,5},{2,0},{3,7},{4,6},{5,1},{6,4},{7,3},{8,10},{9,13},{10,... | collective-permute-start | bytes 2359304 | tf_op jit(solution)/shard_map/ppermute | solution.py:387
  19.6 14.3 %collective-permute-start.5 = (bf16[384,1536]{1,0:T(8,128)(2,1)S(1)}, bf16[384,1536]{1,0:T(8,128)(2,1)S(1)}, u32[]{:S(2)}, u32[]{:S(2)}) collective-permute-start(bf16[384,1536]{1,0:T(8,128)(2,1)S(1)} %collective-permute-done.3.refs_1_), channel_id=1, source_target_pairs={{8,16},{16,24},{9,1},{17,9},{10,18},{18,26},{11,3},{19,11},{12,20}... | collective-permute-start | bytes 3538952 | tf_op jit(solution)/shard_map/ppermute | solution.py:400
  20.4 12.1 %collective-permute-start.9 = (bf16[256,1536]{1,0:T(8,128)(2,1)S(1)}, bf16[256,1536]{1,0:T(8,128)(2,1)S(1)}, u32[]{:S(2)}, u32[]{:S(2)}) collective-permute-start(bf16[256,1536]{1,0:T(8,128)(2,1)S(1)} %collective-permute-done.7.refs_5_), channel_id=1, source_target_pairs={{0,2},{1,5},{2,0},{3,7},{4,6},{5,1},{6,4},{7,3},{8,10},{9,13},{10,... | collective-permute-start | bytes 2359304 | tf_op jit(solution)/shard_map/ppermute | solution.py:387
  21.9 10.5 %collective-permute-start.10 = (bf16[256,1536]{1,0:T(8,128)(2,1)S(1)}, bf16[256,1536]{1,0:T(8,128)(2,1)S(1)}, u32[]{:S(2)}, u32[]{:S(2)}) collective-permute-start(bf16[256,1536]{1,0:T(8,128)(2,1)S(1)} %collective-permute-done.8.refs_6_), channel_id=1, source_target_pairs={{0,1},{1,0},{2,3},{3,2},{4,5},{5,4},{6,7},{7,6},{8,9},{9,8},{10,11... | collective-permute-start | bytes 2359304 | tf_op jit(solution)/shard_map/ppermute | solution.py:384
  22.3 22.9 %collective-permute-start.4 = (bf16[384,1536]{1,0:T(8,128)(2,1)S(1)}, bf16[384,1536]{1,0:T(8,128)(2,1)S(1)}, u32[]{:S(2)}, u32[]{:S(2)}) collective-permute-start(bf16[384,1536]{1,0:T(8,128)(2,1)S(1)} %collective-permute-done.3.refs_1_), channel_id=1, source_target_pairs={{0,1},{1,0},{2,3},{3,2},{4,5},{5,4},{6,7},{7,6},{8,9},{9,8},{10,11... | collective-permute-start | bytes 3538952 | tf_op jit(solution)/shard_map/ppermute | solution.py:384
  32.4 12.0 %collective-permute-start.12 = (bf16[256,1536]{1,0:T(8,128)(2,1)S(1)}, bf16[256,1536]{1,0:T(8,128)(2,1)S(1)}, u32[]{:S(2)}, u32[]{:S(2)}) collective-permute-start(bf16[256,1536]{1,0:T(8,128)(2,1)S(1)} %collective-permute-done.10.refs_8_), channel_id=1, source_target_pairs={{0,2},{1,5},{2,0},{3,7},{4,6},{5,1},{6,4},{7,3},{8,10},{9,13},{10,... | collective-permute-start | bytes 2359304 | tf_op jit(solution)/shard_map/ppermute | solution.py:387
  33.9 12.4 %collective-permute-start.6 = (bf16[384,1536]{1,0:T(8,128)(2,1)S(1)}, bf16[384,1536]{1,0:T(8,128)(2,1)S(1)}, u32[]{:S(2)}, u32[]{:S(2)}) collective-permute-start(bf16[384,1536]{1,0:T(8,128)(2,1)S(1)} %collective-permute-done.5.refs_3_), channel_id=1, source_target_pairs={{0,1},{1,0},{2,3},{3,2},{4,5},{5,4},{6,7},{7,6},{8,9},{9,8},{10,11... | collective-permute-start | bytes 3538952 | tf_op jit(solution)/shard_map/ppermute | solution.py:384
  37.1 11.2 %collective-permute-start.11 = (bf16[256,1536]{1,0:T(8,128)(2,1)S(1)}, bf16[256,1536]{1,0:T(8,128)(2,1)S(1)}, u32[]{:S(2)}, u32[]{:S(2)}) collective-permute-start(bf16[256,1536]{1,0:T(8,128)(2,1)S(1)} %collective-permute-done.9.refs_7_), channel_id=1, source_target_pairs={{0,1},{1,0},{2,3},{3,2},{4,5},{5,4},{6,7},{7,6},{8,9},{9,8},{10,11... | collective-permute-start | bytes 2359304 | tf_op jit(solution)/shard_map/ppermute | solution.py:384
  37.1 8.3 %collective-permute-start.15 = (bf16[384,512]{1,0:T(8,128)(2,1)S(1)}, bf16[384,512]{1,0:T(8,128)(2,1)S(1)}, u32[]{:S(2)}, u32[]{:S(2)}) collective-permute-start(bf16[384,512]{1,0:T(8,128)(2,1)S(1)} %slice.26), channel_id=1, source_target_pairs={{16,24},{9,1},{18,26},{11,3},{20,28},{13,5},{22,30},{15,7}} | collective-permute-start | bytes 1179656 | tf_op jit(solution)/shard_map/ppermute | solution.py:400
  44.5 8.4 %collective-permute-start.17 = (bf16[384,1024]{1,0:T(8,128)(2,1)S(1)}, bf16[384,1024]{1,0:T(8,128)(2,1)S(1)}, u32[]{:S(2)}, u32[]{:S(2)}) collective-permute-start(bf16[384,1024]{1,0:T(8,128)(2,1)S(1)} %slice.27), channel_id=1, source_target_pairs={{16,24},{9,1},{18,26},{11,3},{20,28},{13,5},{22,30},{15,7}} | collective-permute-start | bytes 2359304 | tf_op jit(solution)/shard_map/ppermute | solution.py:400
  45.2 3.1 %collective-permute-start.13 = (bf16[192,1536]{1,0:T(8,128)(2,1)S(1)}, bf16[192,1536]{1,0:T(8,128)(2,1)S(1)}, u32[]{:S(2)}, u32[]{:S(2)}) collective-permute-start(bf16[192,1536]{1,0:T(8,128)(2,1)S(1)} %slice.24), channel_id=1, source_target_pairs={{0,1},{1,0},{2,3},{3,2},{4,5},{5,4},{6,7},{7,6},{8,9},{9,8},{10,11... | collective-permute-start | bytes 1769480 | tf_op jit(solution)/shard_map/ppermute | solution.py:384
  45.4 5.5 %collective-permute-start.16 = (bf16[384,512]{1,0:T(8,128)(2,1)S(1)}, bf16[384,512]{1,0:T(8,128)(2,1)S(1)}, u32[]{:S(2)}, u32[]{:S(2)}) collective-permute-start(bf16[384,512]{1,0:T(8,128)(2,1)S(1)} %collective-permute-done.15.refs_3_), channel_id=1, source_target_pairs={{0,1},{1,0},{2,3},{3,2},{4,5},{5,4},{6,7},{7,6},{8,9},{9,8},{10,11... | collective-permute-start | bytes 1179656 | tf_op jit(solution)/shard_map/ppermute | solution.py:384
  51.3 8.1 %collective-permute-start.24 = (bf16[256,512]{1,0:T(8,128)(2,1)S(1)}, bf16[256,512]{1,0:T(8,128)(2,1)S(1)}, u32[]{:S(2)}, u32[]{:S(2)}) collective-permute-start(bf16[256,512]{1,0:T(8,128)(2,1)S(1)} %get-tuple-element.28.a_ref), channel_id=1, source_target_pairs={{0,2},{1,5},{2,0},{3,7},{4,6},{5,1},{6,4},{7,3},{8,10},{9,13},{10,... | collective-permute-start | bytes 786440 | tf_op jit(solution)/shard_map/ppermute | solution.py:387
  53.0 7.8 %collective-permute-start.18 = (bf16[384,512]{1,0:T(8,128)(2,1)S(1)}, bf16[384,512]{1,0:T(8,128)(2,1)S(1)}, u32[]{:S(2)}, u32[]{:S(2)}) collective-permute-start(bf16[384,512]{1,0:T(8,128)(2,1)S(1)} %get-tuple-element.38), channel_id=1, source_target_pairs={{0,1},{1,0},{2,3},{3,2},{4,5},{5,4},{6,7},{7,6},{8,9},{9,8},{10,11... | collective-permute-start | bytes 1179656 | tf_op jit(solution)/shard_map/ppermute | solution.py:384
  59.5 2.8 %collective-permute-start.25 = (bf16[256,512]{1,0:T(8,128)(2,1)S(1)}, bf16[256,512]{1,0:T(8,128)(2,1)S(1)}, u32[]{:S(2)}, u32[]{:S(2)}) collective-permute-start(bf16[256,512]{1,0:T(8,128)(2,1)S(1)} %collective-permute-done.24.a_ref), channel_id=1, source_target_pairs={{0,1},{1,0},{2,3},{3,2},{4,5},{5,4},{6,7},{7,6},{8,9},{9,8},{10,11... | collective-permute-start | bytes 786440 | tf_op jit(solution)/shard_map/ppermute | solution.py:384
  62.2 12.8 %collective-permute-start.26 = (bf16[256,1152]{1,0:T(8,128)(2,1)S(1)}, bf16[256,1152]{1,0:T(8,128)(2,1)S(1)}, u32[]{:S(2)}, u32[]{:S(2)}) collective-permute-start(bf16[256,1152]{1,0:T(8,128)(2,1)S(1)} %get-tuple-element.32.b_ref), channel_id=1, source_target_pairs={{0,2},{1,5},{2,0},{3,7},{4,6},{5,1},{6,4},{7,3},{8,10},{9,13},{10,... | collective-permute-start | bytes 1769480 | tf_op jit(solution)/shard_map/ppermute | solution.py:387
  62.8 2.3 %collective-permute-start.20 = (bf16[256,512]{1,0:T(8,128)(2,1)S(1)}, bf16[256,512]{1,0:T(8,128)(2,1)S(1)}, u32[]{:S(2)}, u32[]{:S(2)}) collective-permute-start(bf16[256,512]{1,0:T(8,128)(2,1)S(1)} %get-tuple-element.28.a_ref), channel_id=1, source_target_pairs={{0,1},{1,0},{2,3},{3,2},{4,5},{5,4},{6,7},{7,6},{8,9},{9,8},{10,11... | collective-permute-start | bytes 786440 | tf_op jit(solution)/shard_map/ppermute | solution.py:384
  65.1 9.9 %collective-permute-start.21 = (bf16[256,512]{1,0:T(8,128)(2,1)S(1)}, bf16[256,512]{1,0:T(8,128)(2,1)S(1)}, u32[]{:S(2)}, u32[]{:S(2)}) collective-permute-start(bf16[256,512]{1,0:T(8,128)(2,1)S(1)} %collective-permute-done.20), channel_id=1, source_target_pairs={{0,2},{1,5},{2,0},{3,7},{4,6},{5,1},{6,4},{7,3},{8,10},{9,13},{10,... | collective-permute-start | bytes 786440 | tf_op jit(solution)/shard_map/ppermute | solution.py:387
  65.9 9.1 %collective-permute-start.22 = (bf16[256,1152]{1,0:T(8,128)(2,1)S(1)}, bf16[256,1152]{1,0:T(8,128)(2,1)S(1)}, u32[]{:S(2)}, u32[]{:S(2)}) collective-permute-start(bf16[256,1152]{1,0:T(8,128)(2,1)S(1)} %get-tuple-element.32.b_ref), channel_id=1, source_target_pairs={{0,1},{1,0},{2,3},{3,2},{4,5},{5,4},{6,7},{7,6},{8,9},{9,8},{10,11... | collective-permute-start | bytes 1769480 | tf_op jit(solution)/shard_map/ppermute | solution.py:384
  75.0 9.9 %collective-permute-start.23 = (bf16[256,1152]{1,0:T(8,128)(2,1)S(1)}, bf16[256,1152]{1,0:T(8,128)(2,1)S(1)}, u32[]{:S(2)}, u32[]{:S(2)}) collective-permute-start(bf16[256,1152]{1,0:T(8,128)(2,1)S(1)} %collective-permute-done.22), channel_id=1, source_target_pairs={{0,2},{1,5},{2,0},{3,7},{4,6},{5,1},{6,4},{7,3},{8,10},{9,13},{10,... | collective-permute-start | bytes 1769480 | tf_op jit(solution)/shard_map/ppermute | solution.py:387
  77.0 14.3 %collective-permute-start.31 = (bf16[256,1152]{1,0:T(8,128)(2,1)S(1)}, bf16[256,1152]{1,0:T(8,128)(2,1)S(1)}, u32[]{:S(2)}, u32[]{:S(2)}) collective-permute-start(bf16[256,1152]{1,0:T(8,128)(2,1)S(1)} %collective-permute-done.30), channel_id=1, source_target_pairs={{0,2},{1,5},{2,0},{3,7},{4,6},{5,1},{6,4},{7,3},{8,10},{9,13},{10,... | collective-permute-start | bytes 1769480 | tf_op jit(solution)/shard_map/ppermute | solution.py:387
  77.5 16.6 %collective-permute-start.29 = (bf16[256,512]{1,0:T(8,128)(2,1)S(1)}, bf16[256,512]{1,0:T(8,128)(2,1)S(1)}, u32[]{:S(2)}, u32[]{:S(2)}) collective-permute-start(bf16[256,512]{1,0:T(8,128)(2,1)S(1)} %collective-permute-done.25), channel_id=1, source_target_pairs={{0,2},{1,5},{2,0},{3,7},{4,6},{5,1},{6,4},{7,3},{8,10},{9,13},{10,... | collective-permute-start | bytes 786440 | tf_op jit(solution)/shard_map/ppermute | solution.py:387
  84.5 18.2 %collective-permute-start.33 = (bf16[256,1536]{1,0:T(8,128)(2,1)S(1)}, bf16[256,1536]{1,0:T(8,128)(2,1)S(1)}, u32[]{:S(2)}, u32[]{:S(2)}) collective-permute-start(bf16[256,1536]{1,0:T(8,128)(2,1)S(1)} %experts.5), channel_id=1, source_target_pairs={{0,1},{1,0},{2,3},{3,2},{4,5},{5,4},{6,7},{7,6},{8,9},{9,8},{10,11... | collective-permute-start | bytes 2359304 | tf_op jit(solution)/shard_map/ppermute | solution.py:384
  90.6 12.1 %collective-permute-start.27 = (bf16[256,1536]{1,0:T(8,128)(2,1)S(1)}, bf16[256,1536]{1,0:T(8,128)(2,1)S(1)}, u32[]{:S(2)}, u32[]{:S(2)}) collective-permute-start(bf16[256,1536]{1,0:T(8,128)(2,1)S(1)} %experts.6), channel_id=1, source_target_pairs={{0,2},{1,5},{2,0},{3,7},{4,6},{5,1},{6,4},{7,3},{8,10},{9,13},{10,... | collective-permute-start | bytes 2359304 | tf_op jit(solution)/shard_map/ppermute | solution.py:387
  99.5 12.1 %collective-permute-start.32 = (bf16[256,1536]{1,0:T(8,128)(2,1)S(1)}, bf16[256,1536]{1,0:T(8,128)(2,1)S(1)}, u32[]{:S(2)}, u32[]{:S(2)}) collective-permute-start(bf16[256,1536]{1,0:T(8,128)(2,1)S(1)} %experts.7), channel_id=1, source_target_pairs={{0,2},{1,5},{2,0},{3,7},{4,6},{5,1},{6,4},{7,3},{8,10},{9,13},{10,... | collective-permute-start | bytes 2359304 | tf_op jit(solution)/shard_map/ppermute | solution.py:387
  102.7 9.2 %collective-permute-start.28 = (bf16[256,1536]{1,0:T(8,128)(2,1)S(1)}, bf16[256,1536]{1,0:T(8,128)(2,1)S(1)}, u32[]{:S(2)}, u32[]{:S(2)}) collective-permute-start(bf16[256,1536]{1,0:T(8,128)(2,1)S(1)} %collective-permute-done.27), channel_id=1, source_target_pairs={{0,1},{1,0},{2,3},{3,2},{4,5},{5,4},{6,7},{7,6},{8,9},{9,8},{10,11... | collective-permute-start | bytes 2359304 | tf_op jit(solution)/shard_map/ppermute | solution.py:384
  111.8 11.5 %collective-permute-start.34 = (bf16[256,1536]{1,0:T(8,128)(2,1)S(1)}, bf16[256,1536]{1,0:T(8,128)(2,1)S(1)}, u32[]{:S(2)}, u32[]{:S(2)}) collective-permute-start(bf16[256,1536]{1,0:T(8,128)(2,1)S(1)} %add_convert_fusion), channel_id=1, source_target_pairs={{0,5},{1,2},{2,7},{3,0},{4,1},{5,6},{6,3},{7,4},{8,13},{9,10},{10,... | collective-permute-start | bytes 2359304 | tf_op jit(solution)/shard_map/ppermute | solution.py:390
  (16 other events, 105.4 us)

commit v5 on v4

--- a/solution.py
+++ b/solution.py
@@ -314,15 +314,15 @@
         total = hidden[...]
         for p in parts:
             total = total + p[:, at:to].astype(F32)
-        out_ref[:, at:to] = total.astype(BF16)
+        out_ref[:, at:to] = total.astype(out_ref.dtype)
         at = to
 
 
-def finish(left, right, parts):
+def finish(left, right, parts, kind=BF16):
     return call(
         finish_kernel,
         "finish",
-        jax.ShapeDtypeStruct(parts[0].shape, BF16),
+        jax.ShapeDtypeStruct(parts[0].shape, kind),
         [VMEM] * (2 + len(parts)),
         VMEM,
         [],
@@ -425,9 +425,10 @@
     pair_weights.append(beside(weights[2]))
     context = attend_next(2, context, pair_weights[2])
     context = attend_next(3, context)
-    p2 = across(after(p0_other, p1, context))
+    p2 = across(after(p0_other, p1))
     p1_other = beside(p1)
     z1_other, z2_other = beside(z1), beside(z2)
+    z2_other = beside(after(z2, context))
     z3 = [along(z2[:, :cut], 3), along(z2[:, cut:], 3)]
     few = held * 3 // 4
     owners = [
@@ -475,7 +476,8 @@
     far_sum = across(r_far).astype(F32) + ready.astype(F32)
     back1 = beside(back)
     back0 = turned(far_sum.astype(BF16))
-    return finish(hidden0, hidden1, [home, back1, back0])
+    rest = finish(hidden0, hidden1, [home, back1], F32)
+    return (rest + back0.astype(F32)).astype(BF16)
 
 
 def solution(mesh):

time: 125 us -> 125 us (level)
  starting transfers between devices: 32.7 us -> 28.3 us
  waiting for transfers between devices: 47.4 us -> 51.7 us
    ppermute x11, waiting for transfers between devices: 24.8 us -> 30.2 us  [across(): lax.ppermute(a, 'expert', [(e, e ^ (4 if e & 1 else 2)) for e in range(n_...]
    ppermute x19, starting transfers between devices: 14 us -> 10.4 us  [beside(): return lax.ppermute(a, 'expert', [(e, e ^ 1) for e in range(n_ex)])]
  transfers between devices with their start and end apart: 35 -> 35, of which waited for: 12 -> 14; matrix products, arithmetic and copies ran while one was open for 1% -> 1% of each run, Pallas kernels for 33% -> 33%
where the time goes in v5:
time: 125 us; the launch traced here: 124 us
  waiting for transfers between devices  51.7 us (41%)
  Pallas kernels  41.3 us (33%)
  starting transfers between devices  28.3 us (23%)
  other arithmetic  2.47 us (2%)
    ppermute x11, waiting for transfers between devices, across(): lax.ppermute(a, 'expert', [(e, e ^ (4 if e & 1 else 2)) for e in range(n_...  30.2 us
    pallas_call x4, Pallas kernels, run_experts(): call(functools.partial(experts_kernel, groups, spread), 'experts', jax.Sh...  21.9 us
    pallas_call x4, Pallas kernels, attend(): pl.pallas_call(attend_kernel, name='attend', grid=(pairs,), out_shape=jax...  13.3 us
    ppermute x1, waiting for transfers between devices, turned(): lax.ppermute(a, 'expert', [(e, e ^ (3 if e & 1 else 5)) for e in range(n_...  11.1 us
    ppermute x11, starting transfers between devices, across(): lax.ppermute(a, 'expert', [(e, e ^ (4 if e & 1 else 2)) for e in range(n_...  10.9 us
    ppermute x19, starting transfers between devices, beside(): return lax.ppermute(a, 'expert', [(e, e ^ 1) for e in range(n_ex)])  10.4 us
    ppermute x4, waiting for transfers between devices, along(): return lax.ppermute(a, ('dp', 'expert'), sent)  7.41 us
    ppermute x4, starting transfers between devices, along(): return lax.ppermute(a, ('dp', 'expert'), sent)  6.86 us
  transfers between devices with their start and end apart: 35, of which 14 were waited for; matrix products, arithmetic and copies ran while one was open for 1% of the time, Pallas kernels for 33%

profile of v5, /device:TPU:0, one launch (start us, length us, event | category | flops | bytes accessed | tf_op | source)
XLA Modules:
  0.0 124.5 jit_solution(3240165926432768984)
XLA Ops:
  1.0 4.6 %collective-permute-start.3 = (bf16[384,1536]{1,0:T(8,128)(2,1)}, bf16[384,1536]{1,0:T(8,128)(2,1)S(1)}, u32[]{:S(2)}, u32[]{:S(2)}) collective-permute-start(bf16[384,1536]{1,0:T(8,128)(2,1)} %refs_0_.6), channel_id=1, source_target_pairs={{0,8},{8,16},{16,24},{9,1},{17,9},{25,17},{2,10},{10,18},{18,26},{... | collective-permute-start | bytes 3538952 | tf_op jit(solution)/shard_map/ppermute | solution.py:400
  5.7 1.2 pad_maximum_fusion
  7.0 1.9 %collective-permute-start.8 = (bf16[256,1536]{1,0:T(8,128)(2,1)S(1)}, bf16[256,1536]{1,0:T(8,128)(2,1)S(1)}, u32[]{:S(2)}, u32[]{:S(2)}) collective-permute-start(bf16[256,1536]{1,0:T(8,128)(2,1)S(1)} %bitcast.5), channel_id=1, source_target_pairs={{0,2},{1,5},{2,0},{3,7},{4,6},{5,1},{6,4},{7,3},{8,10},{9,13},{10,... | collective-permute-start | bytes 2359304 | tf_op jit(solution)/shard_map/ppermute | solution.py:387
  8.9 3.3 %attend.4.refs_0_ = bf16[256,1536]{1,0:T(8,128)(2,1)S(1)} custom-call(s32[1,4]{1,0:T(1,128)S(1)} %copy-done.7, bf16[256,1536]{1,0:T(8,128)(2,1)S(1)} %copy-done.8, bf16[256,512]{1,0:T(8,128)(2,1)S(1)} %copy-done.9, bf16[256,512]{1,0:T(8,128)(2,1)S(1)} %copy-done.10), custom_call_target="tpu_custom_call" | custom-call | flops 1000000000 | bytes 1024 | tf_op jit(solution)/shard_map/attend/pallas_call | solution.py:72
  12.2 7.4 %collective-permute-done.3.refs_1_ = bf16[384,1536]{1,0:T(8,128)(2,1)S(1)} collective-permute-done((bf16[384,1536]{1,0:T(8,128)(2,1)}, bf16[384,1536]{1,0:T(8,128)(2,1)S(1)}, u32[]{:S(2)}, u32[]{:S(2)}) %collective-permute-start.3) | collective-permute-done | bytes 1179680 | tf_op jit(solution)/shard_map/ppermute | solution.py:400
  20.4 1.6 %collective-permute-start.9 = (bf16[256,1536]{1,0:T(8,128)(2,1)S(1)}, bf16[256,1536]{1,0:T(8,128)(2,1)S(1)}, u32[]{:S(2)}, u32[]{:S(2)}) collective-permute-start(bf16[256,1536]{1,0:T(8,128)(2,1)S(1)} %collective-permute-done.7.refs_5_), channel_id=1, source_target_pairs={{0,2},{1,5},{2,0},{3,7},{4,6},{5,1},{6,4},{7,3},{8,10},{9,13},{10,... | collective-permute-start | bytes 2359304 | tf_op jit(solution)/shard_map/ppermute | solution.py:387
  22.4 3.3 %attend.5.refs_0_ = bf16[256,1536]{1,0:T(8,128)(2,1)S(1)} custom-call(s32[1,4]{1,0:T(1,128)S(1)} %copy-done.7, bf16[256,1536]{1,0:T(8,128)(2,1)S(1)} %copy-done.8, bf16[256,512]{1,0:T(8,128)(2,1)S(1)} %copy-done.9, bf16[256,512]{1,0:T(8,128)(2,1)S(1)} %copy-done.10, bf16[256,1536]{1,0:T(8,128)(2,1)S(1)} %attend.4.refs_0_), custom_call_target="tpu_custom_call", output_to_operand_aliasing={{}: (4, {})} | custom-call | flops 1000000000 | bytes 1024 | tf_op jit(solution)/shard_map/attend/pallas_call | solution.py:72
  25.8 3.3 %attend.6.refs_0_ = bf16[256,1536]{1,0:T(8,128)(2,1)S(1)} custom-call(s32[1,4]{1,0:T(1,128)S(1)} %copy-done.7, bf16[256,1536]{1,0:T(8,128)(2,1)S(1)} %copy-done.8, bf16[256,512]{1,0:T(8,128)(2,1)S(1)} %copy-done.9, bf16[256,512]{1,0:T(8,128)(2,1)S(1)} %copy-done.10, bf16[256,1536]{1,0:T(8,128)(2,1)S(1)} %attend.5.refs_0_), custom_call_target="tpu_custom_call", output_to_operand_aliasing={{}: (4, {})} | custom-call | flops 1000000000 | bytes 1024 | tf_op jit(solution)/shard_map/attend/pallas_call | solution.py:72
  29.1 3.3 %collective-permute-done.9.refs_7_ = bf16[256,1536]{1,0:T(8,128)(2,1)S(1)} collective-permute-done((bf16[256,1536]{1,0:T(8,128)(2,1)S(1)}, bf16[256,1536]{1,0:T(8,128)(2,1)S(1)}, u32[]{:S(2)}, u32[]{:S(2)}) %collective-permute-start.9) | collective-permute-done | bytes 786464 | tf_op jit(solution)/shard_map/ppermute | solution.py:387
  32.4 1.5 %collective-permute-start.12 = (bf16[256,1536]{1,0:T(8,128)(2,1)S(1)}, bf16[256,1536]{1,0:T(8,128)(2,1)S(1)}, u32[]{:S(2)}, u32[]{:S(2)}) collective-permute-start(bf16[256,1536]{1,0:T(8,128)(2,1)S(1)} %collective-permute-done.10.refs_8_), channel_id=1, source_target_pairs={{0,2},{1,5},{2,0},{3,7},{4,6},{5,1},{6,4},{7,3},{8,10},{9,13},{10,... | collective-permute-start | bytes 2359304 | tf_op jit(solution)/shard_map/ppermute | solution.py:387
  33.9 3.3 %attend.7.ctx_ref.refs_2_.refs_1_ = bf16[256,1536]{1,0:T(8,128)(2,1)S(1)} custom-call(s32[1,4]{1,0:T(1,128)S(1)} %copy-done.7, bf16[256,1536]{1,0:T(8,128)(2,1)S(1)} %copy-done.8, bf16[256,512]{1,0:T(8,128)(2,1)S(1)} %copy-done.9, bf16[256,512]{1,0:T(8,128)(2,1)S(1)} %copy-done.10, bf16[256,1536]{1,0:T(8,128)(2,1)S(1)} %attend.6.refs_0_), custom_call_target="tpu_custom_call", output_to_operand_aliasing={{}: (4, {})} | custom-call | flops 1000000000 | bytes 1024 | tf_op jit(solution)/shard_map/attend/pallas_call | solution.py:72
  38.8 5.6 %collective-permute-done.12.refs_10_ = bf16[256,1536]{1,0:T(8,128)(2,1)S(1)} collective-permute-done((bf16[256,1536]{1,0:T(8,128)(2,1)S(1)}, bf16[256,1536]{1,0:T(8,128)(2,1)S(1)}, u32[]{:S(2)}, u32[]{:S(2)}) %collective-permute-start.12) | collective-permute-done | bytes 786464 | tf_op jit(solution)/shard_map/ppermute | solution.py:387
  45.3 4.2 %collective-permute-start.16 = (bf16[384,512]{1,0:T(8,128)(2,1)S(1)}, bf16[384,512]{1,0:T(8,128)(2,1)S(1)}, u32[]{:S(2)}, u32[]{:S(2)}) collective-permute-start(bf16[384,512]{1,0:T(8,128)(2,1)S(1)} %collective-permute-done.15.refs_3_), channel_id=1, source_target_pairs={{0,1},{1,0},{2,3},{3,2},{4,5},{5,4},{6,7},{7,6},{8,9},{9,8},{10,11... | collective-permute-start | bytes 1179656 | tf_op jit(solution)/shard_map/ppermute | solution.py:384
  49.6 1.8 %project.1.refs_3_ = f32[256,1536]{1,0:T(8,128)S(1)} custom-call(bf16[256,1536]{1,0:T(8,128)(2,1)S(1)} %attend.7.ctx_ref.refs_2_.refs_1_, bf16[256,1536]{1,0:T(8,128)(2,1)S(1)} %copy-done.4, bf16[384,1536]{1,0:T(8,128)(2,1)S(1)} %copy-done.3, bf16[384,1536]{1,0:T(8,128)(2,1)S(1)} %collective-permute-done.3.refs_1_, ...), custom_call_target="tpu_custom_call" | custom-call | flops 1000000000 | bytes 1024 | tf_op jit(solution)/shard_map/project/pallas_call | solution.py:182
  51.5 2.6 %adapt.1.refs_0_ = f32[256,1536]{1,0:T(8,128)S(1)} custom-call(s32[4]{0:T(128)S(1)} %copy-done.6, s32[1,4]{1,0:T(1,128)S(1)} %copy-done.7, bf16[256,1536]{1,0:T(8,128)(2,1)S(1)} %attend.7.ctx_ref.refs_2_.refs_1_, f32[256,1536]{1,0:T(8,128)S(1)} %project.1.refs_3_, bf16[256,1536]{1,0:T(8,128)(2,1)S(1)} %bitcast.6, ...), custom_call_target="tpu_custom_call" | custom-call | flops 1000000000 | bytes 1024 | tf_op jit(solution)/shard_map/adapt/pallas_call | solution.py:196
  55.1 2.8 %collective-permute-start.18 = (bf16[384,512]{1,0:T(8,128)(2,1)S(1)}, bf16[384,512]{1,0:T(8,128)(2,1)S(1)}, u32[]{:S(2)}, u32[]{:S(2)}) collective-permute-start(bf16[384,512]{1,0:T(8,128)(2,1)S(1)} %get-tuple-element.40), channel_id=1, source_target_pairs={{0,1},{1,0},{2,3},{3,2},{4,5},{5,4},{6,7},{7,6},{8,9},{9,8},{10,11... | collective-permute-start | bytes 1179656 | tf_op jit(solution)/shard_map/ppermute | solution.py:384
  58.1 2.8 %collective-permute-done.24.a_ref = bf16[256,512]{1,0:T(8,128)(2,1)S(1)} collective-permute-done((bf16[256,512]{1,0:T(8,128)(2,1)S(1)}, bf16[256,512]{1,0:T(8,128)(2,1)S(1)}, u32[]{:S(2)}, u32[]{:S(2)}) %collective-permute-start.24) | collective-permute-done | bytes 262176 | tf_op jit(solution)/shard_map/ppermute | solution.py:387
  61.1 0.9 close.3
  63.9 1.2 collective-permute-done.20
  65.1 1.0 collective-permute-start.21
  66.0 5.4 %experts.4.refs_0_ = bf16[256,1536]{1,0:T(8,128)(2,1)S(1)} custom-call(bf16[256,512]{1,0:T(8,128)(2,1)S(1)} %get-tuple-element.30.a_ref, bf16[256,1152]{1,0:T(8,128)(2,1)S(1)} %get-tuple-element.34.b_ref, bf16[2,1536,512]{2,1,0:T(8,128)(2,1)S(1)} %copy-done, bf16[2,1536,512]{2,1,0:T(8,128)(2,1)S(1)} %copy-done.1, bf16[2,512,1536]{2,1,0:T(8,128)(2,1)S(1)} %copy-done.2, ...), custom_call_target="tpu_custom_call" | custom-call | flops 1000000000 | bytes 1024 | tf_op jit(solution)/shard_map/experts/pallas_call | solution.py:297
  71.5 3.7 %collective-permute-done.21.a_ref = bf16[256,512]{1,0:T(8,128)(2,1)S(1)} collective-permute-done((bf16[256,512]{1,0:T(8,128)(2,1)S(1)}, bf16[256,512]{1,0:T(8,128)(2,1)S(1)}, u32[]{:S(2)}, u32[]{:S(2)}) %collective-permute-start.21) | collective-permute-done | bytes 262176 | tf_op jit(solution)/shard_map/ppermute | solution.py:387
  75.8 1.4 %collective-permute-done.30 = bf16[256,1152]{1,0:T(8,128)(2,1)S(1)} collective-permute-done((bf16[256,1152]{1,0:T(8,128)(2,1)S(1)}, bf16[256,1152]{1,0:T(8,128)(2,1)S(1)}, u32[]{:S(2)}, u32[]{:S(2)}) %collective-permute-start.30) | collective-permute-done | bytes 589856 | tf_op jit(solution)/shard_map/ppermute | solution.py:384
  77.7 1.5 %collective-permute-start.29 = (bf16[256,512]{1,0:T(8,128)(2,1)S(1)}, bf16[256,512]{1,0:T(8,128)(2,1)S(1)}, u32[]{:S(2)}, u32[]{:S(2)}) collective-permute-start(bf16[256,512]{1,0:T(8,128)(2,1)S(1)} %collective-permute-done.25), channel_id=1, source_target_pairs={{0,2},{1,5},{2,0},{3,7},{4,6},{5,1},{6,4},{7,3},{8,10},{9,13},{10,... | collective-permute-start | bytes 786440 | tf_op jit(solution)/shard_map/ppermute | solution.py:387
  79.2 5.4 %experts.5 = bf16[256,1536]{1,0:T(8,128)(2,1)S(1)} custom-call(bf16[256,512]{1,0:T(8,128)(2,1)S(1)} %collective-permute-done.24.a_ref, bf16[256,1152]{1,0:T(8,128)(2,1)S(1)} %collective-permute-done.26.b_ref, bf16[2,1536,512]{2,1,0:T(8,128)(2,1)S(1)} %copy-done, bf16[2,1536,512]{2,1,0:T(8,128)(2,1)S(1)} %copy-done.1, bf16[2,512,1536]{2,1,0:T(8,128)(2,1)S(1)} %copy-done.2, ...), custom_call_target="tpu_custom_call" | custom-call | flops 1000000000 | bytes 1024 | tf_op jit(solution)/shard_map/experts/pallas_call | solution.py:297
  85.1 5.6 %experts.6 = bf16[256,1536]{1,0:T(8,128)(2,1)S(1)} custom-call(bf16[256,512]{1,0:T(8,128)(2,1)S(1)} %collective-permute-done.21.a_ref, bf16[256,1152]{1,0:T(8,128)(2,1)S(1)} %collective-permute-done.23.b_ref, bf16[2,1536,512]{2,1,0:T(8,128)(2,1)S(1)} %copy-done, bf16[2,1536,512]{2,1,0:T(8,128)(2,1)S(1)} %copy-done.1, bf16[2,512,1536]{2,1,0:T(8,128)(2,1)S(1)} %copy-done.2, ...), custom_call_target="tpu_custom_call" | custom-call | flops 1000000000 | bytes 1024 | tf_op jit(solution)/shard_map/experts/pallas_call | solution.py:297
  91.4 2.8 %collective-permute-done.29.a_ref = bf16[256,512]{1,0:T(8,128)(2,1)S(1)} collective-permute-done((bf16[256,512]{1,0:T(8,128)(2,1)S(1)}, bf16[256,512]{1,0:T(8,128)(2,1)S(1)}, u32[]{:S(2)}, u32[]{:S(2)}) %collective-permute-start.29) | collective-permute-done | bytes 262176 | tf_op jit(solution)/shard_map/ppermute | solution.py:387
  94.2 5.4 %experts.7 = bf16[256,1536]{1,0:T(8,128)(2,1)S(1)} custom-call(bf16[256,512]{1,0:T(8,128)(2,1)S(1)} %collective-permute-done.29.a_ref, bf16[256,1152]{1,0:T(8,128)(2,1)S(1)} %collective-permute-done.31.b_ref, bf16[2,1536,512]{2,1,0:T(8,128)(2,1)S(1)} %copy-done, bf16[2,1536,512]{2,1,0:T(8,128)(2,1)S(1)} %copy-done.1, bf16[2,512,1536]{2,1,0:T(8,128)(2,1)S(1)} %copy-done.2, ...), custom_call_target="tpu_custom_call" | custom-call | flops 1000000000 | bytes 1024 | tf_op jit(solution)/shard_map/experts/pallas_call | solution.py:297
  100.3 2.5 %collective-permute-done.27 = bf16[256,1536]{1,0:T(8,128)(2,1)S(1)} collective-permute-done((bf16[256,1536]{1,0:T(8,128)(2,1)S(1)}, bf16[256,1536]{1,0:T(8,128)(2,1)S(1)}, u32[]{:S(2)}, u32[]{:S(2)}) %collective-permute-start.27) | collective-permute-done | bytes 786464 | tf_op jit(solution)/shard_map/ppermute | solution.py:387
  102.8 8.9 %collective-permute-done.32 = bf16[256,1536]{1,0:T(8,128)(2,1)S(1)} collective-permute-done((bf16[256,1536]{1,0:T(8,128)(2,1)S(1)}, bf16[256,1536]{1,0:T(8,128)(2,1)S(1)}, u32[]{:S(2)}, u32[]{:S(2)}) %collective-permute-start.32) | collective-permute-done | bytes 786464 | tf_op jit(solution)/shard_map/ppermute | solution.py:387
  112.3 11.1 %collective-permute-done.34 = bf16[256,1536]{1,0:T(8,128)(2,1)S(1)} collective-permute-done((bf16[256,1536]{1,0:T(8,128)(2,1)S(1)}, bf16[256,1536]{1,0:T(8,128)(2,1)S(1)}, u32[]{:S(2)}, u32[]{:S(2)}) %collective-permute-start.34) | collective-permute-done | bytes 786464 | tf_op jit(solution)/shard_map/ppermute | solution.py:390
  123.4 1.1 add_convert_fusion
  (86 shorter events, 11.4 us)
Async XLA Ops:
  0.0 6.9 %collective-permute-start.2 = (bf16[2,1536,512]{2,1,0:T(8,128)(2,1)}, bf16[2,1536,512]{2,1,0:T(8,128)(2,1)S(1)}, u32[]{:S(2)}, u32[]{:S(2)}) collective-permute-start(bf16[2,1536,512]{2,1,0:T(8,128)(2,1)} %refs_0_.11), channel_id=1, source_target_pairs={{0,1},{1,0},{2,3},{3,2},{4,5},{5,4},{6,7},{7,6},{8,9},{9,8},{10,11... | collective-permute-start | bytes 9437192 | tf_op jit(solution)/shard_map/ppermute | solution.py:384
  0.5 21.8 %collective-permute-start.1 = (bf16[2,1536,512]{2,1,0:T(8,128)(2,1)}, bf16[2,1536,512]{2,1,0:T(8,128)(2,1)S(1)}, u32[]{:S(2)}, u32[]{:S(2)}) collective-permute-start(bf16[2,1536,512]{2,1,0:T(8,128)(2,1)} %refs_1_.9), channel_id=1, source_target_pairs={{0,1},{1,0},{2,3},{3,2},{4,5},{5,4},{6,7},{7,6},{8,9},{9,8},{10,11... | collective-permute-start | bytes 9437192 | tf_op jit(solution)/shard_map/ppermute | solution.py:384
  0.6 21.8 %collective-permute-start = (bf16[2,512,1536]{2,1,0:T(8,128)(2,1)}, bf16[2,512,1536]{2,1,0:T(8,128)(2,1)S(1)}, u32[]{:S(2)}, u32[]{:S(2)}) collective-permute-start(bf16[2,512,1536]{2,1,0:T(8,128)(2,1)} %refs_2_.11), channel_id=1, source_target_pairs={{0,1},{1,0},{2,3},{3,2},{4,5},{5,4},{6,7},{7,6},{8,9},{9,8},{10,11... | collective-permute-start | bytes 9437192 | tf_op jit(solution)/shard_map/ppermute | solution.py:384
  1.0 18.6 %collective-permute-start.3 = (bf16[384,1536]{1,0:T(8,128)(2,1)}, bf16[384,1536]{1,0:T(8,128)(2,1)S(1)}, u32[]{:S(2)}, u32[]{:S(2)}) collective-permute-start(bf16[384,1536]{1,0:T(8,128)(2,1)} %refs_0_.6), channel_id=1, source_target_pairs={{0,8},{8,16},{16,24},{9,1},{17,9},{25,17},{2,10},{10,18},{18,26},{... | collective-permute-start | bytes 3538952 | tf_op jit(solution)/shard_map/ppermute | solution.py:400
  6.9 13.5 %collective-permute-start.7 = (bf16[256,1536]{1,0:T(8,128)(2,1)S(1)}, bf16[256,1536]{1,0:T(8,128)(2,1)S(1)}, u32[]{:S(2)}, u32[]{:S(2)}) collective-permute-start(bf16[256,1536]{1,0:T(8,128)(2,1)S(1)} %bitcast.4), channel_id=1, source_target_pairs={{0,1},{1,0},{2,3},{3,2},{4,5},{5,4},{6,7},{7,6},{8,9},{9,8},{10,11... | collective-permute-start | bytes 2359304 | tf_op jit(solution)/shard_map/ppermute | solution.py:384
  7.0 15.0 %collective-permute-start.8 = (bf16[256,1536]{1,0:T(8,128)(2,1)S(1)}, bf16[256,1536]{1,0:T(8,128)(2,1)S(1)}, u32[]{:S(2)}, u32[]{:S(2)}) collective-permute-start(bf16[256,1536]{1,0:T(8,128)(2,1)S(1)} %bitcast.5), channel_id=1, source_target_pairs={{0,2},{1,5},{2,0},{3,7},{4,6},{5,1},{6,4},{7,3},{8,10},{9,13},{10,... | collective-permute-start | bytes 2359304 | tf_op jit(solution)/shard_map/ppermute | solution.py:387
  19.6 17.6 %collective-permute-start.5 = (bf16[384,1536]{1,0:T(8,128)(2,1)S(1)}, bf16[384,1536]{1,0:T(8,128)(2,1)S(1)}, u32[]{:S(2)}, u32[]{:S(2)}) collective-permute-start(bf16[384,1536]{1,0:T(8,128)(2,1)S(1)} %collective-permute-done.3.refs_1_), channel_id=1, source_target_pairs={{8,16},{16,24},{9,1},{17,9},{10,18},{18,26},{11,3},{19,11},{12,20}... | collective-permute-start | bytes 3538952 | tf_op jit(solution)/shard_map/ppermute | solution.py:400
  20.4 12.1 %collective-permute-start.9 = (bf16[256,1536]{1,0:T(8,128)(2,1)S(1)}, bf16[256,1536]{1,0:T(8,128)(2,1)S(1)}, u32[]{:S(2)}, u32[]{:S(2)}) collective-permute-start(bf16[256,1536]{1,0:T(8,128)(2,1)S(1)} %collective-permute-done.7.refs_5_), channel_id=1, source_target_pairs={{0,2},{1,5},{2,0},{3,7},{4,6},{5,1},{6,4},{7,3},{8,10},{9,13},{10,... | collective-permute-start | bytes 2359304 | tf_op jit(solution)/shard_map/ppermute | solution.py:387
  21.9 10.5 %collective-permute-start.10 = (bf16[256,1536]{1,0:T(8,128)(2,1)S(1)}, bf16[256,1536]{1,0:T(8,128)(2,1)S(1)}, u32[]{:S(2)}, u32[]{:S(2)}) collective-permute-start(bf16[256,1536]{1,0:T(8,128)(2,1)S(1)} %collective-permute-done.8.refs_6_), channel_id=1, source_target_pairs={{0,1},{1,0},{2,3},{3,2},{4,5},{5,4},{6,7},{7,6},{8,9},{9,8},{10,11... | collective-permute-start | bytes 2359304 | tf_op jit(solution)/shard_map/ppermute | solution.py:384
  22.3 22.9 %collective-permute-start.4 = (bf16[384,1536]{1,0:T(8,128)(2,1)S(1)}, bf16[384,1536]{1,0:T(8,128)(2,1)S(1)}, u32[]{:S(2)}, u32[]{:S(2)}) collective-permute-start(bf16[384,1536]{1,0:T(8,128)(2,1)S(1)} %collective-permute-done.3.refs_1_), channel_id=1, source_target_pairs={{0,1},{1,0},{2,3},{3,2},{4,5},{5,4},{6,7},{7,6},{8,9},{9,8},{10,11... | collective-permute-start | bytes 3538952 | tf_op jit(solution)/shard_map/ppermute | solution.py:384
  32.4 12.0 %collective-permute-start.12 = (bf16[256,1536]{1,0:T(8,128)(2,1)S(1)}, bf16[256,1536]{1,0:T(8,128)(2,1)S(1)}, u32[]{:S(2)}, u32[]{:S(2)}) collective-permute-start(bf16[256,1536]{1,0:T(8,128)(2,1)S(1)} %collective-permute-done.10.refs_8_), channel_id=1, source_target_pairs={{0,2},{1,5},{2,0},{3,7},{4,6},{5,1},{6,4},{7,3},{8,10},{9,13},{10,... | collective-permute-start | bytes 2359304 | tf_op jit(solution)/shard_map/ppermute | solution.py:387
  37.2 12.2 %collective-permute-start.6 = (bf16[384,1536]{1,0:T(8,128)(2,1)S(1)}, bf16[384,1536]{1,0:T(8,128)(2,1)S(1)}, u32[]{:S(2)}, u32[]{:S(2)}) collective-permute-start(bf16[384,1536]{1,0:T(8,128)(2,1)S(1)} %collective-permute-done.5.refs_3_), channel_id=1, source_target_pairs={{0,1},{1,0},{2,3},{3,2},{4,5},{5,4},{6,7},{7,6},{8,9},{9,8},{10,11... | collective-permute-start | bytes 3538952 | tf_op jit(solution)/shard_map/ppermute | solution.py:384
  37.3 14.1 %collective-permute-start.11 = (bf16[256,1536]{1,0:T(8,128)(2,1)S(1)}, bf16[256,1536]{1,0:T(8,128)(2,1)S(1)}, u32[]{:S(2)}, u32[]{:S(2)}) collective-permute-start(bf16[256,1536]{1,0:T(8,128)(2,1)S(1)} %collective-permute-done.9.refs_7_), channel_id=1, source_target_pairs={{0,1},{1,0},{2,3},{3,2},{4,5},{5,4},{6,7},{7,6},{8,9},{9,8},{10,11... | collective-permute-start | bytes 2359304 | tf_op jit(solution)/shard_map/ppermute | solution.py:384
  37.9 7.4 %collective-permute-start.15 = (bf16[384,512]{1,0:T(8,128)(2,1)S(1)}, bf16[384,512]{1,0:T(8,128)(2,1)S(1)}, u32[]{:S(2)}, u32[]{:S(2)}) collective-permute-start(bf16[384,512]{1,0:T(8,128)(2,1)S(1)} %slice.26), channel_id=1, source_target_pairs={{16,24},{9,1},{18,26},{11,3},{20,28},{13,5},{22,30},{15,7}} | collective-permute-start | bytes 1179656 | tf_op jit(solution)/shard_map/ppermute | solution.py:400
  44.4 10.7 %collective-permute-start.17 = (bf16[384,1024]{1,0:T(8,128)(2,1)S(1)}, bf16[384,1024]{1,0:T(8,128)(2,1)S(1)}, u32[]{:S(2)}, u32[]{:S(2)}) collective-permute-start(bf16[384,1024]{1,0:T(8,128)(2,1)S(1)} %slice.27), channel_id=1, source_target_pairs={{16,24},{9,1},{18,26},{11,3},{20,28},{13,5},{22,30},{15,7}} | collective-permute-start | bytes 2359304 | tf_op jit(solution)/shard_map/ppermute | solution.py:400
  45.2 6.3 %collective-permute-start.13 = (bf16[192,1536]{1,0:T(8,128)(2,1)S(1)}, bf16[192,1536]{1,0:T(8,128)(2,1)S(1)}, u32[]{:S(2)}, u32[]{:S(2)}) collective-permute-start(bf16[192,1536]{1,0:T(8,128)(2,1)S(1)} %slice.24), channel_id=1, source_target_pairs={{0,1},{1,0},{2,3},{3,2},{4,5},{5,4},{6,7},{7,6},{8,9},{9,8},{10,11... | collective-permute-start | bytes 1769480 | tf_op jit(solution)/shard_map/ppermute | solution.py:384
  45.3 8.8 %collective-permute-start.16 = (bf16[384,512]{1,0:T(8,128)(2,1)S(1)}, bf16[384,512]{1,0:T(8,128)(2,1)S(1)}, u32[]{:S(2)}, u32[]{:S(2)}) collective-permute-start(bf16[384,512]{1,0:T(8,128)(2,1)S(1)} %collective-permute-done.15.refs_3_), channel_id=1, source_target_pairs={{0,1},{1,0},{2,3},{3,2},{4,5},{5,4},{6,7},{7,6},{8,9},{9,8},{10,11... | collective-permute-start | bytes 1179656 | tf_op jit(solution)/shard_map/ppermute | solution.py:384
  54.5 6.4 %collective-permute-start.24 = (bf16[256,512]{1,0:T(8,128)(2,1)S(1)}, bf16[256,512]{1,0:T(8,128)(2,1)S(1)}, u32[]{:S(2)}, u32[]{:S(2)}) collective-permute-start(bf16[256,512]{1,0:T(8,128)(2,1)S(1)} %get-tuple-element.30.a_ref), channel_id=1, source_target_pairs={{0,2},{1,5},{2,0},{3,7},{4,6},{5,1},{6,4},{7,3},{8,10},{9,13},{10,... | collective-permute-start | bytes 786440 | tf_op jit(solution)/shard_map/ppermute | solution.py:387
  55.1 6.0 %collective-permute-start.18 = (bf16[384,512]{1,0:T(8,128)(2,1)S(1)}, bf16[384,512]{1,0:T(8,128)(2,1)S(1)}, u32[]{:S(2)}, u32[]{:S(2)}) collective-permute-start(bf16[384,512]{1,0:T(8,128)(2,1)S(1)} %get-tuple-element.40), channel_id=1, source_target_pairs={{0,1},{1,0},{2,3},{3,2},{4,5},{5,4},{6,7},{7,6},{8,9},{9,8},{10,11... | collective-permute-start | bytes 1179656 | tf_op jit(solution)/shard_map/ppermute | solution.py:384
  58.0 3.1 %collective-permute-start.19 = (bf16[384,512]{1,0:T(8,128)(2,1)S(1)}, bf16[384,512]{1,0:T(8,128)(2,1)S(1)}, u32[]{:S(2)}, u32[]{:S(2)}) collective-permute-start(bf16[384,512]{1,0:T(8,128)(2,1)S(1)} %get-tuple-element.39), channel_id=1, source_target_pairs={{0,1},{1,0},{2,3},{3,2},{4,5},{5,4},{6,7},{7,6},{8,9},{9,8},{10,11... | collective-permute-start | bytes 1179656 | tf_op jit(solution)/shard_map/ppermute | solution.py:384
  62.4 12.7 %collective-permute-start.26 = (bf16[256,1152]{1,0:T(8,128)(2,1)S(1)}, bf16[256,1152]{1,0:T(8,128)(2,1)S(1)}, u32[]{:S(2)}, u32[]{:S(2)}) collective-permute-start(bf16[256,1152]{1,0:T(8,128)(2,1)S(1)} %get-tuple-element.34.b_ref), channel_id=1, source_target_pairs={{0,2},{1,5},{2,0},{3,7},{4,6},{5,1},{6,4},{7,3},{8,10},{9,13},{10,... | collective-permute-start | bytes 1769480 | tf_op jit(solution)/shard_map/ppermute | solution.py:387
  63.0 2.1 %collective-permute-start.20 = (bf16[256,512]{1,0:T(8,128)(2,1)S(1)}, bf16[256,512]{1,0:T(8,128)(2,1)S(1)}, u32[]{:S(2)}, u32[]{:S(2)}) collective-permute-start(bf16[256,512]{1,0:T(8,128)(2,1)S(1)} %get-tuple-element.30.a_ref), channel_id=1, source_target_pairs={{0,1},{1,0},{2,3},{3,2},{4,5},{5,4},{6,7},{7,6},{8,9},{9,8},{10,11... | collective-permute-start | bytes 786440 | tf_op jit(solution)/shard_map/ppermute | solution.py:384
  65.1 10.1 %collective-permute-start.21 = (bf16[256,512]{1,0:T(8,128)(2,1)S(1)}, bf16[256,512]{1,0:T(8,128)(2,1)S(1)}, u32[]{:S(2)}, u32[]{:S(2)}) collective-permute-start(bf16[256,512]{1,0:T(8,128)(2,1)S(1)} %collective-permute-done.20), channel_id=1, source_target_pairs={{0,2},{1,5},{2,0},{3,7},{4,6},{5,1},{6,4},{7,3},{8,10},{9,13},{10,... | collective-permute-start | bytes 786440 | tf_op jit(solution)/shard_map/ppermute | solution.py:387
  66.0 9.1 %collective-permute-start.22 = (bf16[256,1152]{1,0:T(8,128)(2,1)S(1)}, bf16[256,1152]{1,0:T(8,128)(2,1)S(1)}, u32[]{:S(2)}, u32[]{:S(2)}) collective-permute-start(bf16[256,1152]{1,0:T(8,128)(2,1)S(1)} %get-tuple-element.34.b_ref), channel_id=1, source_target_pairs={{0,1},{1,0},{2,3},{3,2},{4,5},{5,4},{6,7},{7,6},{8,9},{9,8},{10,11... | collective-permute-start | bytes 1769480 | tf_op jit(solution)/shard_map/ppermute | solution.py:384
  75.1 9.9 %collective-permute-start.23 = (bf16[256,1152]{1,0:T(8,128)(2,1)S(1)}, bf16[256,1152]{1,0:T(8,128)(2,1)S(1)}, u32[]{:S(2)}, u32[]{:S(2)}) collective-permute-start(bf16[256,1152]{1,0:T(8,128)(2,1)S(1)} %collective-permute-done.22), channel_id=1, source_target_pairs={{0,2},{1,5},{2,0},{3,7},{4,6},{5,1},{6,4},{7,3},{8,10},{9,13},{10,... | collective-permute-start | bytes 1769480 | tf_op jit(solution)/shard_map/ppermute | solution.py:387
  77.1 14.3 %collective-permute-start.31 = (bf16[256,1152]{1,0:T(8,128)(2,1)S(1)}, bf16[256,1152]{1,0:T(8,128)(2,1)S(1)}, u32[]{:S(2)}, u32[]{:S(2)}) collective-permute-start(bf16[256,1152]{1,0:T(8,128)(2,1)S(1)} %collective-permute-done.30), channel_id=1, source_target_pairs={{0,2},{1,5},{2,0},{3,7},{4,6},{5,1},{6,4},{7,3},{8,10},{9,13},{10,... | collective-permute-start | bytes 1769480 | tf_op jit(solution)/shard_map/ppermute | solution.py:387
  77.7 16.5 %collective-permute-start.29 = (bf16[256,512]{1,0:T(8,128)(2,1)S(1)}, bf16[256,512]{1,0:T(8,128)(2,1)S(1)}, u32[]{:S(2)}, u32[]{:S(2)}) collective-permute-start(bf16[256,512]{1,0:T(8,128)(2,1)S(1)} %collective-permute-done.25), channel_id=1, source_target_pairs={{0,2},{1,5},{2,0},{3,7},{4,6},{5,1},{6,4},{7,3},{8,10},{9,13},{10,... | collective-permute-start | bytes 786440 | tf_op jit(solution)/shard_map/ppermute | solution.py:387
  84.6 18.2 %collective-permute-start.33 = (bf16[256,1536]{1,0:T(8,128)(2,1)S(1)}, bf16[256,1536]{1,0:T(8,128)(2,1)S(1)}, u32[]{:S(2)}, u32[]{:S(2)}) collective-permute-start(bf16[256,1536]{1,0:T(8,128)(2,1)S(1)} %experts.5), channel_id=1, source_target_pairs={{0,1},{1,0},{2,3},{3,2},{4,5},{5,4},{6,7},{7,6},{8,9},{9,8},{10,11... | collective-permute-start | bytes 2359304 | tf_op jit(solution)/shard_map/ppermute | solution.py:384
  90.7 12.1 %collective-permute-start.27 = (bf16[256,1536]{1,0:T(8,128)(2,1)S(1)}, bf16[256,1536]{1,0:T(8,128)(2,1)S(1)}, u32[]{:S(2)}, u32[]{:S(2)}) collective-permute-start(bf16[256,1536]{1,0:T(8,128)(2,1)S(1)} %experts.6), channel_id=1, source_target_pairs={{0,2},{1,5},{2,0},{3,7},{4,6},{5,1},{6,4},{7,3},{8,10},{9,13},{10,... | collective-permute-start | bytes 2359304 | tf_op jit(solution)/shard_map/ppermute | solution.py:387
  99.7 12.1 %collective-permute-start.32 = (bf16[256,1536]{1,0:T(8,128)(2,1)S(1)}, bf16[256,1536]{1,0:T(8,128)(2,1)S(1)}, u32[]{:S(2)}, u32[]{:S(2)}) collective-permute-start(bf16[256,1536]{1,0:T(8,128)(2,1)S(1)} %experts.7), channel_id=1, source_target_pairs={{0,2},{1,5},{2,0},{3,7},{4,6},{5,1},{6,4},{7,3},{8,10},{9,13},{10,... | collective-permute-start | bytes 2359304 | tf_op jit(solution)/shard_map/ppermute | solution.py:387
  102.8 9.3 %collective-permute-start.28 = (bf16[256,1536]{1,0:T(8,128)(2,1)S(1)}, bf16[256,1536]{1,0:T(8,128)(2,1)S(1)}, u32[]{:S(2)}, u32[]{:S(2)}) collective-permute-start(bf16[256,1536]{1,0:T(8,128)(2,1)S(1)} %collective-permute-done.27), channel_id=1, source_target_pairs={{0,1},{1,0},{2,3},{3,2},{4,5},{5,4},{6,7},{7,6},{8,9},{9,8},{10,11... | collective-permute-start | bytes 2359304 | tf_op jit(solution)/shard_map/ppermute | solution.py:384
  111.9 11.5 %collective-permute-start.34 = (bf16[256,1536]{1,0:T(8,128)(2,1)S(1)}, bf16[256,1536]{1,0:T(8,128)(2,1)S(1)}, u32[]{:S(2)}, u32[]{:S(2)}) collective-permute-start(bf16[256,1536]{1,0:T(8,128)(2,1)S(1)} %add_convert_fusion.1), channel_id=1, source_target_pairs={{0,5},{1,2},{2,7},{3,0},{4,1},{5,6},{6,3},{7,4},{8,13},{9,10},{10,... | collective-permute-start | bytes 2359304 | tf_op jit(solution)/shard_map/ppermute | solution.py:390
  (16 other events, 103.0 us)

commit v6 on v5

--- a/solution.py
+++ b/solution.py
@@ -417,7 +417,7 @@
     pair_weights = [beside(w) for w in weights[:2]]
     p0 = across(own)
     other = beside(own)
-    p1 = across(other)
+    p1 = turned(own)
     context = attend_next(0, None, pair_weights[0])
     z2 = along(after(z1, context), 2)
     p0_other = beside(after(p0, context))

time: 125 us -> 124 us (level)
  waiting for transfers between devices: 51.7 us -> 47.2 us
  starting transfers between devices: 28.3 us -> 32.4 us
    ppermute x11 -> x10, waiting for transfers between devices: 30.2 us -> 23.3 us  [across(): lax.ppermute(a, 'expert', [(e, e ^ (4 if e & 1 else 2)) for e in range(n_...]
    ppermute x1 -> x2, waiting for transfers between devices: 11.1 us -> 13.6 us  [turned(): lax.ppermute(a, 'expert', [(e, e ^ (3 if e & 1 else 5)) for e in range(n_...]
    ppermute x1 -> x2, starting transfers between devices: 0.14 us -> 1.87 us  [turned(): lax.ppermute(a, 'expert', [(e, e ^ (3 if e & 1 else 5)) for e in range(n_...]
    ppermute x11 -> x10, starting transfers between devices: 10.9 us -> 12.5 us  [across(): lax.ppermute(a, 'expert', [(e, e ^ (4 if e & 1 else 2)) for e in range(n_...]
  transfers between devices with their start and end apart: 35 -> 35, of which waited for: 14 -> 13; matrix products, arithmetic and copies ran while one was open for 1% -> 1% of each run, Pallas kernels for 33% -> 33%
where the time goes in v6:
time: 124 us
  waiting for transfers between devices  47.2 us (38%)
  Pallas kernels  41.3 us (33%)
  starting transfers between devices  32.4 us (26%)
  other arithmetic  2.47 us (2%)
    ppermute x10, waiting for transfers between devices, across(): lax.ppermute(a, 'expert', [(e, e ^ (4 if e & 1 else 2)) for e in range(n_...  23.3 us
    pallas_call x4, Pallas kernels, run_experts(): call(functools.partial(experts_kernel, groups, spread), 'experts', jax.Sh...  21.9 us
    ppermute x2, waiting for transfers between devices, turned(): lax.ppermute(a, 'expert', [(e, e ^ (3 if e & 1 else 5)) for e in range(n_...  13.6 us
    pallas_call x4, Pallas kernels, attend(): pl.pallas_call(attend_kernel, name='attend', grid=(pairs,), out_shape=jax...  13.3 us
    ppermute x10, starting transfers between devices, across(): lax.ppermute(a, 'expert', [(e, e ^ (4 if e & 1 else 2)) for e in range(n_...  12.5 us
    ppermute x19, starting transfers between devices, beside(): return lax.ppermute(a, 'expert', [(e, e ^ 1) for e in range(n_ex)])  11.2 us
    ppermute x4, waiting for transfers between devices, along(): return lax.ppermute(a, ('dp', 'expert'), sent)  7.86 us
    ppermute x4, starting transfers between devices, along(): return lax.ppermute(a, ('dp', 'expert'), sent)  6.86 us
  transfers between devices with their start and end apart: 35, of which 13 were waited for; matrix products, arithmetic and copies ran while one was open for 1% of the time, Pallas kernels for 33%

profile of v6, /device:TPU:0, one launch (start us, length us, event | category | flops | bytes accessed | tf_op | source)
XLA Modules:
  0.0 124.0 jit_solution(9046088179138474121)
XLA Ops:
  1.0 4.6 %collective-permute-start.3 = (bf16[384,1536]{1,0:T(8,128)(2,1)}, bf16[384,1536]{1,0:T(8,128)(2,1)S(1)}, u32[]{:S(2)}, u32[]{:S(2)}) collective-permute-start(bf16[384,1536]{1,0:T(8,128)(2,1)} %refs_0_.6), channel_id=1, source_target_pairs={{0,8},{8,16},{16,24},{9,1},{17,9},{25,17},{2,10},{10,18},{18,26},{... | collective-permute-start | bytes 3538952 | tf_op jit(solution)/shard_map/ppermute | solution.py:400
  5.7 1.2 pad_maximum_fusion
  6.9 1.6 %collective-permute-start.8 = (bf16[256,1536]{1,0:T(8,128)(2,1)S(1)}, bf16[256,1536]{1,0:T(8,128)(2,1)S(1)}, u32[]{:S(2)}, u32[]{:S(2)}) collective-permute-start(bf16[256,1536]{1,0:T(8,128)(2,1)S(1)} %bitcast.4), channel_id=1, source_target_pairs={{0,2},{1,5},{2,0},{3,7},{4,6},{5,1},{6,4},{7,3},{8,10},{9,13},{10,... | collective-permute-start | bytes 2359304 | tf_op jit(solution)/shard_map/ppermute | solution.py:387
  8.5 3.3 %attend.4.refs_0_ = bf16[256,1536]{1,0:T(8,128)(2,1)S(1)} custom-call(s32[1,4]{1,0:T(1,128)S(1)} %copy-done.7, bf16[256,1536]{1,0:T(8,128)(2,1)S(1)} %copy-done.8, bf16[256,512]{1,0:T(8,128)(2,1)S(1)} %copy-done.9, bf16[256,512]{1,0:T(8,128)(2,1)S(1)} %copy-done.10), custom_call_target="tpu_custom_call" | custom-call | flops 1000000000 | bytes 1024 | tf_op jit(solution)/shard_map/attend/pallas_call | solution.py:72
  11.8 7.9 %collective-permute-done.3.refs_1_ = bf16[384,1536]{1,0:T(8,128)(2,1)S(1)} collective-permute-done((bf16[384,1536]{1,0:T(8,128)(2,1)}, bf16[384,1536]{1,0:T(8,128)(2,1)S(1)}, u32[]{:S(2)}, u32[]{:S(2)}) %collective-permute-start.3) | collective-permute-done | bytes 1179680 | tf_op jit(solution)/shard_map/ppermute | solution.py:400
  20.4 1.8 %collective-permute-start.9 = (bf16[256,1536]{1,0:T(8,128)(2,1)S(1)}, bf16[256,1536]{1,0:T(8,128)(2,1)S(1)}, u32[]{:S(2)}, u32[]{:S(2)}) collective-permute-start(bf16[256,1536]{1,0:T(8,128)(2,1)S(1)} %bitcast.5), channel_id=1, source_target_pairs={{0,5},{1,2},{2,7},{3,0},{4,1},{5,6},{6,3},{7,4},{8,13},{9,10},{10,... | collective-permute-start | bytes 2359304 | tf_op jit(solution)/shard_map/ppermute | solution.py:390
  22.8 3.3 %attend.5.refs_0_ = bf16[256,1536]{1,0:T(8,128)(2,1)S(1)} custom-call(s32[1,4]{1,0:T(1,128)S(1)} %copy-done.7, bf16[256,1536]{1,0:T(8,128)(2,1)S(1)} %copy-done.8, bf16[256,512]{1,0:T(8,128)(2,1)S(1)} %copy-done.9, bf16[256,512]{1,0:T(8,128)(2,1)S(1)} %copy-done.10, bf16[256,1536]{1,0:T(8,128)(2,1)S(1)} %attend.4.refs_0_), custom_call_target="tpu_custom_call", output_to_operand_aliasing={{}: (4, {})} | custom-call | flops 1000000000 | bytes 1024 | tf_op jit(solution)/shard_map/attend/pallas_call | solution.py:72
  26.1 3.3 %attend.6.refs_0_ = bf16[256,1536]{1,0:T(8,128)(2,1)S(1)} custom-call(s32[1,4]{1,0:T(1,128)S(1)} %copy-done.7, bf16[256,1536]{1,0:T(8,128)(2,1)S(1)} %copy-done.8, bf16[256,512]{1,0:T(8,128)(2,1)S(1)} %copy-done.9, bf16[256,512]{1,0:T(8,128)(2,1)S(1)} %copy-done.10, bf16[256,1536]{1,0:T(8,128)(2,1)S(1)} %attend.5.refs_0_), custom_call_target="tpu_custom_call", output_to_operand_aliasing={{}: (4, {})} | custom-call | flops 1000000000 | bytes 1024 | tf_op jit(solution)/shard_map/attend/pallas_call | solution.py:72
  29.4 2.4 %collective-permute-done.9.refs_7_ = bf16[256,1536]{1,0:T(8,128)(2,1)S(1)} collective-permute-done((bf16[256,1536]{1,0:T(8,128)(2,1)S(1)}, bf16[256,1536]{1,0:T(8,128)(2,1)S(1)}, u32[]{:S(2)}, u32[]{:S(2)}) %collective-permute-start.9) | collective-permute-done | bytes 786464 | tf_op jit(solution)/shard_map/ppermute | solution.py:390
  31.8 1.5 %collective-permute-start.12 = (bf16[256,1536]{1,0:T(8,128)(2,1)S(1)}, bf16[256,1536]{1,0:T(8,128)(2,1)S(1)}, u32[]{:S(2)}, u32[]{:S(2)}) collective-permute-start(bf16[256,1536]{1,0:T(8,128)(2,1)S(1)} %collective-permute-done.10.refs_8_), channel_id=1, source_target_pairs={{0,2},{1,5},{2,0},{3,7},{4,6},{5,1},{6,4},{7,3},{8,10},{9,13},{10,... | collective-permute-start | bytes 2359304 | tf_op jit(solution)/shard_map/ppermute | solution.py:387
  33.3 3.3 %attend.7.ctx_ref.refs_2_.refs_1_ = bf16[256,1536]{1,0:T(8,128)(2,1)S(1)} custom-call(s32[1,4]{1,0:T(1,128)S(1)} %copy-done.7, bf16[256,1536]{1,0:T(8,128)(2,1)S(1)} %copy-done.8, bf16[256,512]{1,0:T(8,128)(2,1)S(1)} %copy-done.9, bf16[256,512]{1,0:T(8,128)(2,1)S(1)} %copy-done.10, bf16[256,1536]{1,0:T(8,128)(2,1)S(1)} %attend.6.refs_0_), custom_call_target="tpu_custom_call", output_to_operand_aliasing={{}: (4, {})} | custom-call | flops 1000000000 | bytes 1024 | tf_op jit(solution)/shard_map/attend/pallas_call | solution.py:72
  38.2 5.6 %collective-permute-done.12.refs_10_ = bf16[256,1536]{1,0:T(8,128)(2,1)S(1)} collective-permute-done((bf16[256,1536]{1,0:T(8,128)(2,1)S(1)}, bf16[256,1536]{1,0:T(8,128)(2,1)S(1)}, u32[]{:S(2)}, u32[]{:S(2)}) %collective-permute-start.12) | collective-permute-done | bytes 786464 | tf_op jit(solution)/shard_map/ppermute | solution.py:387
  44.9 4.0 %collective-permute-start.16 = (bf16[384,512]{1,0:T(8,128)(2,1)S(1)}, bf16[384,512]{1,0:T(8,128)(2,1)S(1)}, u32[]{:S(2)}, u32[]{:S(2)}) collective-permute-start(bf16[384,512]{1,0:T(8,128)(2,1)S(1)} %collective-permute-done.15.refs_3_), channel_id=1, source_target_pairs={{0,1},{1,0},{2,3},{3,2},{4,5},{5,4},{6,7},{7,6},{8,9},{9,8},{10,11... | collective-permute-start | bytes 1179656 | tf_op jit(solution)/shard_map/ppermute | solution.py:384
  49.0 1.8 %project.1.refs_3_ = f32[256,1536]{1,0:T(8,128)S(1)} custom-call(bf16[256,1536]{1,0:T(8,128)(2,1)S(1)} %attend.7.ctx_ref.refs_2_.refs_1_, bf16[256,1536]{1,0:T(8,128)(2,1)S(1)} %copy-done.4, bf16[384,1536]{1,0:T(8,128)(2,1)S(1)} %copy-done.3, bf16[384,1536]{1,0:T(8,128)(2,1)S(1)} %collective-permute-done.3.refs_1_, ...), custom_call_target="tpu_custom_call" | custom-call | flops 1000000000 | bytes 1024 | tf_op jit(solution)/shard_map/project/pallas_call | solution.py:182
  50.9 2.6 %adapt.1.refs_0_ = f32[256,1536]{1,0:T(8,128)S(1)} custom-call(s32[4]{0:T(128)S(1)} %copy-done.6, s32[1,4]{1,0:T(1,128)S(1)} %copy-done.7, bf16[256,1536]{1,0:T(8,128)(2,1)S(1)} %attend.7.ctx_ref.refs_2_.refs_1_, f32[256,1536]{1,0:T(8,128)S(1)} %project.1.refs_3_, bf16[256,1536]{1,0:T(8,128)(2,1)S(1)} %bitcast.7, ...), custom_call_target="tpu_custom_call" | custom-call | flops 1000000000 | bytes 1024 | tf_op jit(solution)/shard_map/adapt/pallas_call | solution.py:196
  54.5 4.5 %collective-permute-start.18 = (bf16[384,512]{1,0:T(8,128)(2,1)S(1)}, bf16[384,512]{1,0:T(8,128)(2,1)S(1)}, u32[]{:S(2)}, u32[]{:S(2)}) collective-permute-start(bf16[384,512]{1,0:T(8,128)(2,1)S(1)} %get-tuple-element.40), channel_id=1, source_target_pairs={{0,1},{1,0},{2,3},{3,2},{4,5},{5,4},{6,7},{7,6},{8,9},{9,8},{10,11... | collective-permute-start | bytes 1179656 | tf_op jit(solution)/shard_map/ppermute | solution.py:384
  59.1 1.2 collective-permute-done.24.a_ref
  61.9 1.6 %collective-permute-start.26 = (bf16[256,1152]{1,0:T(8,128)(2,1)S(1)}, bf16[256,1152]{1,0:T(8,128)(2,1)S(1)}, u32[]{:S(2)}, u32[]{:S(2)}) collective-permute-start(bf16[256,1152]{1,0:T(8,128)(2,1)S(1)} %get-tuple-element.34.b_ref), channel_id=1, source_target_pairs={{0,2},{1,5},{2,0},{3,7},{4,6},{5,1},{6,4},{7,3},{8,10},{9,13},{10,... | collective-permute-start | bytes 1769480 | tf_op jit(solution)/shard_map/ppermute | solution.py:387
  63.5 1.5 %collective-permute-done.20 = bf16[256,512]{1,0:T(8,128)(2,1)S(1)} collective-permute-done((bf16[256,512]{1,0:T(8,128)(2,1)S(1)}, bf16[256,512]{1,0:T(8,128)(2,1)S(1)}, u32[]{:S(2)}, u32[]{:S(2)}) %collective-permute-start.20) | collective-permute-done | bytes 262176 | tf_op jit(solution)/shard_map/ppermute | solution.py:384
  65.6 5.4 %experts.4.refs_0_ = bf16[256,1536]{1,0:T(8,128)(2,1)S(1)} custom-call(bf16[256,512]{1,0:T(8,128)(2,1)S(1)} %get-tuple-element.30.a_ref, bf16[256,1152]{1,0:T(8,128)(2,1)S(1)} %get-tuple-element.34.b_ref, bf16[2,1536,512]{2,1,0:T(8,128)(2,1)S(1)} %copy-done, bf16[2,1536,512]{2,1,0:T(8,128)(2,1)S(1)} %copy-done.1, bf16[2,512,1536]{2,1,0:T(8,128)(2,1)S(1)} %copy-done.2, ...), custom_call_target="tpu_custom_call" | custom-call | flops 1000000000 | bytes 1024 | tf_op jit(solution)/shard_map/experts/pallas_call | solution.py:297
  71.0 3.7 %collective-permute-done.21.a_ref = bf16[256,512]{1,0:T(8,128)(2,1)S(1)} collective-permute-done((bf16[256,512]{1,0:T(8,128)(2,1)S(1)}, bf16[256,512]{1,0:T(8,128)(2,1)S(1)}, u32[]{:S(2)}, u32[]{:S(2)}) %collective-permute-start.21) | collective-permute-done | bytes 262176 | tf_op jit(solution)/shard_map/ppermute | solution.py:387
  74.7 1.6 %collective-permute-start.23 = (bf16[256,1152]{1,0:T(8,128)(2,1)S(1)}, bf16[256,1152]{1,0:T(8,128)(2,1)S(1)}, u32[]{:S(2)}, u32[]{:S(2)}) collective-permute-start(bf16[256,1152]{1,0:T(8,128)(2,1)S(1)} %collective-permute-done.22), channel_id=1, source_target_pairs={{0,2},{1,5},{2,0},{3,7},{4,6},{5,1},{6,4},{7,3},{8,10},{9,13},{10,... | collective-permute-start | bytes 1769480 | tf_op jit(solution)/shard_map/ppermute | solution.py:387
  76.7 1.5 %collective-permute-start.31 = (bf16[256,1152]{1,0:T(8,128)(2,1)S(1)}, bf16[256,1152]{1,0:T(8,128)(2,1)S(1)}, u32[]{:S(2)}, u32[]{:S(2)}) collective-permute-start(bf16[256,1152]{1,0:T(8,128)(2,1)S(1)} %collective-permute-done.30), channel_id=1, source_target_pairs={{0,2},{1,5},{2,0},{3,7},{4,6},{5,1},{6,4},{7,3},{8,10},{9,13},{10,... | collective-permute-start | bytes 1769480 | tf_op jit(solution)/shard_map/ppermute | solution.py:387
  78.7 5.4 %experts.5 = bf16[256,1536]{1,0:T(8,128)(2,1)S(1)} custom-call(bf16[256,512]{1,0:T(8,128)(2,1)S(1)} %collective-permute-done.24.a_ref, bf16[256,1152]{1,0:T(8,128)(2,1)S(1)} %collective-permute-done.26.b_ref, bf16[2,1536,512]{2,1,0:T(8,128)(2,1)S(1)} %copy-done, bf16[2,1536,512]{2,1,0:T(8,128)(2,1)S(1)} %copy-done.1, bf16[2,512,1536]{2,1,0:T(8,128)(2,1)S(1)} %copy-done.2, ...), custom_call_target="tpu_custom_call" | custom-call | flops 1000000000 | bytes 1024 | tf_op jit(solution)/shard_map/experts/pallas_call | solution.py:297
  84.6 5.6 %experts.6 = bf16[256,1536]{1,0:T(8,128)(2,1)S(1)} custom-call(bf16[256,512]{1,0:T(8,128)(2,1)S(1)} %collective-permute-done.21.a_ref, bf16[256,1152]{1,0:T(8,128)(2,1)S(1)} %collective-permute-done.23.b_ref, bf16[2,1536,512]{2,1,0:T(8,128)(2,1)S(1)} %copy-done, bf16[2,1536,512]{2,1,0:T(8,128)(2,1)S(1)} %copy-done.1, bf16[2,512,1536]{2,1,0:T(8,128)(2,1)S(1)} %copy-done.2, ...), custom_call_target="tpu_custom_call" | custom-call | flops 1000000000 | bytes 1024 | tf_op jit(solution)/shard_map/experts/pallas_call | solution.py:297
  90.3 1.6 %collective-permute-start.27 = (bf16[256,1536]{1,0:T(8,128)(2,1)S(1)}, bf16[256,1536]{1,0:T(8,128)(2,1)S(1)}, u32[]{:S(2)}, u32[]{:S(2)}) collective-permute-start(bf16[256,1536]{1,0:T(8,128)(2,1)S(1)} %experts.6), channel_id=1, source_target_pairs={{0,2},{1,5},{2,0},{3,7},{4,6},{5,1},{6,4},{7,3},{8,10},{9,13},{10,... | collective-permute-start | bytes 2359304 | tf_op jit(solution)/shard_map/ppermute | solution.py:387
  91.9 1.9 %collective-permute-done.29.a_ref = bf16[256,512]{1,0:T(8,128)(2,1)S(1)} collective-permute-done((bf16[256,512]{1,0:T(8,128)(2,1)S(1)}, bf16[256,512]{1,0:T(8,128)(2,1)S(1)}, u32[]{:S(2)}, u32[]{:S(2)}) %collective-permute-start.29) | collective-permute-done | bytes 262176 | tf_op jit(solution)/shard_map/ppermute | solution.py:387
  93.8 5.4 %experts.7 = bf16[256,1536]{1,0:T(8,128)(2,1)S(1)} custom-call(bf16[256,512]{1,0:T(8,128)(2,1)S(1)} %collective-permute-done.29.a_ref, bf16[256,1152]{1,0:T(8,128)(2,1)S(1)} %collective-permute-done.31.b_ref, bf16[2,1536,512]{2,1,0:T(8,128)(2,1)S(1)} %copy-done, bf16[2,1536,512]{2,1,0:T(8,128)(2,1)S(1)} %copy-done.1, bf16[2,512,1536]{2,1,0:T(8,128)(2,1)S(1)} %copy-done.2, ...), custom_call_target="tpu_custom_call" | custom-call | flops 1000000000 | bytes 1024 | tf_op jit(solution)/shard_map/experts/pallas_call | solution.py:297
  99.2 1.6 %collective-permute-start.32 = (bf16[256,1536]{1,0:T(8,128)(2,1)S(1)}, bf16[256,1536]{1,0:T(8,128)(2,1)S(1)}, u32[]{:S(2)}, u32[]{:S(2)}) collective-permute-start(bf16[256,1536]{1,0:T(8,128)(2,1)S(1)} %experts.7), channel_id=1, source_target_pairs={{0,2},{1,5},{2,0},{3,7},{4,6},{5,1},{6,4},{7,3},{8,10},{9,13},{10,... | collective-permute-start | bytes 2359304 | tf_op jit(solution)/shard_map/ppermute | solution.py:387
  100.8 1.6 %collective-permute-done.27 = bf16[256,1536]{1,0:T(8,128)(2,1)S(1)} collective-permute-done((bf16[256,1536]{1,0:T(8,128)(2,1)S(1)}, bf16[256,1536]{1,0:T(8,128)(2,1)S(1)}, u32[]{:S(2)}, u32[]{:S(2)}) %collective-permute-start.27) | collective-permute-done | bytes 786464 | tf_op jit(solution)/shard_map/ppermute | solution.py:387
  102.4 8.9 %collective-permute-done.32 = bf16[256,1536]{1,0:T(8,128)(2,1)S(1)} collective-permute-done((bf16[256,1536]{1,0:T(8,128)(2,1)S(1)}, bf16[256,1536]{1,0:T(8,128)(2,1)S(1)}, u32[]{:S(2)}, u32[]{:S(2)}) %collective-permute-start.32) | collective-permute-done | bytes 786464 | tf_op jit(solution)/shard_map/ppermute | solution.py:387
  111.8 11.2 %collective-permute-done.34 = bf16[256,1536]{1,0:T(8,128)(2,1)S(1)} collective-permute-done((bf16[256,1536]{1,0:T(8,128)(2,1)S(1)}, bf16[256,1536]{1,0:T(8,128)(2,1)S(1)}, u32[]{:S(2)}, u32[]{:S(2)}) %collective-permute-start.34) | collective-permute-done | bytes 786464 | tf_op jit(solution)/shard_map/ppermute | solution.py:390
  (86 shorter events, 11.3 us)
Async XLA Ops:
  0.0 8.4 %collective-permute-start.2 = (bf16[2,1536,512]{2,1,0:T(8,128)(2,1)}, bf16[2,1536,512]{2,1,0:T(8,128)(2,1)S(1)}, u32[]{:S(2)}, u32[]{:S(2)}) collective-permute-start(bf16[2,1536,512]{2,1,0:T(8,128)(2,1)} %refs_0_.11), channel_id=1, source_target_pairs={{0,1},{1,0},{2,3},{3,2},{4,5},{5,4},{6,7},{7,6},{8,9},{9,8},{10,11... | collective-permute-start | bytes 9437192 | tf_op jit(solution)/shard_map/ppermute | solution.py:384
  0.5 21.6 %collective-permute-start.1 = (bf16[2,1536,512]{2,1,0:T(8,128)(2,1)}, bf16[2,1536,512]{2,1,0:T(8,128)(2,1)S(1)}, u32[]{:S(2)}, u32[]{:S(2)}) collective-permute-start(bf16[2,1536,512]{2,1,0:T(8,128)(2,1)} %refs_1_.9), channel_id=1, source_target_pairs={{0,1},{1,0},{2,3},{3,2},{4,5},{5,4},{6,7},{7,6},{8,9},{9,8},{10,11... | collective-permute-start | bytes 9437192 | tf_op jit(solution)/shard_map/ppermute | solution.py:384
  0.6 22.1 %collective-permute-start = (bf16[2,512,1536]{2,1,0:T(8,128)(2,1)}, bf16[2,512,1536]{2,1,0:T(8,128)(2,1)S(1)}, u32[]{:S(2)}, u32[]{:S(2)}) collective-permute-start(bf16[2,512,1536]{2,1,0:T(8,128)(2,1)} %refs_2_.11), channel_id=1, source_target_pairs={{0,1},{1,0},{2,3},{3,2},{4,5},{5,4},{6,7},{7,6},{8,9},{9,8},{10,11... | collective-permute-start | bytes 9437192 | tf_op jit(solution)/shard_map/ppermute | solution.py:384
  1.0 18.6 %collective-permute-start.3 = (bf16[384,1536]{1,0:T(8,128)(2,1)}, bf16[384,1536]{1,0:T(8,128)(2,1)S(1)}, u32[]{:S(2)}, u32[]{:S(2)}) collective-permute-start(bf16[384,1536]{1,0:T(8,128)(2,1)} %refs_0_.6), channel_id=1, source_target_pairs={{0,8},{8,16},{16,24},{9,1},{17,9},{25,17},{2,10},{10,18},{18,26},{... | collective-permute-start | bytes 3538952 | tf_op jit(solution)/shard_map/ppermute | solution.py:400
  6.9 15.3 %collective-permute-start.8 = (bf16[256,1536]{1,0:T(8,128)(2,1)S(1)}, bf16[256,1536]{1,0:T(8,128)(2,1)S(1)}, u32[]{:S(2)}, u32[]{:S(2)}) collective-permute-start(bf16[256,1536]{1,0:T(8,128)(2,1)S(1)} %bitcast.4), channel_id=1, source_target_pairs={{0,2},{1,5},{2,0},{3,7},{4,6},{5,1},{6,4},{7,3},{8,10},{9,13},{10,... | collective-permute-start | bytes 2359304 | tf_op jit(solution)/shard_map/ppermute | solution.py:387
  19.6 17.0 %collective-permute-start.5 = (bf16[384,1536]{1,0:T(8,128)(2,1)S(1)}, bf16[384,1536]{1,0:T(8,128)(2,1)S(1)}, u32[]{:S(2)}, u32[]{:S(2)}) collective-permute-start(bf16[384,1536]{1,0:T(8,128)(2,1)S(1)} %collective-permute-done.3.refs_1_), channel_id=1, source_target_pairs={{8,16},{16,24},{9,1},{17,9},{10,18},{18,26},{11,3},{19,11},{12,20}... | collective-permute-start | bytes 3538952 | tf_op jit(solution)/shard_map/ppermute | solution.py:400
  20.4 11.5 %collective-permute-start.9 = (bf16[256,1536]{1,0:T(8,128)(2,1)S(1)}, bf16[256,1536]{1,0:T(8,128)(2,1)S(1)}, u32[]{:S(2)}, u32[]{:S(2)}) collective-permute-start(bf16[256,1536]{1,0:T(8,128)(2,1)S(1)} %bitcast.5), channel_id=1, source_target_pairs={{0,5},{1,2},{2,7},{3,0},{4,1},{5,6},{6,3},{7,4},{8,13},{9,10},{10,... | collective-permute-start | bytes 2359304 | tf_op jit(solution)/shard_map/ppermute | solution.py:390
  22.2 9.7 %collective-permute-start.10 = (bf16[256,1536]{1,0:T(8,128)(2,1)S(1)}, bf16[256,1536]{1,0:T(8,128)(2,1)S(1)}, u32[]{:S(2)}, u32[]{:S(2)}) collective-permute-start(bf16[256,1536]{1,0:T(8,128)(2,1)S(1)} %collective-permute-done.8.refs_6_), channel_id=1, source_target_pairs={{0,1},{1,0},{2,3},{3,2},{4,5},{5,4},{6,7},{7,6},{8,9},{9,8},{10,11... | collective-permute-start | bytes 2359304 | tf_op jit(solution)/shard_map/ppermute | solution.py:384
  22.2 22.4 %collective-permute-start.4 = (bf16[384,1536]{1,0:T(8,128)(2,1)S(1)}, bf16[384,1536]{1,0:T(8,128)(2,1)S(1)}, u32[]{:S(2)}, u32[]{:S(2)}) collective-permute-start(bf16[384,1536]{1,0:T(8,128)(2,1)S(1)} %collective-permute-done.3.refs_1_), channel_id=1, source_target_pairs={{0,1},{1,0},{2,3},{3,2},{4,5},{5,4},{6,7},{7,6},{8,9},{9,8},{10,11... | collective-permute-start | bytes 3538952 | tf_op jit(solution)/shard_map/ppermute | solution.py:384
  22.7 14.6 %collective-permute-start.7 = (bf16[256,1536]{1,0:T(8,128)(2,1)S(1)}, bf16[256,1536]{1,0:T(8,128)(2,1)S(1)}, u32[]{:S(2)}, u32[]{:S(2)}) collective-permute-start(bf16[256,1536]{1,0:T(8,128)(2,1)S(1)} %bitcast.6), channel_id=1, source_target_pairs={{0,1},{1,0},{2,3},{3,2},{4,5},{5,4},{6,7},{7,6},{8,9},{9,8},{10,11... | collective-permute-start | bytes 2359304 | tf_op jit(solution)/shard_map/ppermute | solution.py:384
  31.8 12.0 %collective-permute-start.12 = (bf16[256,1536]{1,0:T(8,128)(2,1)S(1)}, bf16[256,1536]{1,0:T(8,128)(2,1)S(1)}, u32[]{:S(2)}, u32[]{:S(2)}) collective-permute-start(bf16[256,1536]{1,0:T(8,128)(2,1)S(1)} %collective-permute-done.10.refs_8_), channel_id=1, source_target_pairs={{0,2},{1,5},{2,0},{3,7},{4,6},{5,1},{6,4},{7,3},{8,10},{9,13},{10,... | collective-permute-start | bytes 2359304 | tf_op jit(solution)/shard_map/ppermute | solution.py:387
  36.6 12.2 %collective-permute-start.6 = (bf16[384,1536]{1,0:T(8,128)(2,1)S(1)}, bf16[384,1536]{1,0:T(8,128)(2,1)S(1)}, u32[]{:S(2)}, u32[]{:S(2)}) collective-permute-start(bf16[384,1536]{1,0:T(8,128)(2,1)S(1)} %collective-permute-done.5.refs_3_), channel_id=1, source_target_pairs={{0,1},{1,0},{2,3},{3,2},{4,5},{5,4},{6,7},{7,6},{8,9},{9,8},{10,11... | collective-permute-start | bytes 3538952 | tf_op jit(solution)/shard_map/ppermute | solution.py:384
  37.1 13.8 %collective-permute-start.11 = (bf16[256,1536]{1,0:T(8,128)(2,1)S(1)}, bf16[256,1536]{1,0:T(8,128)(2,1)S(1)}, u32[]{:S(2)}, u32[]{:S(2)}) collective-permute-start(bf16[256,1536]{1,0:T(8,128)(2,1)S(1)} %collective-permute-done.9.refs_7_), channel_id=1, source_target_pairs={{0,1},{1,0},{2,3},{3,2},{4,5},{5,4},{6,7},{7,6},{8,9},{9,8},{10,11... | collective-permute-start | bytes 2359304 | tf_op jit(solution)/shard_map/ppermute | solution.py:384
  37.3 7.6 %collective-permute-start.15 = (bf16[384,512]{1,0:T(8,128)(2,1)S(1)}, bf16[384,512]{1,0:T(8,128)(2,1)S(1)}, u32[]{:S(2)}, u32[]{:S(2)}) collective-permute-start(bf16[384,512]{1,0:T(8,128)(2,1)S(1)} %slice.26), channel_id=1, source_target_pairs={{16,24},{9,1},{18,26},{11,3},{20,28},{13,5},{22,30},{15,7}} | collective-permute-start | bytes 1179656 | tf_op jit(solution)/shard_map/ppermute | solution.py:400
  43.8 10.7 %collective-permute-start.17 = (bf16[384,1024]{1,0:T(8,128)(2,1)S(1)}, bf16[384,1024]{1,0:T(8,128)(2,1)S(1)}, u32[]{:S(2)}, u32[]{:S(2)}) collective-permute-start(bf16[384,1024]{1,0:T(8,128)(2,1)S(1)} %slice.27), channel_id=1, source_target_pairs={{16,24},{9,1},{18,26},{11,3},{20,28},{13,5},{22,30},{15,7}} | collective-permute-start | bytes 2359304 | tf_op jit(solution)/shard_map/ppermute | solution.py:400
  44.6 6.3 %collective-permute-start.13 = (bf16[192,1536]{1,0:T(8,128)(2,1)S(1)}, bf16[192,1536]{1,0:T(8,128)(2,1)S(1)}, u32[]{:S(2)}, u32[]{:S(2)}) collective-permute-start(bf16[192,1536]{1,0:T(8,128)(2,1)S(1)} %slice.24), channel_id=1, source_target_pairs={{0,1},{1,0},{2,3},{3,2},{4,5},{5,4},{6,7},{7,6},{8,9},{9,8},{10,11... | collective-permute-start | bytes 1769480 | tf_op jit(solution)/shard_map/ppermute | solution.py:384
  44.9 8.6 %collective-permute-start.16 = (bf16[384,512]{1,0:T(8,128)(2,1)S(1)}, bf16[384,512]{1,0:T(8,128)(2,1)S(1)}, u32[]{:S(2)}, u32[]{:S(2)}) collective-permute-start(bf16[384,512]{1,0:T(8,128)(2,1)S(1)} %collective-permute-done.15.refs_3_), channel_id=1, source_target_pairs={{0,1},{1,0},{2,3},{3,2},{4,5},{5,4},{6,7},{7,6},{8,9},{9,8},{10,11... | collective-permute-start | bytes 1179656 | tf_op jit(solution)/shard_map/ppermute | solution.py:384
  48.9 2.0 %collective-permute-start.14 = (bf16[64,1536]{1,0:T(8,128)(2,1)S(1)}, bf16[64,1536]{1,0:T(8,128)(2,1)S(1)}, u32[]{:S(2)}, u32[]{:S(2)}) collective-permute-start(bf16[64,1536]{1,0:T(8,128)(2,1)S(1)} %slice.25), channel_id=1, source_target_pairs={{0,1},{1,0},{2,3},{3,2},{4,5},{5,4},{6,7},{7,6},{8,9},{9,8},{10,11... | collective-permute-start | bytes 589832 | tf_op jit(solution)/shard_map/ppermute | solution.py:384
  53.9 6.4 %collective-permute-start.24 = (bf16[256,512]{1,0:T(8,128)(2,1)S(1)}, bf16[256,512]{1,0:T(8,128)(2,1)S(1)}, u32[]{:S(2)}, u32[]{:S(2)}) collective-permute-start(bf16[256,512]{1,0:T(8,128)(2,1)S(1)} %get-tuple-element.30.a_ref), channel_id=1, source_target_pairs={{0,2},{1,5},{2,0},{3,7},{4,6},{5,1},{6,4},{7,3},{8,10},{9,13},{10,... | collective-permute-start | bytes 786440 | tf_op jit(solution)/shard_map/ppermute | solution.py:387
  54.5 6.0 %collective-permute-start.18 = (bf16[384,512]{1,0:T(8,128)(2,1)S(1)}, bf16[384,512]{1,0:T(8,128)(2,1)S(1)}, u32[]{:S(2)}, u32[]{:S(2)}) collective-permute-start(bf16[384,512]{1,0:T(8,128)(2,1)S(1)} %get-tuple-element.40), channel_id=1, source_target_pairs={{0,1},{1,0},{2,3},{3,2},{4,5},{5,4},{6,7},{7,6},{8,9},{9,8},{10,11... | collective-permute-start | bytes 1179656 | tf_op jit(solution)/shard_map/ppermute | solution.py:384
  61.9 12.8 %collective-permute-start.26 = (bf16[256,1152]{1,0:T(8,128)(2,1)S(1)}, bf16[256,1152]{1,0:T(8,128)(2,1)S(1)}, u32[]{:S(2)}, u32[]{:S(2)}) collective-permute-start(bf16[256,1152]{1,0:T(8,128)(2,1)S(1)} %get-tuple-element.34.b_ref), channel_id=1, source_target_pairs={{0,2},{1,5},{2,0},{3,7},{4,6},{5,1},{6,4},{7,3},{8,10},{9,13},{10,... | collective-permute-start | bytes 1769480 | tf_op jit(solution)/shard_map/ppermute | solution.py:387
  65.0 9.7 %collective-permute-start.21 = (bf16[256,512]{1,0:T(8,128)(2,1)S(1)}, bf16[256,512]{1,0:T(8,128)(2,1)S(1)}, u32[]{:S(2)}, u32[]{:S(2)}) collective-permute-start(bf16[256,512]{1,0:T(8,128)(2,1)S(1)} %collective-permute-done.20), channel_id=1, source_target_pairs={{0,2},{1,5},{2,0},{3,7},{4,6},{5,1},{6,4},{7,3},{8,10},{9,13},{10,... | collective-permute-start | bytes 786440 | tf_op jit(solution)/shard_map/ppermute | solution.py:387
  65.5 9.1 %collective-permute-start.22 = (bf16[256,1152]{1,0:T(8,128)(2,1)S(1)}, bf16[256,1152]{1,0:T(8,128)(2,1)S(1)}, u32[]{:S(2)}, u32[]{:S(2)}) collective-permute-start(bf16[256,1152]{1,0:T(8,128)(2,1)S(1)} %get-tuple-element.34.b_ref), channel_id=1, source_target_pairs={{0,1},{1,0},{2,3},{3,2},{4,5},{5,4},{6,7},{7,6},{8,9},{9,8},{10,11... | collective-permute-start | bytes 1769480 | tf_op jit(solution)/shard_map/ppermute | solution.py:384
  74.7 2.0 %collective-permute-start.30 = (bf16[256,1152]{1,0:T(8,128)(2,1)S(1)}, bf16[256,1152]{1,0:T(8,128)(2,1)S(1)}, u32[]{:S(2)}, u32[]{:S(2)}) collective-permute-start(bf16[256,1152]{1,0:T(8,128)(2,1)S(1)} %collective-permute-done.26.b_ref), channel_id=1, source_target_pairs={{0,1},{1,0},{2,3},{3,2},{4,5},{5,4},{6,7},{7,6},{8,9},{9,8},{10,11... | collective-permute-start | bytes 1769480 | tf_op jit(solution)/shard_map/ppermute | solution.py:384
  74.7 9.9 %collective-permute-start.23 = (bf16[256,1152]{1,0:T(8,128)(2,1)S(1)}, bf16[256,1152]{1,0:T(8,128)(2,1)S(1)}, u32[]{:S(2)}, u32[]{:S(2)}) collective-permute-start(bf16[256,1152]{1,0:T(8,128)(2,1)S(1)} %collective-permute-done.22), channel_id=1, source_target_pairs={{0,2},{1,5},{2,0},{3,7},{4,6},{5,1},{6,4},{7,3},{8,10},{9,13},{10,... | collective-permute-start | bytes 1769480 | tf_op jit(solution)/shard_map/ppermute | solution.py:387
  76.7 15.2 %collective-permute-start.31 = (bf16[256,1152]{1,0:T(8,128)(2,1)S(1)}, bf16[256,1152]{1,0:T(8,128)(2,1)S(1)}, u32[]{:S(2)}, u32[]{:S(2)}) collective-permute-start(bf16[256,1152]{1,0:T(8,128)(2,1)S(1)} %collective-permute-done.30), channel_id=1, source_target_pairs={{0,2},{1,5},{2,0},{3,7},{4,6},{5,1},{6,4},{7,3},{8,10},{9,13},{10,... | collective-permute-start | bytes 1769480 | tf_op jit(solution)/shard_map/ppermute | solution.py:387
  78.2 15.6 %collective-permute-start.29 = (bf16[256,512]{1,0:T(8,128)(2,1)S(1)}, bf16[256,512]{1,0:T(8,128)(2,1)S(1)}, u32[]{:S(2)}, u32[]{:S(2)}) collective-permute-start(bf16[256,512]{1,0:T(8,128)(2,1)S(1)} %collective-permute-done.25), channel_id=1, source_target_pairs={{0,2},{1,5},{2,0},{3,7},{4,6},{5,1},{6,4},{7,3},{8,10},{9,13},{10,... | collective-permute-start | bytes 786440 | tf_op jit(solution)/shard_map/ppermute | solution.py:387
  84.1 18.2 %collective-permute-start.33 = (bf16[256,1536]{1,0:T(8,128)(2,1)S(1)}, bf16[256,1536]{1,0:T(8,128)(2,1)S(1)}, u32[]{:S(2)}, u32[]{:S(2)}) collective-permute-start(bf16[256,1536]{1,0:T(8,128)(2,1)S(1)} %experts.5), channel_id=1, source_target_pairs={{0,1},{1,0},{2,3},{3,2},{4,5},{5,4},{6,7},{7,6},{8,9},{9,8},{10,11... | collective-permute-start | bytes 2359304 | tf_op jit(solution)/shard_map/ppermute | solution.py:384
  90.3 12.1 %collective-permute-start.27 = (bf16[256,1536]{1,0:T(8,128)(2,1)S(1)}, bf16[256,1536]{1,0:T(8,128)(2,1)S(1)}, u32[]{:S(2)}, u32[]{:S(2)}) collective-permute-start(bf16[256,1536]{1,0:T(8,128)(2,1)S(1)} %experts.6), channel_id=1, source_target_pairs={{0,2},{1,5},{2,0},{3,7},{4,6},{5,1},{6,4},{7,3},{8,10},{9,13},{10,... | collective-permute-start | bytes 2359304 | tf_op jit(solution)/shard_map/ppermute | solution.py:387
  99.2 12.1 %collective-permute-start.32 = (bf16[256,1536]{1,0:T(8,128)(2,1)S(1)}, bf16[256,1536]{1,0:T(8,128)(2,1)S(1)}, u32[]{:S(2)}, u32[]{:S(2)}) collective-permute-start(bf16[256,1536]{1,0:T(8,128)(2,1)S(1)} %experts.7), channel_id=1, source_target_pairs={{0,2},{1,5},{2,0},{3,7},{4,6},{5,1},{6,4},{7,3},{8,10},{9,13},{10,... | collective-permute-start | bytes 2359304 | tf_op jit(solution)/shard_map/ppermute | solution.py:387
  102.3 9.2 %collective-permute-start.28 = (bf16[256,1536]{1,0:T(8,128)(2,1)S(1)}, bf16[256,1536]{1,0:T(8,128)(2,1)S(1)}, u32[]{:S(2)}, u32[]{:S(2)}) collective-permute-start(bf16[256,1536]{1,0:T(8,128)(2,1)S(1)} %collective-permute-done.27), channel_id=1, source_target_pairs={{0,1},{1,0},{2,3},{3,2},{4,5},{5,4},{6,7},{7,6},{8,9},{9,8},{10,11... | collective-permute-start | bytes 2359304 | tf_op jit(solution)/shard_map/ppermute | solution.py:384
  111.5 11.5 %collective-permute-start.34 = (bf16[256,1536]{1,0:T(8,128)(2,1)S(1)}, bf16[256,1536]{1,0:T(8,128)(2,1)S(1)}, u32[]{:S(2)}, u32[]{:S(2)}) collective-permute-start(bf16[256,1536]{1,0:T(8,128)(2,1)S(1)} %add_convert_fusion.1), channel_id=1, source_target_pairs={{0,5},{1,2},{2,7},{3,0},{4,1},{5,6},{6,3},{7,4},{8,13},{9,10},{10,... | collective-permute-start | bytes 2359304 | tf_op jit(solution)/shard_map/ppermute | solution.py:390
  (16 other events, 100.7 us)
